TPU v7x, 32 devices: a whole 2x2x4 slice. The times are simulated.
32 devices in a mesh: page: 8 (over z, x), seq: 4 (over y, core).
Axes of the slice: x: 2, y: 2, z: 4, core: 2. Of those that a mesh axis runs over, the one named last changes fastest.
Arguments:
- tokens: bfloat16 [16, 512, 1024], P('page', 'seq'), may hold values from -6 to 6
- cells: int32 [16, 512], P('page', 'seq'), may hold values from 0 to 511, as said below
- lengths: int32 [16], P('page'), may hold values from 64 to 512, as said below
- cotangent: bfloat16 [16, 512, 1024], P('page', 'seq'), may hold values from -6 to 6
- w_qkv: float32 [1024, 3072], P(('page', 'seq')), may hold values from -0.1875 to 0.1875
- w_out: float32 [1024, 1024], P(('page', 'seq')), may hold values from -0.75 to 0.75
- w_up: float32 [1024, 4096], P(('page', 'seq')), may hold values from -0.1875 to 0.1875
- w_down: float32 [4096, 1024], P(('page', 'seq')), may hold values from -0.09375 to 0.09375
- biases: float32 [10, 1024], P(None, ('page', 'seq')), may hold values from -3 to 3
- gains: float32 [2, 1024], P(None, ('page', 'seq')), may hold values from 0.5 to 1.5
- cell_bias: float32 [16], replicated, may hold values from 0.5 to 2
Outputs:
- output: bfloat16 [16, 512, 1024], P('page', 'seq')
- grad_tokens: float32 [16, 512, 1024], P('page', 'seq')
- grad_qkv: float32 [1024, 3072], P(('page', 'seq'))
- grad_out: float32 [1024, 1024], P(('page', 'seq'))
- grad_up: float32 [1024, 4096], P(('page', 'seq'))
- grad_down: float32 [4096, 1024], P(('page', 'seq'))
- grad_biases: float32 [10, 1024], P(None, ('page', 'seq'))
- grad_gains: float32 [2, 1024], P(None, ('page', 'seq'))
- grad_cell: float32 [16], replicated
Inputs may be any that keep to these rules, and one draw needn't show every extreme that they name: `lengths`: every page has at least 64 valid tokens, and some page is full. `cells`: within a page cell numbers never fall, rise by at most one from token to token, and the first token is in cell 0; some page has every token in a cell of its own.
All inputs are finite; a program needn't handle non-finite values.
Results may differ from a plain program's by a relative error of at most 0.014.
The roundings to bfloat16 on the way count: a program that leaves them out, or rounds other values in their place, can miss the bound.
Values may be sent and summed in bfloat16 or wider, within the bound.
No kernel may reach another device: no remote copies, remote signals or barrier semaphores. Data moves between devices by JAX's collectives and lax.ppermute only.
A program may use at most 256 MiB of HBM per device.

v0:
```python
import jax
import jax.numpy as jnp
from jax import lax
from jax.sharding import PartitionSpec as P


def layer_norm(values, gain, shift):
    center = values - jnp.mean(values, axis=-1, keepdims=True)
    spread = jnp.mean(center * center, axis=-1, keepdims=True)
    return center * lax.rsqrt(spread + 1e-05) * gain + shift


def gelu_exact(values):
    return 0.5 * values * (1.0 + jax.scipy.special.erf(values * 0.7071067811865476))


def split_heads(gathered, width_full, head_count):
    page_count, slot_count = (gathered.shape[0], gathered.shape[1])
    head_depth = width_full // head_count
    keys = gathered[:, :, :width_full].reshape(page_count, slot_count, head_count, head_depth)
    values = gathered[:, :, width_full:].reshape(page_count, slot_count, head_count, head_depth)
    return (keys, values)


def scores_of(query, keys, cells_here, cells_all, lengths, cell_bias):
    page_count = query.shape[0]
    slot_count = keys.shape[1]
    raw_scores = (
        jnp.einsum("pqhe,pkhe->phqk", query, keys, preferred_element_type=jnp.float32) * 0.125
    )
    same_cell = (cells_here[:, :, None] == cells_all[:, None, :]).astype(jnp.float32)
    key_valid = lax.broadcasted_iota(jnp.int32, (page_count, slot_count), 1) < lengths[:, None]
    scores = raw_scores + cell_bias[None, :, None, None] * same_cell[:, None]
    return (jnp.where(key_valid[:, None, None, :], scores, -1e30), same_cell)


def local(tokens, cells, lengths, cotangent, w_qkv, w_out, w_up, w_down, biases, gains, cell_bias):
    page_count, row_count, width_full = tokens.shape
    head_count = cell_bias.shape[0]
    head_depth = width_full // head_count
    flat_rows = page_count * row_count
    forward_full = (
        lax.all_gather(w_qkv.astype(jnp.bfloat16), ("page", "seq"), axis=0, tiled=True),
        lax.all_gather(w_out.astype(jnp.bfloat16), ("page", "seq"), axis=0, tiled=True),
        lax.all_gather(w_up.astype(jnp.bfloat16), ("page", "seq"), axis=0, tiled=True),
        lax.all_gather(w_down.astype(jnp.bfloat16), ("page", "seq"), axis=0, tiled=True),
        lax.all_gather(biases.astype(jnp.bfloat16), ("page", "seq"), axis=1, tiled=True),
        lax.all_gather(gains.astype(jnp.bfloat16), ("page", "seq"), axis=1, tiled=True),
    )
    w_proj, w_mix, w_expand, w_reduce = (
        forward_full[0],
        forward_full[1],
        forward_full[2],
        forward_full[3],
    )
    vectors = forward_full[4].astype(jnp.float32)
    scales = forward_full[5].astype(jnp.float32)
    inputs = tokens.reshape(flat_rows, width_full)
    inputs_wide = inputs.astype(jnp.float32)
    bias_qkv = jnp.concatenate([vectors[0], jnp.zeros_like(vectors[0]), vectors[1]])
    projected = (jnp.dot(inputs, w_proj, preferred_element_type=jnp.float32) + bias_qkv).astype(
        jnp.bfloat16
    )
    projected = projected.reshape(page_count, row_count, 3 * width_full)
    query = projected[:, :, :width_full].reshape(page_count, row_count, head_count, head_depth)
    key_value = projected[:, :, width_full:]
    gathered, cells_all = (
        lax.all_gather(key_value, "seq", axis=1, tiled=True),
        lax.all_gather(cells, "seq", axis=1, tiled=True),
    )
    slot_count = gathered.shape[1]
    keys, values = split_heads(gathered, width_full, head_count)
    scores, same_cell = scores_of(query, keys, cells, cells_all, lengths, cell_bias)
    peak = jnp.max(scores, axis=-1, keepdims=True)
    exponent = jnp.exp(scores - peak)
    totals = jnp.sum(exponent, axis=-1, keepdims=True)
    log_total = peak + jnp.log(totals)
    weights_low = (exponent / totals).astype(jnp.bfloat16)
    context = jnp.einsum("phqk,pkhe->pqhe", weights_low, values, preferred_element_type=jnp.float32)
    context = context.reshape(flat_rows, width_full).astype(jnp.bfloat16)
    attended = jnp.dot(context, w_mix, preferred_element_type=jnp.float32) + vectors[2]
    normed, norm_first = jax.vjp(layer_norm, inputs_wide + attended, scales[0], vectors[4])
    normed_low = normed.astype(jnp.bfloat16)
    expanded = jnp.dot(normed_low, w_expand, preferred_element_type=jnp.float32) + vectors[
        6:10
    ].reshape(-1)
    activated, gelu_back = jax.vjp(gelu_exact, expanded)
    activated_low = activated.astype(jnp.bfloat16)
    reduced = jnp.dot(activated_low, w_reduce, preferred_element_type=jnp.float32) + vectors[3]
    output_wide, norm_second = jax.vjp(layer_norm, normed + reduced, scales[1], vectors[5])
    output = output_wide.astype(jnp.bfloat16).reshape(page_count, row_count, width_full)
    back_full = (
        lax.all_gather(w_qkv.astype(jnp.bfloat16), ("page", "seq"), axis=0, tiled=True),
        lax.all_gather(w_out.astype(jnp.bfloat16), ("page", "seq"), axis=0, tiled=True),
        lax.all_gather(w_up.astype(jnp.bfloat16), ("page", "seq"), axis=0, tiled=True),
        lax.all_gather(w_down.astype(jnp.bfloat16), ("page", "seq"), axis=0, tiled=True),
    )
    w_proj, w_mix, w_expand, w_reduce = (back_full[0], back_full[1], back_full[2], back_full[3])
    grad_output = cotangent.reshape(flat_rows, width_full).astype(jnp.float32)
    grad_second, grad_gain_two, grad_shift_two = norm_second(grad_output)
    grad_second_low = grad_second.astype(jnp.bfloat16)
    grad_reduce = jnp.dot(activated_low.T, grad_second_low, preferred_element_type=jnp.float32)
    grad_activated = jnp.dot(grad_second_low, w_reduce.T, preferred_element_type=jnp.float32)
    grad_expanded = gelu_back(grad_activated)[0]
    grad_expanded_low = grad_expanded.astype(jnp.bfloat16)
    grad_expand = jnp.dot(normed_low.T, grad_expanded_low, preferred_element_type=jnp.float32)
    grad_normed = grad_second + jnp.dot(
        grad_expanded_low, w_expand.T, preferred_element_type=jnp.float32
    )
    grad_first, grad_gain_one, grad_shift_one = norm_first(grad_normed)
    grad_first_low = grad_first.astype(jnp.bfloat16)
    grad_mix = jnp.dot(context.T, grad_first_low, preferred_element_type=jnp.float32)
    grad_context = jnp.dot(grad_first_low, w_mix.T, preferred_element_type=jnp.float32).astype(
        jnp.bfloat16
    )
    grad_context = grad_context.reshape(page_count, row_count, head_count, head_depth)
    scores, same_cell = scores_of(query, keys, cells, cells_all, lengths, cell_bias)
    weights_wide = jnp.exp(scores - log_total)
    weights_low = weights_wide.astype(jnp.bfloat16)
    grad_weights = jnp.einsum(
        "pqhe,pkhe->phqk", grad_context, values, preferred_element_type=jnp.float32
    )
    grad_values = jnp.einsum(
        "phqk,pqhe->pkhe", weights_low, grad_context, preferred_element_type=jnp.float32
    )
    inner_sum = jnp.sum(weights_wide * grad_weights, axis=-1, keepdims=True)
    grad_scores = weights_wide * (grad_weights - inner_sum)
    grad_cell_local = jnp.sum(grad_scores * same_cell[:, None], axis=(0, 2, 3))
    grad_scores_low = grad_scores.astype(jnp.bfloat16)
    grad_query = (
        jnp.einsum("phqk,pkhe->pqhe", grad_scores_low, keys, preferred_element_type=jnp.float32)
        * 0.125
    )
    grad_keys = (
        jnp.einsum("phqk,pqhe->pkhe", grad_scores_low, query, preferred_element_type=jnp.float32)
        * 0.125
    )
    grad_kv_all = jnp.concatenate(
        [
            grad_keys.reshape(page_count, slot_count, width_full),
            grad_values.reshape(page_count, slot_count, width_full),
        ],
        axis=2,
    )
    grad_kv = lax.psum_scatter(
        grad_kv_all.astype(jnp.bfloat16), "seq", scatter_dimension=1, tiled=True
    ).astype(jnp.float32)
    grad_kv = grad_kv.reshape(flat_rows, 2 * width_full)
    grad_query = grad_query.reshape(flat_rows, width_full)
    grad_proj_low = jnp.concatenate([grad_query, grad_kv], axis=1).astype(jnp.bfloat16)
    grad_proj = jnp.dot(inputs.T, grad_proj_low, preferred_element_type=jnp.float32)
    grad_inputs = grad_first + jnp.dot(grad_proj_low, w_proj.T, preferred_element_type=jnp.float32)
    grad_rows = jnp.stack(
        [
            jnp.sum(grad_query, axis=0),
            jnp.sum(grad_kv[:, width_full:], axis=0),
            jnp.sum(grad_first, axis=0),
            jnp.sum(grad_second, axis=0),
            grad_shift_one,
            grad_shift_two,
        ]
    )
    grad_vectors = jnp.concatenate(
        [grad_rows, jnp.sum(grad_expanded, axis=0).reshape(4, width_full)], axis=0
    )
    grad_scales = jnp.stack([grad_gain_one, grad_gain_two])
    owned_all = (
        lax.psum_scatter(grad_proj, ("page", "seq"), scatter_dimension=0, tiled=True),
        lax.psum_scatter(grad_mix, ("page", "seq"), scatter_dimension=0, tiled=True),
        lax.psum_scatter(grad_expand, ("page", "seq"), scatter_dimension=0, tiled=True),
        lax.psum_scatter(grad_reduce, ("page", "seq"), scatter_dimension=0, tiled=True),
        lax.psum_scatter(grad_vectors, ("page", "seq"), scatter_dimension=1, tiled=True),
        lax.psum_scatter(grad_scales, ("page", "seq"), scatter_dimension=1, tiled=True),
    )
    cell_total = lax.psum(grad_cell_local, ("page", "seq"))
    return (
        output,
        grad_inputs.reshape(page_count, row_count, width_full),
        owned_all[0],
        owned_all[1],
        owned_all[2],
        owned_all[3],
        owned_all[4],
        owned_all[5],
        cell_total,
    )


def solution(mesh):
    placed = (
        P("page", "seq", None),
        P("page", "seq"),
        P("page"),
        P("page", "seq", None),
        P(("page", "seq"), None),
        P(("page", "seq"), None),
        P(("page", "seq"), None),
        P(("page", "seq"), None),
        P(None, ("page", "seq")),
        P(None, ("page", "seq")),
        P(),
    )
    return jax.shard_map(
        local,
        mesh=mesh,
        in_specs=placed,
        out_specs=(
            P("page", "seq", None),
            P("page", "seq", None),
            P(("page", "seq"), None),
            P(("page", "seq"), None),
            P(("page", "seq"), None),
            P(("page", "seq"), None),
            P(None, ("page", "seq")),
            P(None, ("page", "seq")),
            P(),
        ),
        check_vma=False,
    )
```

profile of v0, /device:TPU:0, one launch (start us, length us, event | category | flops | bytes accessed | tf_op | source)
XLA Modules:
  0.0 1394.2 jit_solution(10630205725843938995)
XLA Ops:
  9.7 44.0 %all-gather = bf16[32,32,10]{1,2,0:T(8,128)(2,1)S(1)} all-gather(bf16[1,32,10]{1,2,0:T(8,128)(2,1)S(1)} %convert_bitcast_fusion), channel_id=1, replica_groups=mesh['page'=8,'seq'=4] {'page','seq'}, dimensions={0}, use_global_device_ids=true | all-gather | bytes 21120 | tf_op jit(solution)/shard_map/all_gather | solution.py:47
  53.9 29.9 %all-gather.8.cloned.1.call-done = bf16[1024,3072]{1,0:T(8,128)(2,1)} async-done(((bf16[32,3072]{1,0:T(8,128)(2,1)}), bf16[1024,3072]{1,0:T(8,128)(2,1)}) %all-gather.8.cloned.1.call-update) | async-done | bytes 6291472 | tf_op jit(solution)/shard_map/all_gather | solution.py:43
  83.8 4.8 fusion.6
  92.2 38.8 %all-gather.1 = bf16[32,32,2]{1,2,0:T(2,128)(2,1)S(1)} all-gather(bf16[1,32,2]{1,2,0:T(2,128)(2,1)S(1)} %convert_bitcast_fusion.1), channel_id=1, replica_groups=mesh['page'=8,'seq'=4] {'page','seq'}, dimensions={0}, use_global_device_ids=true | all-gather | bytes 4224 | tf_op jit(solution)/shard_map/all_gather | solution.py:48
  131.2 5.2 all_gather.31
  137.0 4.4 fusion.39
  146.9 4.4 fusion.43
  158.0 24.8 %all-gather.12.cloned.1.call-done = bf16[1024,1024]{1,0:T(8,128)(2,1)} async-done(((bf16[32,1024]{1,0:T(8,128)(2,1)}), bf16[1024,1024]{1,0:T(8,128)(2,1)}) %all-gather.12.cloned.1.call-update) | async-done | bytes 2097168 | tf_op jit(solution)/shard_map/all_gather | solution.py:44
  185.6 77.0 %all-gather.14.cloned.1.call-done = bf16[1024,4096]{1,0:T(8,128)(2,1)} async-done(((bf16[32,4096]{1,0:T(8,128)(2,1)}), bf16[1024,4096]{1,0:T(8,128)(2,1)}) %all-gather.14.cloned.1.call-update) | async-done | bytes 8388624 | tf_op jit(solution)/shard_map/all_gather | solution.py:45
  262.6 7.8 convolution_add_fusion
  270.4 71.7 %all-gather.16.cloned.1.call-done = bf16[4096,1024]{1,0:T(8,128)(2,1)} async-done(((bf16[128,1024]{1,0:T(8,128)(2,1)}), bf16[4096,1024]{1,0:T(8,128)(2,1)}) %all-gather.16.cloned.1.call-update) | async-done | bytes 8388624 | tf_op jit(solution)/shard_map/all_gather | solution.py:46
  342.1 7.3 fusion.45
  351.7 4.5 fusion.46
  366.2 6.7 fusion.8
  372.9 6.9 multiply_reduce_fusion.1
  383.8 7.4 multiply_reduce_fusion
  395.2 4.3 copy.64
  399.5 4.8 pad_maximum_fusion
  406.6 5.8 fusion.40
  412.9 34.7 %reduce-scatter.14.cloned.1.call-done = bf16[2,128,2048]{2,1,0:T(8,128)(2,1)} async-done(((bf16[2,512,2048]{2,1,0:T(8,128)(2,1)}), bf16[2,128,2048]{2,1,0:T(8,128)(2,1)}) %reduce-scatter.14.cloned.1.call-update) | async-done | bytes 1048592 | tf_op jit(solution)/shard_map/reduce_scatter | solution.py:145
  459.2 7.9 convolution_bitcast_fusion
  467.1 12.6 copy.69
  479.7 10.4 fusion.33
  490.2 9.8 fusion.20
  500.0 39.6 %psum.7 = f32[16]{0:T(128)} all-reduce(f32[16]{0:T(128)S(1)} %get-tuple-element.54), channel_id=1, replica_groups=mesh['page'=8,'seq'=4] {'page','seq'}, use_global_device_ids=true, to_apply=%region_28.29 | all-reduce | flops 16 | bytes 128 | tf_op jit(solution)/shard_map/psum | solution.py:175
  539.6 44.2 %reduce-scatter.26.cloned.1.call-done = f32[32,2]{1,0:T(8,128)} async-done(((f32[1024,2]{1,0:T(8,128)}), f32[32,2]{1,0:T(8,128)}) %reduce-scatter.26.cloned.1.call-update) | async-done | bytes 272
  585.2 5.6 convolution_add_fusion.3
  590.7 125.3 %reduce-scatter.24.cloned.1.call-done = f32[32,10]{1,0:T(8,128)} async-done(((f32[1024,10]{1,0:T(8,128)}), f32[32,10]{1,0:T(8,128)}) %reduce-scatter.24.cloned.1.call-update) | async-done | bytes 1296
  717.4 138.7 %reduce-scatter.16.cloned.1.call-done = f32[32,1024]{1,0:T(8,128)} async-done(((f32[1024,1024]{1,0:T(8,128)}), f32[32,1024]{1,0:T(8,128)}) %reduce-scatter.16.cloned.1.call-update) | async-done | bytes 131088 | tf_op jit(solution)/shard_map/reduce_scatter | solution.py:169
  856.1 158.8 %reduce-scatter.22.cloned.1.call-done = f32[32,3072]{1,0:T(8,128)} async-done(((f32[1024,3072]{1,0:T(8,128)}), f32[32,3072]{1,0:T(8,128)}) %reduce-scatter.22.cloned.1.call-update) | async-done | bytes 393232
  1014.8 185.0 %reduce-scatter.20.cloned.1.call-done = f32[128,1024]{1,0:T(8,128)} async-done(((f32[4096,1024]{1,0:T(8,128)}), f32[128,1024]{1,0:T(8,128)}) %reduce-scatter.20.cloned.1.call-update) | async-done | bytes 524304 | tf_op jit(solution)/shard_map/reduce_scatter | solution.py:171
  1199.9 187.3 %reduce-scatter.18.cloned.1.call-done = f32[32,4096]{1,0:T(8,128)} async-done(((f32[1024,4096]{1,0:T(8,128)}), f32[32,4096]{1,0:T(8,128)}) %reduce-scatter.18.cloned.1.call-update) | async-done | bytes 524304 | tf_op jit(solution)/shard_map/reduce_scatter | solution.py:170
  (143 shorter events, 58.8 us)
Async XLA Ops:
  7.2 76.6 %all-gather.8.cloned.1.call-start = ((), (), s32[]{:S(2)}) async-start(), calls=%async_computation.7 | async-start | bytes 6488064 | tf_op jit(solution)/shard_map/all_gather | solution.py:43
  8.9 128.0 %all-gather.10.cloned.1.call-start = ((), (), s32[]{:S(2)}) async-start(), calls=%async_computation.8 | async-start | bytes 5242880 | tf_op jit(solution)/shard_map/all_gather | solution.py:68
  83.8 6.0 copy-start.18
  83.8 6.7 copy-start.16
  88.7 42.5 %copy-start.19 = (s32[2,128]{1,0:T(2,128)S(1)}, s32[2,128]{1,0:T(2,128)}, u32[]{:S(2)}) copy-start(s32[2,128]{1,0:T(2,128)} %param.12) | copy-start | bytes 3076
  88.7 47.7 %copy-start.20 = (s32[2]{0:T(128)S(1)}, s32[2]{0:T(128)}, u32[]{:S(2)}) copy-start(s32[2]{0:T(128)} %param.13) | copy-start | bytes 28
  89.8 93.1 %all-gather.12.cloned.1.call-start = ((), (), s32[]{:S(2)}) async-start(), calls=%async_computation.9 | async-start | bytes 2162688 | tf_op jit(solution)/shard_map/all_gather | solution.py:44
  90.5 172.1 %all-gather.14.cloned.1.call-start = ((), (), s32[]{:S(2)}) async-start(), calls=%async_computation.10 | async-start | bytes 8650752 | tf_op jit(solution)/shard_map/all_gather | solution.py:45
  91.3 250.8 %all-gather.16.cloned.1.call-start = ((), (), s32[]{:S(2)}) async-start(), calls=%async_computation.11 | async-start | bytes 8650752 | tf_op jit(solution)/shard_map/all_gather | solution.py:46
  92.1 355.4 %reduce-scatter.14.cloned.1.call-start = ((), (), s32[]{:S(2)}) async-start(), calls=%async_computation.12 | async-start | bytes 5242880 | tf_op jit(solution)/shard_map/reduce_scatter | solution.py:145
  136.6 10.2 copy-start.12
  136.9 9.9 copy-start.13
  141.4 5.5 copy-start.22
  146.8 6.6 copy-start.2
  154.5 28.4 %copy-start.9 = (bf16[2,128,1024]{2,1,0:T(8,128)(2,1)S(1)}, bf16[2,128,1024]{2,1,0:T(8,128)(2,1)}, u32[]{:S(2)}) copy-start(bf16[2,128,1024]{2,1,0:T(8,128)(2,1)} %param.11) | copy-start | bytes 1572868
  158.0 112.4 %copy-start.5 = (bf16[2,128,16,64]{1,0,3,2:T(2,128)(2,1)}, bf16[2,128,16,64]{1,0,3,2:T(2,128)(2,1)S(1)}, u32[]{:S(2)}) copy-start(bf16[2,128,16,64]{1,0,3,2:T(2,128)(2,1)S(1)} %copy.58) | copy-start | bytes 1572868
  342.1 9.3 slice-start.2
  342.1 7.6 copy-start.6
  342.1 9.3 slice-start.3
  350.1 6.1 slice-start
  351.7 4.6 slice-start.1
  366.2 6.7 copy-start.3
  366.2 6.7 copy-start.7
  383.7 9.4 copy-start.14
  404.3 179.5 %reduce-scatter.26.cloned.1.call-start = ((), (), s32[]{:S(2)}) async-start(), calls=%async_computation.18 | async-start | bytes 540672
  412.8 303.2 %reduce-scatter.24.cloned.1.call-start = ((), (), s32[]{:S(2)}) async-start(), calls=%async_computation.17 | async-start | bytes 540672
  449.9 406.1 %reduce-scatter.16.cloned.1.call-start = ((), (), s32[]{:S(2)}) async-start(), calls=%async_computation.13 | async-start | bytes 4325376 | tf_op jit(solution)/shard_map/reduce_scatter | solution.py:169
  453.8 561.0 %reduce-scatter.22.cloned.1.call-start = ((), (), s32[]{:S(2)}) async-start(), calls=%async_computation.16 | async-start | bytes 12976128
  479.7 720.2 %reduce-scatter.20.cloned.1.call-start = ((), (), s32[]{:S(2)}) async-start(), calls=%async_computation.15 | async-start | bytes 17301504 | tf_op jit(solution)/shard_map/reduce_scatter | solution.py:171
  490.1 897.1 %reduce-scatter.18.cloned.1.call-start = ((), (), s32[]{:S(2)}) async-start(), calls=%async_computation.14 | async-start | bytes 17301504 | tf_op jit(solution)/shard_map/reduce_scatter | solution.py:170
  500.0 85.2 %copy-start.8 = (bf16[2,128,2048]{2,1,0:T(8,128)(2,1)S(1)}, bf16[2,128,2048]{2,1,0:T(8,128)(2,1)}, u32[]{:S(2)}) copy-start(bf16[2,128,2048]{2,1,0:T(8,128)(2,1)} %reduce-scatter.14.cloned.1.call-done) | copy-start | bytes 3145732
  500.0 85.2 %copy-start.10 = (bf16[256,1024]{1,0:T(8,128)(2,1)S(1)}, bf16[256,1024]{1,0:T(8,128)(2,1)}, u32[]{:S(2)}) copy-start(bf16[256,1024]{1,0:T(8,128)(2,1)} %reshape.193) | copy-start | bytes 1572868
  (7 other events, 19.7 us)
Sparse Core Ops, SparseCore 0:
  11.5 72.2 all-gather.7
  89.9 33.0 all-gather.9
  126.5 56.3 all-gather.11
  186.2 76.4 all-gather.13
  265.9 76.1 all-gather.15
  404.4 43.0 reduce-scatter.13
  449.9 133.8 reduce-scatter.25
  586.0 129.9 reduce-scatter.23
  719.0 137.0 reduce-scatter.15
  863.5 151.2 reduce-scatter.21
  1017.7 182.1 reduce-scatter.19
  1202.6 184.5 reduce-scatter.17
where the time goes:
time: 1400 us; the launch traced here: 1390 us
  waiting for transfers between devices  1080 us (77%)
  blocking collectives  128 us (9%)
  matrix products  97.4 us (7%)
  local copies, waits for them, and re-layouts  51.9 us (4%)
  other arithmetic  24.2 us (2%)
  between operations  14.9 us (1%)
    unnamed x15, waiting for transfers between devices  328 us
    reduce_scatter x1, waiting for transfers between devices, local(): lax.psum_scatter(grad_expand, ('page', 'seq'), scatter_dimension=0, tiled...  187 us
    reduce_scatter x1, waiting for transfers between devices, local(): lax.psum_scatter(grad_reduce, ('page', 'seq'), scatter_dimension=0, tiled...  185 us
    reduce_scatter x1, waiting for transfers between devices, local(): lax.psum_scatter(grad_mix, ('page', 'seq'), scatter_dimension=0, tiled=True)  139 us
    all_gather x1, waiting for transfers between devices, local(): lax.all_gather(w_up.astype(jnp.bfloat16), ('page', 'seq'), axis=0, tiled=...  77 us
    all_gather x1, waiting for transfers between devices, local(): lax.all_gather(w_down.astype(jnp.bfloat16), ('page', 'seq'), axis=0, tile...  71.7 us
    all_gather x1, blocking collectives, local(): lax.all_gather(biases.astype(jnp.bfloat16), ('page', 'seq'), axis=1, tile...  44 us
    psum x1, blocking collectives, local(): cell_total = lax.psum(grad_cell_local, ('page', 'seq'))  39.6 us
  transfers between devices with their start and end apart: 12, of which 11 were waited for; matrix products, arithmetic and copies ran while one was open for 7% of the time, Pallas kernels for 0%

commit v1 on v0

v1 whole, which is shorter than its diff:
```python
import jax
import jax.numpy as jnp
from jax import lax
from jax.sharding import PartitionSpec as P

LOW = jnp.bfloat16
WIDE = jnp.float32


def layer_norm(values, gain, shift):
    center = values - jnp.mean(values, axis=-1, keepdims=True)
    spread = jnp.mean(center * center, axis=-1, keepdims=True)
    return center * lax.rsqrt(spread + 1e-05) * gain + shift


def gelu_exact(values):
    return 0.5 * values * (1.0 + jax.scipy.special.erf(values * 0.7071067811865476))


def swap(values, axis, count, mask):
    return lax.ppermute(values, axis, [(i, i ^ mask) for i in range(count)])


def bits_of(count):
    return [1 << k for k in range(count.bit_length() - 1)]


def gather_bits(values, axis, count, dim, order):
    index = lax.axis_index(axis)
    done = []
    for mask in order:
        other = swap(values, axis, count, mask)
        place = dim + sum(1 for m in done if m > mask)
        first = ((index // mask) % 2) == 0
        values = jnp.stack(
            [jnp.where(first, values, other), jnp.where(first, other, values)], axis=place
        )
        done.append(mask)
    shape = values.shape
    rest = shape[dim + len(order):]
    return values.reshape(shape[:dim] + (count,) + rest)


def scatter_bits(values, axis, count, dim, order):
    index = lax.axis_index(axis)
    left = sorted(order, reverse=True)
    shape = values.shape
    values = values.reshape(shape[:dim] + (2,) * len(left) + shape[dim + 1:])
    for mask in order:
        at = dim + left.index(mask)
        bit = (index // mask) % 2
        keep = lax.dynamic_index_in_dim(values, bit, at, keepdims=False)
        send = lax.dynamic_index_in_dim(values, 1 - bit, at, keepdims=False)
        values = keep.astype(WIDE) + swap(send.astype(LOW), axis, count, mask).astype(WIDE)
        left.remove(mask)
    return values


def local(counts, tokens, cells, lengths, cotangent, w_qkv, w_out, w_up, w_down, biases, gains, cell_bias):
    pages, seqs = counts
    page_count, row_count, width = tokens.shape
    slots = row_count * seqs
    heads = cell_bias.shape[0]
    depth = width // heads
    heads_here = heads // seqs
    span = heads_here * depth
    flat = page_count * row_count
    rows = w_qkv.shape[0]
    ff_rows = w_down.shape[0]
    ff_here = ff_rows * pages
    seq_index = lax.axis_index("seq")
    high_page = bits_of(pages)[::-1]
    low_page = bits_of(pages)
    high_seq = bits_of(seqs)[::-1]
    low_seq = bits_of(seqs)

    def gather_seq(values, dim):
        return gather_bits(values, "seq", seqs, dim, high_seq)

    def scatter_seq(values, dim):
        return scatter_bits(values, "seq", seqs, dim, low_seq)

    def turn(values):
        return lax.all_to_all(values, "seq", 0, 0)

    part_qkv = w_qkv.astype(LOW).reshape(rows, 3, seqs, span).transpose(2, 0, 1, 3)
    part_qkv = turn(part_qkv.reshape(seqs, rows, 3 * span)).reshape(seqs * rows, 3 * span)
    w_proj = gather_bits(part_qkv, "page", pages, 0, high_page).reshape(width, 3 * span)
    small = jnp.concatenate([biases, gains], axis=0).astype(LOW)
    small_rows = small.shape[0]
    small_pad = -(-small.size // width)
    small_pad = -(-small_pad // 8) * 8
    small_flat = jnp.pad(small.reshape(-1), (0, small_pad * width - small.size)).reshape(small_pad, width)
    both = lax.all_gather(
        jnp.concatenate([w_out.astype(LOW), small_flat], axis=0), ("page", "seq"), axis=0, tiled=False
    )
    w_mix = both[:, :rows].reshape(width, width)
    lanes = small.shape[1]
    vectors = both[:, rows:].reshape(pages * seqs, small_pad * width)[:, : small.size]
    vectors = vectors.reshape(pages * seqs, small_rows, lanes).transpose(1, 0, 2)
    vectors = vectors.reshape(small_rows, width).astype(WIDE)
    scales = vectors[small_rows - 2:]
    part_up = w_up.astype(LOW).reshape(rows, pages, seqs, ff_rows).transpose(2, 0, 1, 3)
    part_up = turn(part_up.reshape(seqs, rows, ff_here)).reshape(seqs * rows, ff_here)
    w_expand = gather_bits(part_up, "page", pages, 0, high_page).reshape(width, ff_here)
    w_reduce = gather_bits(w_down.astype(LOW), "page", pages, 0, high_page).reshape(ff_here, width)
    hidden_bias = vectors[6:10].reshape(pages, seqs, ff_rows)
    hidden_bias = lax.dynamic_index_in_dim(hidden_bias, seq_index, 1, keepdims=False).reshape(ff_here)

    everything = gather_seq(tokens, 1).reshape(page_count * slots, width)
    cells_all = lax.all_gather(cells, "seq", axis=1, tiled=True)
    bias_q = lax.dynamic_slice_in_dim(vectors[0], seq_index * span, span)
    bias_v = lax.dynamic_slice_in_dim(vectors[1], seq_index * span, span)
    bias_qkv = jnp.concatenate([bias_q, jnp.zeros_like(bias_q), bias_v])
    projected = (jnp.dot(everything, w_proj, preferred_element_type=WIDE) + bias_qkv).astype(LOW)
    projected = projected.reshape(page_count, slots, 3, heads_here, depth)
    query, keys, values = projected[:, :, 0], projected[:, :, 1], projected[:, :, 2]
    own_bias = lax.dynamic_slice_in_dim(cell_bias, seq_index * heads_here, heads_here)
    same_cell = (cells_all[:, :, None] == cells_all[:, None, :]).astype(WIDE)
    key_valid = lax.broadcasted_iota(jnp.int32, (page_count, slots), 1) < lengths[:, None]

    def scores_of():
        raw = jnp.einsum("pqhe,pkhe->phqk", query, keys, preferred_element_type=WIDE) * 0.125
        scores = raw + own_bias[None, :, None, None] * same_cell[:, None]
        return jnp.where(key_valid[:, None, None, :], scores, -1e30)

    scores = scores_of()
    peak = jnp.max(scores, axis=-1, keepdims=True)
    exponent = jnp.exp(scores - peak)
    totals = jnp.sum(exponent, axis=-1, keepdims=True)
    log_total = peak + jnp.log(totals)
    weights_low = (exponent / totals).astype(LOW)
    context_here = jnp.einsum("phqk,pkhe->pqhe", weights_low, values, preferred_element_type=WIDE)
    context_here = context_here.astype(LOW).reshape(page_count, seqs, row_count, span)
    context = turn(context_here.transpose(1, 0, 2, 3)).transpose(1, 2, 0, 3).reshape(flat, width)

    inputs_wide = tokens.reshape(flat, width).astype(WIDE)
    attended = jnp.dot(context, w_mix, preferred_element_type=WIDE) + vectors[2]
    normed, norm_first = jax.vjp(layer_norm, inputs_wide + attended, scales[0], vectors[4])
    normed_all = gather_seq(normed.astype(LOW), 0).reshape(seqs * flat, width)
    expanded = jnp.dot(normed_all, w_expand, preferred_element_type=WIDE) + hidden_bias
    activated, gelu_back = jax.vjp(gelu_exact, expanded)
    activated_low = activated.astype(LOW)
    reduced = jnp.dot(activated_low, w_reduce, preferred_element_type=WIDE)
    reduced = scatter_seq(reduced.reshape(seqs, flat, width), 0) + vectors[3]
    output_wide, norm_second = jax.vjp(layer_norm, normed + reduced, scales[1], vectors[5])
    output = output_wide.astype(LOW).reshape(page_count, row_count, width)

    grad_second, grad_gain_two, grad_shift_two = norm_second(cotangent.reshape(flat, width).astype(WIDE))
    second_all = gather_seq(grad_second.astype(LOW), 0).reshape(seqs * flat, width)
    grad_activated = jnp.einsum("td,fd->tf", second_all, w_reduce, preferred_element_type=WIDE)
    grad_expanded = gelu_back(grad_activated)[0]
    expanded_low = grad_expanded.astype(LOW)
    grad_normed = jnp.einsum("tf,df->td", expanded_low, w_expand, preferred_element_type=WIDE)
    grad_normed = grad_second + scatter_seq(grad_normed.reshape(seqs, flat, width), 0)
    grad_reduce = jnp.einsum("tf,td->fd", activated_low, second_all, preferred_element_type=WIDE)
    grad_reduce = scatter_bits(grad_reduce.reshape(pages, ff_rows, width), "page", pages, 0, low_page)
    grad_expand = jnp.einsum("td,tf->df", normed_all, expanded_low, preferred_element_type=WIDE)
    grad_expand = scatter_bits(grad_expand.reshape(pages, seqs * rows, ff_here), "page", pages, 0, low_page)
    grad_expand = turn(grad_expand.astype(LOW).reshape(seqs, rows, ff_here))
    grad_expand = grad_expand.reshape(seqs, rows, pages, ff_rows).transpose(1, 2, 0, 3)
    grad_expand = grad_expand.reshape(rows, seqs * ff_here).astype(WIDE)
    grad_first, grad_gain_one, grad_shift_one = norm_first(grad_normed)
    first_low = grad_first.astype(LOW)
    grad_context = jnp.einsum("td,cd->tc", first_low, w_mix, preferred_element_type=WIDE).astype(LOW)
    grad_context = grad_context.reshape(page_count, row_count, seqs, span).transpose(2, 0, 1, 3)
    grad_context = turn(grad_context).transpose(1, 0, 2, 3).reshape(page_count, slots, heads_here, depth)
    grad_mix = jnp.einsum("tc,td->cd", context, first_low, preferred_element_type=WIDE)
    grad_mix = scatter_bits(grad_mix.reshape(pages, seqs, rows, width), "seq", seqs, 1, low_seq)
    grad_mix = scatter_bits(grad_mix, "page", pages, 0, low_page)

    weights_wide = jnp.exp(scores_of() - log_total)
    weights_low = weights_wide.astype(LOW)
    grad_weights = jnp.einsum("pqhe,pkhe->phqk", grad_context, values, preferred_element_type=WIDE)
    inner = jnp.sum(weights_wide * grad_weights, axis=-1, keepdims=True)
    grad_scores = weights_wide * (grad_weights - inner)
    grad_cell = jnp.sum(grad_scores * same_cell[:, None], axis=(0, 2, 3))
    scores_low = grad_scores.astype(LOW)
    grad_values = jnp.einsum("phqk,pqhe->pkhe", weights_low, grad_context, preferred_element_type=WIDE)
    grad_query = jnp.einsum("phqk,pkhe->pqhe", scores_low, keys, preferred_element_type=WIDE) * 0.125
    grad_keys = jnp.einsum("phqk,pqhe->pkhe", scores_low, query, preferred_element_type=WIDE) * 0.125
    grad_proj_low = jnp.stack([grad_query, grad_keys, grad_values], axis=2).astype(LOW)
    grad_proj_low = grad_proj_low.reshape(page_count * slots, 3 * span)
    grad_proj = jnp.einsum("td,tc->dc", everything, grad_proj_low, preferred_element_type=WIDE)
    grad_proj = scatter_bits(grad_proj.reshape(pages, seqs * rows, 3 * span), "page", pages, 0, low_page)
    grad_proj = turn(grad_proj.astype(LOW).reshape(seqs, rows, 3 * span))
    grad_proj = grad_proj.reshape(seqs, rows, 3, span).transpose(1, 2, 0, 3).reshape(rows, 3 * width)
    grad_proj = grad_proj.astype(WIDE)
    grad_inputs = jnp.einsum("tc,dc->td", grad_proj_low, w_proj, preferred_element_type=WIDE)
    grad_inputs = scatter_seq(grad_inputs.reshape(page_count, seqs, row_count, width), 1)
    grad_inputs = grad_first.reshape(page_count, row_count, width) + grad_inputs

    def place(vector, size):
        blank = jnp.zeros((width,), WIDE)
        return lax.dynamic_update_slice_in_dim(blank, vector, seq_index * size, 0)

    hidden = jnp.sum(grad_expanded, axis=0).reshape(pages, 1, ff_rows)
    hidden = lax.dynamic_update_slice_in_dim(
        jnp.zeros((pages, seqs, ff_rows), WIDE), hidden, seq_index, 1
    ).reshape(4, width)
    head_rows = jnp.stack(
        [
            place(jnp.sum(grad_query, axis=(0, 1)).reshape(span), span),
            place(jnp.sum(grad_values, axis=(0, 1)).reshape(span), span),
            jnp.sum(grad_first, axis=0),
            jnp.sum(grad_second, axis=0),
            grad_shift_one,
            grad_shift_two,
        ]
    )
    table = jnp.concatenate(
        [
            head_rows,
            hidden,
            grad_gain_one[None],
            grad_gain_two[None],
            place(grad_cell, heads_here)[None],
        ],
        axis=0,
    )
    for mask in low_seq:
        table = table + swap(table, "seq", seqs, mask)
    for mask in low_page:
        table = table + swap(table, "page", pages, mask)
    own = lax.axis_index("page") * seqs + seq_index
    mine = lax.dynamic_slice_in_dim(table, own * lanes, lanes, axis=1)
    return (
        output,
        grad_inputs,
        grad_proj,
        grad_mix,
        grad_expand,
        grad_reduce,
        mine[:10],
        mine[10:12],
        table[12, :heads],
    )


def solution(mesh):
    counts = (mesh.shape["page"], mesh.shape["seq"])
    placed = (
        P("page", "seq", None),
        P("page", "seq"),
        P("page"),
        P("page", "seq", None),
        P(("page", "seq"), None),
        P(("page", "seq"), None),
        P(("page", "seq"), None),
        P(("page", "seq"), None),
        P(None, ("page", "seq")),
        P(None, ("page", "seq")),
        P(),
    )

    def step(*args):
        return local(counts, *args)

    return jax.shard_map(
        step,
        mesh=mesh,
        in_specs=placed,
        out_specs=(
            P("page", "seq", None),
            P("page", "seq", None),
            P(("page", "seq"), None),
            P(("page", "seq"), None),
            P(("page", "seq"), None),
            P(("page", "seq"), None),
            P(None, ("page", "seq")),
            P(None, ("page", "seq")),
            P(),
        ),
        check_vma=False,
    )
```

time: 1400 us -> 507 us (0.36)
  waiting for transfers between devices: 1080 us -> 166 us
  blocking collectives: 128 us -> 12.6 us
  starting transfers between devices: 0.5 us -> 73.7 us
  local copies, waits for them, and re-layouts: 51.9 us -> 109 us
  matrix products: 97.4 us -> 52.9 us
  other arithmetic: 24.2 us -> 66.7 us
    reduce_scatter x4 -> x0, waiting for transfers between devices: 546 us -> none  [the longest x1 187 us: local(): lax.psum_scatter(grad_expand, ('page', 'seq'), scatter_dimension=0, tiled...]
    unnamed x15 -> x1, waiting for transfers between devices: 328 us -> 0.02 us
    all_gather x5 -> x1, waiting for transfers between devices: 203 us -> 0.01 us  [local(): lax.all_gather(jnp.concatenate([w_out.astype(LOW), small_flat], axis=0),...]
    ppermute x0 -> x40, waiting for transfers between devices: none -> 161 us  [swap(): return lax.ppermute(values, axis, [(i, i ^ mask) for i in range(count)])]
    all_gather x3 -> x1, blocking collectives: 88.1 us -> 12.6 us  [local(): cells_all = lax.all_gather(cells, 'seq', axis=1, tiled=True)]
    ppermute x0 -> x40, starting transfers between devices: none -> 50 us  [swap(): return lax.ppermute(values, axis, [(i, i ^ mask) for i in range(count)])]
    dot_general x15, matrix products: 80.9 us -> 40.9 us  [the longest x1 4.97 us: local(): jnp.dot(everything, w_proj, preferred_element_type=WIDE) + bias_qkv]
    psum x1 -> x0, blocking collectives: 39.6 us -> none  [local(): cell_total = lax.psum(grad_cell_local, ('page', 'seq'))]
  transfers between devices with their start and end apart: 12 -> 47, of which waited for: 11 -> 21; matrix products, arithmetic and copies ran while one was open for 7% -> 36% of each run, Pallas kernels for 0% -> 0%
where the time goes in v1:
time: 507 us; the launch traced here: 497 us
  waiting for transfers between devices  166 us (33%)
  local copies, waits for them, and re-layouts  109 us (21%)
  starting transfers between devices  73.7 us (15%)
  other arithmetic  66.7 us (13%)
  matrix products  52.9 us (10%)
  between operations  16 us (3%)
  blocking collectives  12.6 us (2%)
    ppermute x40, waiting for transfers between devices, swap(): return lax.ppermute(values, axis, [(i, i ^ mask) for i in range(count)])  161 us
    ppermute x40, starting transfers between devices, swap(): return lax.ppermute(values, axis, [(i, i ^ mask) for i in range(count)])  50 us
    another operation x30, other arithmetic, gather_bits(): jnp.stack([jnp.where(first, values, other), jnp.where(first, other, value...  24.8 us
    unnamed x130, local copies, waits for them, and re-layouts  24.1 us
    all_to_all x6, starting transfers between devices, turn(): return lax.all_to_all(values, 'seq', 0, 0)  23.7 us
    add x15, other arithmetic, scatter_bits(): keep.astype(WIDE) + swap(send.astype(LOW), axis, count, mask).astype(WIDE)  20.7 us
    convert_element_type x3, local copies, waits for them, and re-layouts, local(): jnp.stack([grad_query, grad_keys, grad_values], axis=2).astype(LOW)  13.5 us
    dot_general x1, local copies, waits for them, and re-layouts, local(): jnp.einsum('tf,td->fd', activated_low, second_all, preferred_element_type...  13.2 us
  transfers between devices with their start and end apart: 47, of which 21 were waited for; matrix products, arithmetic and copies ran while one was open for 36% of the time, Pallas kernels for 0%

profile of v1, /device:TPU:0, one launch (start us, length us, event | category | flops | bytes accessed | tf_op | source)
XLA Modules:
  0.0 497.4 jit_solution(14796424124524267543)
XLA Ops:
  12.6 4.2 all-to-all-start
  23.9 12.6 %all_gather.11 = s32[2,512]{1,0:T(2,128)S(1)} all-gather(s32[2,128]{1,0:T(2,128)S(1)} %copy-done.56), channel_id=1, replica_groups=mesh['page'=8,'seq'=4] {'seq'}, dimensions={1}, use_global_device_ids=true | all-gather | bytes 5120 | tf_op jit(solution)/shard_map/all_gather | solution.py:111
  36.5 4.2 all-to-all-start.2
  42.6 13.6 %collective-permute-done.2 = bf16[128,768]{1,0:T(8,128)(2,1)S(1)} collective-permute-done((bf16[128,768]{1,0:T(8,128)(2,1)S(1)}, bf16[128,768]{1,0:T(8,128)(2,1)S(1)}, u32[]{:S(2)}, u32[]{:S(2)}) %collective-permute-start.2) | collective-permute-done | bytes 196640 | tf_op jit(solution)/shard_map/ppermute | solution.py:21
  61.4 18.7 %collective-permute-done.3 = bf16[2,128,768]{2,1,0:T(8,128)(2,1)} collective-permute-done((bf16[2,128,768]{2,1,0:T(8,128)(2,1)}, bf16[2,128,768]{2,1,0:T(8,128)(2,1)}, u32[]{:S(2)}, u32[]{:S(2)}) %collective-permute-start.3) | collective-permute-done | bytes 393248 | tf_op jit(solution)/shard_map/ppermute | solution.py:21
  89.0 7.7 %collective-permute-done.4 = bf16[2,2,128,768]{3,2,1,0:T(8,128)(2,1)S(1)} collective-permute-done((bf16[2,2,128,768]{3,2,1,0:T(8,128)(2,1)S(1)}, bf16[2,2,128,768]{3,2,1,0:T(8,128)(2,1)S(1)}, u32[]{:S(2)}, u32[]{:S(2)}) %collective-permute-start.4) | collective-permute-done | bytes 786464 | tf_op jit(solution)/shard_map/ppermute | solution.py:21
  101.9 5.0 add_convert_fusion
  106.9 5.7 %reshape.329 = bf16[2,512,3,4,64]{4,3,2,1,0:T(4,128)(2,1)} reshape(bf16[1024,768]{1,0:T(8,128)(2,1)} %add_convert_fusion) | data formatting | bytes 3145728 | tf_op jit(solution)/shard_map/reshape | solution.py:116
  112.6 4.3 fusion.69
  132.6 4.1 all-to-all-start.1
  141.2 4.5 all-to-all-done.1
  154.6 9.5 %collective-permute-done.5 = bf16[256,1024]{1,0:T(8,128)(2,1)} collective-permute-done((bf16[256,1024]{1,0:T(8,128)(2,1)S(1)}, bf16[256,1024]{1,0:T(8,128)(2,1)}, u32[]{:S(2)}, u32[]{:S(2)}) %collective-permute-start.5) | collective-permute-done | bytes 524320 | tf_op jit(solution)/shard_map/ppermute | solution.py:21
  169.7 17.9 %collective-permute-done.9 = bf16[2,2,128,1024]{3,2,0,1:T(8,128)(2,1)} collective-permute-done((bf16[2,2,128,1024]{3,2,0,1:T(8,128)(2,1)}, bf16[2,2,128,1024]{3,2,0,1:T(8,128)(2,1)}, u32[]{:S(2)}, u32[]{:S(2)}) %collective-permute-start.9) | collective-permute-done | bytes 1048608 | tf_op jit(solution)/shard_map/ppermute | solution.py:21
  195.8 4.2 multiply_convert_fusion
  212.3 12.4 %collective-permute-done.14 = bf16[256,1024]{1,0:T(8,128)(2,1)} collective-permute-done((bf16[256,1024]{1,0:T(8,128)(2,1)}, bf16[256,1024]{1,0:T(8,128)(2,1)}, u32[]{:S(2)}, u32[]{:S(2)}) %collective-permute-start.14) | collective-permute-done | bytes 524320 | tf_op jit(solution)/shard_map/ppermute | solution.py:21
  230.1 11.5 %collective-permute-done.15 = bf16[256,1024]{1,0:T(8,128)(2,1)S(1)} collective-permute-done((bf16[256,1024]{1,0:T(8,128)(2,1)S(1)}, bf16[256,1024]{1,0:T(8,128)(2,1)S(1)}, u32[]{:S(2)}, u32[]{:S(2)}) %collective-permute-start.15) | collective-permute-done | bytes 524320 | tf_op jit(solution)/shard_map/ppermute | solution.py:21
  243.8 4.0 copy.136
  247.8 4.0 copy.143
  251.7 13.2 %copy.159 = bf16[1024,1024]{1,0:T(8,128)(2,1)} copy(bf16[1024,1024]{0,1:T(8,128)(2,1)} %bitcast.380) | data formatting | bytes 4194304 | tf_op jit(solution)/shard_map/tf,td->fd/dot_general | solution.py:156
  269.2 4.4 fusion.62
  297.0 11.9 %collective-permute-done.29 = bf16[2,2,128,1024]{3,2,1,0:T(8,128)(2,1)} collective-permute-done((bf16[2,2,128,1024]{3,2,1,0:T(8,128)(2,1)}, bf16[2,2,128,1024]{3,2,1,0:T(8,128)(2,1)}, u32[]{:S(2)}, u32[]{:S(2)}) %collective-permute-start.29) | collective-permute-done | bytes 1048608 | tf_op jit(solution)/shard_map/ppermute | solution.py:21
  311.7 19.4 %collective-permute-done.32 = bf16[2,2,128,1024]{3,2,1,0:T(8,128)(2,1)} collective-permute-done((bf16[2,2,128,1024]{3,2,1,0:T(8,128)(2,1)}, bf16[2,2,128,1024]{3,2,1,0:T(8,128)(2,1)}, u32[]{:S(2)}, u32[]{:S(2)}) %collective-permute-start.32) | collective-permute-done | bytes 1048608 | tf_op jit(solution)/shard_map/ppermute | solution.py:21
  341.9 4.1 all-to-all-start.3
  347.5 7.2 %collective-permute-start.31 = (bf16[128,1024]{1,0:T(8,128)(2,1)S(1)}, bf16[128,1024]{1,0:T(8,128)(2,1)S(1)}, u32[]{:S(2)}, u32[]{:S(2)}) collective-permute-start(bf16[128,1024]{1,0:T(8,128)(2,1)S(1)} %fusion.52), channel_id=1, source_target_pairs={{0,16},{4,20},{8,24},{12,28},{16,0},{20,4},{24,8},{28,12},{1,17},{... | collective-permute-start | bytes 786440 | tf_op jit(solution)/shard_map/ppermute | solution.py:21
  361.1 11.2 %collective-permute-done.31 = bf16[128,1024]{1,0:T(8,128)(2,1)S(1)} collective-permute-done((bf16[128,1024]{1,0:T(8,128)(2,1)S(1)}, bf16[128,1024]{1,0:T(8,128)(2,1)S(1)}, u32[]{:S(2)}, u32[]{:S(2)}) %collective-permute-start.31) | collective-permute-done | bytes 262176 | tf_op jit(solution)/shard_map/ppermute | solution.py:21
  378.3 4.9 fusion.9
  383.2 5.4 %multiply_reduce_fusion.1 = (f32[2,4,512]{2,1,0:T(4,128)S(1)}, f32[2,4,512,512]{2,3,1,0:T(8,128)S(1)}) fusion(f32[2,4,512,512]{2,3,1,0:T(8,128)} %copy-done, f32[2,4,512]{2,1,0:T(4,128)S(1)} %bitcast.403, bf16[2,512,4,64]{1,3,2,0:T(8,128)(2,1)S(1)} %reshape.300, bf16[2,512,1,4,64]{1,4,3,0,2:T(8,128)(2,1)S(1)} %copy-done.38), kind=kOutput, calls=%fused_computation.2 | convolution fusion | flops 274722816 | bytes 17858560 | tf_op jit(solution)/shard_map/pqhe,pkhe->phqk/dot_general | solution.py:174
  400.6 3.8 reshape.328
  404.5 3.9 fusion.79
  416.6 5.9 %reshape.325 = bf16[2,2,2,128,768]{4,3,2,1,0:T(8,128)(2,1)} reshape(bf16[2,512,3,4,64]{4,3,2,1,0:T(4,128)(2,1)} %copy.157) | data formatting | bytes 3145728 | tf_op jit(solution)/shard_map/convert_element_type | solution.py:182
  426.3 9.7 %collective-permute-done.37 = f32[13,1024]{1,0:T(8,128)S(1)} collective-permute-done((f32[13,1024]{1,0:T(8,128)S(1)}, f32[13,1024]{1,0:T(8,128)S(1)}, u32[]{:S(2)}, u32[]{:S(2)}) %collective-permute-start.37) | collective-permute-done | bytes 53280 | tf_op jit(solution)/shard_map/ppermute | solution.py:21
  454.8 5.4 %collective-permute-done.25 = bf16[8,32,1024]{2,1,0:T(8,128)(2,1)S(1)} collective-permute-done((bf16[8,32,1024]{2,1,0:T(8,128)(2,1)S(1)}, bf16[8,32,1024]{2,1,0:T(8,128)(2,1)S(1)}, u32[]{:S(2)}, u32[]{:S(2)}) %collective-permute-start.25) | collective-permute-done | bytes 524320 | tf_op jit(solution)/shard_map/ppermute | solution.py:21
  (391 shorter events, 222.9 us)
Async XLA Ops:
  7.2 92.6 %all-gather.3.cloned.1.call-start = ((), (), s32[]{:S(2)}) async-start(), calls=%async_computation.6 | async-start | bytes 2703360 | tf_op jit(solution)/shard_map/all_gather | solution.py:94
  12.6 23.9 %all-to-all-start = ((bf16[4,32,768]{2,1,0:T(8,128)(2,1)}), bf16[4,32,768]{2,1,0:T(8,128)(2,1)S(1)}, u32[]{:S(2)}, u32[]{:S(2)}) async-start(bf16[4,32,768]{2,1,0:T(8,128)(2,1)} %reshape.285), calls=%async_computation | async-start | bytes 393216 | tf_op jit(solution)/shard_map/all_to_all | solution.py:84
  17.6 65.4 %collective-permute-start.10 = (bf16[128,1024]{1,0:T(8,128)(2,1)}, bf16[128,1024]{1,0:T(8,128)(2,1)}, u32[]{:S(2)}, u32[]{:S(2)}) collective-permute-start(bf16[128,1024]{1,0:T(8,128)(2,1)} %convert_element_type.340), channel_id=1, source_target_pairs={{0,16},{4,20},{8,24},{12,28},{16,0},{20,4},{24,8},{28,12},{1,17},{... | collective-permute-start | bytes 786440 | tf_op jit(solution)/shard_map/ppermute | solution.py:21
  20.8 39.3 %collective-permute-start = (bf16[2,128,1024]{2,1,0:T(8,128)(2,1)}, bf16[2,128,1024]{2,1,0:T(8,128)(2,1)}, u32[]{:S(2)}, u32[]{:S(2)}) collective-permute-start(bf16[2,128,1024]{2,1,0:T(8,128)(2,1)} %param.11), channel_id=1, source_target_pairs={{0,2},{1,3},{2,0},{3,1},{4,6},{5,7},{6,4},{7,5},{8,10},{9,11},{10,... | collective-permute-start | bytes 1572872 | tf_op jit(solution)/shard_map/ppermute | solution.py:21
  36.5 20.6 %all-to-all-start.2 = ((bf16[4,32,1024]{2,1,0:T(8,128)(2,1)}), bf16[4,32,1024]{2,1,0:T(8,128)(2,1)}, u32[]{:S(2)}, u32[]{:S(2)}) async-start(bf16[4,32,1024]{2,1,0:T(8,128)(2,1)} %reshape.294), calls=%async_computation.2 | async-start | bytes 524288 | tf_op jit(solution)/shard_map/all_to_all | solution.py:84
  40.7 15.5 %collective-permute-start.2 = (bf16[128,768]{1,0:T(8,128)(2,1)S(1)}, bf16[128,768]{1,0:T(8,128)(2,1)S(1)}, u32[]{:S(2)}, u32[]{:S(2)}) collective-permute-start(bf16[128,768]{1,0:T(8,128)(2,1)S(1)} %bitcast.399), channel_id=1, source_target_pairs={{0,16},{4,20},{8,24},{12,28},{16,0},{20,4},{24,8},{28,12},{1,17},{... | collective-permute-start | bytes 589832 | tf_op jit(solution)/shard_map/ppermute | solution.py:21
  57.1 23.0 %collective-permute-start.3 = (bf16[2,128,768]{2,1,0:T(8,128)(2,1)}, bf16[2,128,768]{2,1,0:T(8,128)(2,1)}, u32[]{:S(2)}, u32[]{:S(2)}) collective-permute-start(bf16[2,128,768]{2,1,0:T(8,128)(2,1)} %pad_maximum_fusion.15), channel_id=1, source_target_pairs={{0,8},{4,12},{8,0},{12,4},{16,24},{20,28},{24,16},{28,20},{1,9},{5... | collective-permute-start | bytes 1179656 | tf_op jit(solution)/shard_map/ppermute | solution.py:21
  57.1 27.8 %collective-permute-start.7 = (bf16[128,1024]{1,0:T(8,128)(2,1)}, bf16[128,1024]{1,0:T(8,128)(2,1)S(1)}, u32[]{:S(2)}, u32[]{:S(2)}) collective-permute-start(bf16[128,1024]{1,0:T(8,128)(2,1)} %bitcast.36), channel_id=1, source_target_pairs={{0,16},{4,20},{8,24},{12,28},{16,0},{20,4},{24,8},{28,12},{1,17},{... | collective-permute-start | bytes 786440 | tf_op jit(solution)/shard_map/ppermute | solution.py:21
  81.2 15.5 %collective-permute-start.4 = (bf16[2,2,128,768]{3,2,1,0:T(8,128)(2,1)S(1)}, bf16[2,2,128,768]{3,2,1,0:T(8,128)(2,1)S(1)}, u32[]{:S(2)}, u32[]{:S(2)}) collective-permute-start(bf16[2,2,128,768]{3,2,1,0:T(8,128)(2,1)S(1)} %pad_maximum_fusion.12), channel_id=1, source_target_pairs={{0,4},{4,0},{8,12},{12,8},{16,20},{20,16},{24,28},{28,24},{1,5},{5... | collective-permute-start | bytes 2359304 | tf_op jit(solution)/shard_map/ppermute | solution.py:21
  82.9 15.2 %collective-permute-start.1 = (bf16[2,2,128,1024]{3,2,1,0:T(8,128)(2,1)S(1)}, bf16[2,2,128,1024]{3,2,1,0:T(8,128)(2,1)S(1)}, u32[]{:S(2)}, u32[]{:S(2)}) collective-permute-start(bf16[2,2,128,1024]{3,2,1,0:T(8,128)(2,1)S(1)} %pad_maximum_fusion.7), channel_id=1, source_target_pairs={{0,1},{1,0},{2,3},{3,2},{4,5},{5,4},{6,7},{7,6},{8,9},{9,8},{10,11... | collective-permute-start | bytes 3145736 | tf_op jit(solution)/shard_map/ppermute | solution.py:21
  85.0 51.8 %collective-permute-start.11 = (bf16[2,128,1024]{2,1,0:T(8,128)(2,1)}, bf16[2,128,1024]{2,1,0:T(8,128)(2,1)}, u32[]{:S(2)}, u32[]{:S(2)}) collective-permute-start(bf16[2,128,1024]{2,1,0:T(8,128)(2,1)} %pad_maximum_fusion.14), channel_id=1, source_target_pairs={{0,8},{4,12},{8,0},{12,4},{16,24},{20,28},{24,16},{28,20},{1,9},{5... | collective-permute-start | bytes 1572872 | tf_op jit(solution)/shard_map/ppermute | solution.py:21
  87.0 63.9 %collective-permute-start.8 = (bf16[2,128,1024]{2,1,0:T(8,128)(2,1)}, bf16[2,128,1024]{2,1,0:T(8,128)(2,1)}, u32[]{:S(2)}, u32[]{:S(2)}) collective-permute-start(bf16[2,128,1024]{2,1,0:T(8,128)(2,1)} %pad_maximum_fusion.13), channel_id=1, source_target_pairs={{0,8},{4,12},{8,0},{12,4},{16,24},{20,28},{24,16},{28,20},{1,9},{5... | collective-permute-start | bytes 1572872 | tf_op jit(solution)/shard_map/ppermute | solution.py:21
  139.3 27.3 %collective-permute-start.12 = (bf16[2,2,128,1024]{3,2,0,1:T(8,128)(2,1)}, bf16[2,2,128,1024]{3,2,0,1:T(8,128)(2,1)}, u32[]{:S(2)}, u32[]{:S(2)}) collective-permute-start(bf16[2,2,128,1024]{3,2,0,1:T(8,128)(2,1)} %pad_maximum_fusion.10), channel_id=1, source_target_pairs={{0,4},{4,0},{8,12},{12,8},{16,20},{20,16},{24,28},{28,24},{1,5},{5... | collective-permute-start | bytes 3145736 | tf_op jit(solution)/shard_map/ppermute | solution.py:21
  153.1 34.5 %collective-permute-start.9 = (bf16[2,2,128,1024]{3,2,0,1:T(8,128)(2,1)}, bf16[2,2,128,1024]{3,2,0,1:T(8,128)(2,1)}, u32[]{:S(2)}, u32[]{:S(2)}) collective-permute-start(bf16[2,2,128,1024]{3,2,0,1:T(8,128)(2,1)} %pad_maximum_fusion.9), channel_id=1, source_target_pairs={{0,4},{4,0},{8,12},{12,8},{16,20},{20,16},{24,28},{28,24},{1,5},{5... | collective-permute-start | bytes 3145736 | tf_op jit(solution)/shard_map/ppermute | solution.py:21
  166.6 25.3 %collective-permute-start.6 = (bf16[2,256,1024]{2,1,0:T(8,128)(2,1)}, bf16[2,256,1024]{2,1,0:T(8,128)(2,1)}, u32[]{:S(2)}, u32[]{:S(2)}) collective-permute-start(bf16[2,256,1024]{2,1,0:T(8,128)(2,1)} %pad_maximum_fusion.8), channel_id=1, source_target_pairs={{0,1},{1,0},{2,3},{3,2},{4,5},{5,4},{6,7},{7,6},{8,9},{9,8},{10,11... | collective-permute-start | bytes 3145736 | tf_op jit(solution)/shard_map/ppermute | solution.py:21
  210.4 14.3 %collective-permute-start.14 = (bf16[256,1024]{1,0:T(8,128)(2,1)}, bf16[256,1024]{1,0:T(8,128)(2,1)}, u32[]{:S(2)}, u32[]{:S(2)}) collective-permute-start(bf16[256,1024]{1,0:T(8,128)(2,1)} %fusion.34), channel_id=1, source_target_pairs={{0,2},{1,3},{2,0},{3,1},{4,6},{5,7},{6,4},{7,5},{8,10},{9,11},{10,... | collective-permute-start | bytes 1572872 | tf_op jit(solution)/shard_map/ppermute | solution.py:21
  242.7 22.3 %collective-permute-start.16 = (bf16[2,256,1024]{2,1,0:T(8,128)(2,1)}, bf16[2,256,1024]{2,1,0:T(8,128)(2,1)}, u32[]{:S(2)}, u32[]{:S(2)}) collective-permute-start(bf16[2,256,1024]{2,1,0:T(8,128)(2,1)} %pad_maximum_fusion.11), channel_id=1, source_target_pairs={{0,1},{1,0},{2,3},{3,2},{4,5},{5,4},{6,7},{7,6},{8,9},{9,8},{10,11... | collective-permute-start | bytes 3145736 | tf_op jit(solution)/shard_map/ppermute | solution.py:21
  277.2 15.6 %collective-permute-start.17 = (bf16[2,256,1024]{2,1,0:T(8,128)(2,1)}, bf16[2,256,1024]{2,1,0:T(8,128)(2,1)}, u32[]{:S(2)}, u32[]{:S(2)}) collective-permute-start(bf16[2,256,1024]{2,1,0:T(8,128)(2,1)} %fusion.23), channel_id=1, source_target_pairs={{0,1},{1,0},{2,3},{3,2},{4,5},{5,4},{6,7},{7,6},{8,9},{9,8},{10,11... | collective-permute-start | bytes 3145736 | tf_op jit(solution)/shard_map/ppermute | solution.py:21
  282.7 26.3 %collective-permute-start.29 = (bf16[2,2,128,1024]{3,2,1,0:T(8,128)(2,1)}, bf16[2,2,128,1024]{3,2,1,0:T(8,128)(2,1)}, u32[]{:S(2)}, u32[]{:S(2)}) collective-permute-start(bf16[2,2,128,1024]{3,2,1,0:T(8,128)(2,1)} %fusion.20), channel_id=1, source_target_pairs={{0,4},{4,0},{8,12},{12,8},{16,20},{20,16},{24,28},{28,24},{1,5},{5... | collective-permute-start | bytes 3145736 | tf_op jit(solution)/shard_map/ppermute | solution.py:21
  290.2 40.9 %collective-permute-start.32 = (bf16[2,2,128,1024]{3,2,1,0:T(8,128)(2,1)}, bf16[2,2,128,1024]{3,2,1,0:T(8,128)(2,1)}, u32[]{:S(2)}, u32[]{:S(2)}) collective-permute-start(bf16[2,2,128,1024]{3,2,1,0:T(8,128)(2,1)} %fusion.21), channel_id=1, source_target_pairs={{0,4},{4,0},{8,12},{12,8},{16,20},{20,16},{24,28},{28,24},{1,5},{5... | collective-permute-start | bytes 3145736 | tf_op jit(solution)/shard_map/ppermute | solution.py:21
  295.3 38.5 %collective-permute-start.18 = (bf16[256,1024]{1,0:T(8,128)(2,1)S(1)}, bf16[256,1024]{1,0:T(8,128)(2,1)S(1)}, u32[]{:S(2)}, u32[]{:S(2)}) collective-permute-start(bf16[256,1024]{1,0:T(8,128)(2,1)S(1)} %fusion.35), channel_id=1, source_target_pairs={{0,2},{1,3},{2,0},{3,1},{4,6},{5,7},{6,4},{7,5},{8,10},{9,11},{10,... | collective-permute-start | bytes 1572872 | tf_op jit(solution)/shard_map/ppermute | solution.py:21
  311.7 34.4 %collective-permute-start.30 = (bf16[2,128,1024]{2,1,0:T(8,128)(2,1)}, bf16[2,128,1024]{2,1,0:T(8,128)(2,1)}, u32[]{:S(2)}, u32[]{:S(2)}) collective-permute-start(bf16[2,128,1024]{2,1,0:T(8,128)(2,1)} %fusion.38), channel_id=1, source_target_pairs={{0,8},{4,12},{8,0},{12,4},{16,24},{20,28},{24,16},{28,20},{1,9},{5... | collective-permute-start | bytes 1572872 | tf_op jit(solution)/shard_map/ppermute | solution.py:21
  333.7 21.0 %collective-permute-start.33 = (bf16[2,128,1024]{2,1,0:T(8,128)(2,1)}, bf16[2,128,1024]{2,1,0:T(8,128)(2,1)}, u32[]{:S(2)}, u32[]{:S(2)}) collective-permute-start(bf16[2,128,1024]{2,1,0:T(8,128)(2,1)} %fusion.39), channel_id=1, source_target_pairs={{0,8},{4,12},{8,0},{12,4},{16,24},{20,28},{24,16},{28,20},{1,9},{5... | collective-permute-start | bytes 1572872 | tf_op jit(solution)/shard_map/ppermute | solution.py:21
  341.9 31.2 %all-to-all-start.3 = ((bf16[4,2,128,256]{3,2,1,0:T(8,128)(2,1)}), bf16[4,2,128,256]{3,2,1,0:T(8,128)(2,1)}, u32[]{:S(2)}, u32[]{:S(2)}) async-start(bf16[4,2,128,256]{3,2,1,0:T(8,128)(2,1)} %bitcast.387), calls=%async_computation.3 | async-start | bytes 1048576 | tf_op jit(solution)/shard_map/all_to_all | solution.py:84
  347.5 24.8 %collective-permute-start.31 = (bf16[128,1024]{1,0:T(8,128)(2,1)S(1)}, bf16[128,1024]{1,0:T(8,128)(2,1)S(1)}, u32[]{:S(2)}, u32[]{:S(2)}) collective-permute-start(bf16[128,1024]{1,0:T(8,128)(2,1)S(1)} %fusion.52), channel_id=1, source_target_pairs={{0,16},{4,20},{8,24},{12,28},{16,0},{20,4},{24,8},{28,12},{1,17},{... | collective-permute-start | bytes 786440 | tf_op jit(solution)/shard_map/ppermute | solution.py:21
  356.8 85.2 %collective-permute-start.34 = (bf16[128,1024]{1,0:T(8,128)(2,1)}, bf16[128,1024]{1,0:T(8,128)(2,1)}, u32[]{:S(2)}, u32[]{:S(2)}) collective-permute-start(bf16[128,1024]{1,0:T(8,128)(2,1)} %fusion.53), channel_id=1, source_target_pairs={{0,16},{4,20},{8,24},{12,28},{16,0},{20,4},{24,8},{28,12},{1,17},{... | collective-permute-start | bytes 786440 | tf_op jit(solution)/shard_map/ppermute | solution.py:21
  360.9 85.3 %collective-permute-start.24 = (bf16[8,2,32,1024]{3,2,1,0:T(8,128)(2,1)}, bf16[8,2,32,1024]{3,2,1,0:T(8,128)(2,1)}, u32[]{:S(2)}, u32[]{:S(2)}) collective-permute-start(bf16[8,2,32,1024]{3,2,1,0:T(8,128)(2,1)} %fusion.19), channel_id=1, source_target_pairs={{0,1},{1,0},{2,3},{3,2},{4,5},{5,4},{6,7},{7,6},{8,9},{9,8},{10,11... | collective-permute-start | bytes 3145736 | tf_op jit(solution)/shard_map/ppermute | solution.py:21
  373.1 70.8 %all-to-all-start.5 = ((bf16[4,32,1024]{2,1,0:T(8,128)(2,1)}), bf16[4,32,1024]{2,1,0:T(8,128)(2,1)S(1)}, u32[]{:S(2)}, u32[]{:S(2)}) async-start(bf16[4,32,1024]{2,1,0:T(8,128)(2,1)} %bitcast.123), calls=%async_computation.5 | async-start | bytes 524288 | tf_op jit(solution)/shard_map/all_to_all | solution.py:84
  408.4 14.1 %collective-permute-start.36 = (f32[13,1024]{1,0:T(8,128)S(1)}, f32[13,1024]{1,0:T(8,128)S(1)}, u32[]{:S(2)}, u32[]{:S(2)}) collective-permute-start(f32[13,1024]{1,0:T(8,128)S(1)} %add.410), channel_id=1, source_target_pairs={{0,2},{1,3},{2,0},{3,1},{4,6},{5,7},{6,4},{7,5},{8,10},{9,11},{10,... | collective-permute-start | bytes 159752 | tf_op jit(solution)/shard_map/ppermute | solution.py:21
  414.8 35.8 %collective-permute-start.21 = (bf16[2,2,128,768]{3,2,1,0:T(8,128)(2,1)}, bf16[2,2,128,768]{3,2,1,0:T(8,128)(2,1)}, u32[]{:S(2)}, u32[]{:S(2)}) collective-permute-start(bf16[2,2,128,768]{3,2,1,0:T(8,128)(2,1)} %fusion.33), channel_id=1, source_target_pairs={{0,4},{4,0},{8,12},{12,8},{16,20},{20,16},{24,28},{28,24},{1,5},{5... | collective-permute-start | bytes 2359304 | tf_op jit(solution)/shard_map/ppermute | solution.py:21
  436.5 16.7 %collective-permute-start.19 = (bf16[2,2,128,1024]{3,2,1,0:T(8,128)(2,1)S(1)}, bf16[2,2,128,1024]{3,2,1,0:T(8,128)(2,1)}, u32[]{:S(2)}, u32[]{:S(2)}) collective-permute-start(bf16[2,2,128,1024]{3,2,1,0:T(8,128)(2,1)S(1)} %fusion.18), channel_id=1, source_target_pairs={{0,1},{1,0},{2,3},{3,2},{4,5},{5,4},{6,7},{7,6},{8,9},{9,8},{10,11... | collective-permute-start | bytes 3145736 | tf_op jit(solution)/shard_map/ppermute | solution.py:21
  465.3 19.8 %collective-permute-start.20 = (bf16[2,128,1024]{2,1,0:T(8,128)(2,1)}, bf16[2,128,1024]{2,1,0:T(8,128)(2,1)}, u32[]{:S(2)}, u32[]{:S(2)}) collective-permute-start(bf16[2,128,1024]{2,1,0:T(8,128)(2,1)} %fusion.36), channel_id=1, source_target_pairs={{0,2},{1,3},{2,0},{3,1},{4,6},{5,7},{6,4},{7,5},{8,10},{9,11},{10,... | collective-permute-start | bytes 1572872 | tf_op jit(solution)/shard_map/ppermute | solution.py:21
  (77 other events, 618.4 us)
Sparse Core Ops, SparseCore 0:
  11.5 70.7 all-gather.2

commit v2 on v1

v2 whole, which is shorter than its diff:
```python
import functools

import jax
import jax.numpy as jnp
from jax import lax
from jax.experimental import pallas as pl
from jax.experimental.pallas import tpu as pltpu
from jax.sharding import PartitionSpec as P

LOW = jnp.bfloat16
WIDE = jnp.float32


def gelu_exact(values):
    return 0.5 * values * (1.0 + lax.erf(values * 0.7071067811865476))


NT = (((1,), (1,)), ((), ()))
TN = (((0,), (0,)), ((), ()))
NN = (((1,), (0,)), ((), ()))
ONCE = pl.Buffered(1)


def mul(left, right, dims=NN):
    return lax.dot_general(left, right, dims, preferred_element_type=WIDE)


def shaped(shape, dtype):
    return pltpu.HBM(shape, dtype)


def kept(shape, dtype):
    return pltpu.VMEM(shape, dtype)


def fixed(shape):
    zeros = (0,) * len(shape)
    return pl.BlockSpec(shape, lambda *_: zeros, pipeline_mode=ONCE)


def scalars():
    return pl.BlockSpec(memory_space=pltpu.SMEM)


def remote():
    return pl.BlockSpec(memory_space=pltpu.HBM)


def outside(values):
    return [pltpu.with_memory_space_constraint(value, pltpu.HBM) for value in values]


def inside(values):
    return [pltpu.with_memory_space_constraint(value, pltpu.VMEM) for value in values]


def near():
    return pl.BlockSpec(memory_space=pltpu.VMEM)


def bring(pairs, sems):
    copies = []
    for source, target in pairs:
        copy = pltpu.make_async_copy(source, target, sems.at[len(copies)])
        copy.start()
        copies.append(copy)
    return copies


def params(megabytes):
    return pltpu.CompilerParams(vmem_limit_bytes=megabytes * 1024 * 1024)


def cost(flops, moved, extra=0):
    return pl.CostEstimate(flops=int(flops), bytes_accessed=int(moved), transcendentals=int(extra))


def swap(values, axis, count, mask):
    return lax.ppermute(values, axis, [(i, i ^ mask) for i in range(count)])


def bits_of(count):
    return [1 << k for k in range(count.bit_length() - 1)]


def gather_near(values, seqs, between=None, wait=()):
    top = bits_of(seqs)[-1]
    far = swap(values, "seq", seqs, top)
    pieces = {0: after(values, *wait) if wait else values}
    for mask in bits_of(top)[::-1]:
        for rel in list(pieces):
            pieces[rel | mask] = swap(pieces[rel], "seq", seqs, mask)
    if between is not None:
        far = after(far, between([pieces[rel] for rel in range(top)]))
    pieces[top] = far
    for mask in bits_of(top)[::-1]:
        for rel in [rel for rel in pieces if rel & top]:
            pieces[rel | mask] = swap(pieces[rel], "seq", seqs, mask)
    return [pieces[rel] for rel in range(seqs)]


def gather_pages(values, pages, hold=None):
    stack, rels = values[None], [0]
    masks = bits_of(pages)[::-1]
    low, high = masks[-1], masks[:-1]
    split = high[-2:]
    for mask in high[:-2]:
        stack = jnp.concatenate([stack, swap(stack, "page", pages, mask)], axis=0)
        rels = rels + [rel | mask for rel in rels]
    found = [(stack, rels)]
    jumps = [0]
    for mask in split:
        jumps = jumps + [jump | mask for jump in jumps]
    for jump in jumps[1:]:
        found.append((swap(stack, "page", pages, jump), [rel ^ jump for rel in rels]))

    def finish(*others):
        first = swap(stack, "page", pages, low)
        more = [(first, [rel ^ low for rel in rels])]
        for array, rels_of in found[1:]:
            array = after(array, first, *others)
            more.append((swap(array, "page", pages, low), [rel ^ low for rel in rels_of]))
        return found + more

    return [array for array, _ in found[1:]], finish


def scatter_first(send, pages):
    return swap(send, "page", pages, 1)


def scatter_rest(keep, got, pages, direct):
    return scatter_last(keep + got.astype(WIDE), pages, 1, direct)


class Sum:
    def __init__(self, total, pages):
        self.pages = pages
        self.total = total
        if pages == 8:
            lows = [self.total[k].astype(LOW) for k in range(1, pages // 2)]
            self.ready = lows[0]
            self.parts = [swap(low, "page", pages, 2 * (k + 1)) for k, low in enumerate(lows)]
        else:
            self.ready = self.total
            self.parts = []

    def arrive(self, *others):
        if self.pages == 8:
            self.parts = [after(part, *others) for part in self.parts]
        else:
            self.parts = []

    def finish(self, *others):
        if self.pages != 8:
            return scatter_last(self.total, self.pages, 1, False)
        final = after(self.total[0], *others)
        for part in self.parts:
            final = final + part.astype(WIDE)
        return final


def scatter_last(total, pages, level, direct):
    left = pages >> level
    mask = 1 << level
    if direct and left == 4:
        lows = [total[k].astype(LOW) for k in range(1, left)]
        parts = [swap(low, "page", pages, 2 * (k + 1)) for k, low in enumerate(lows)]
        final = total[0]
        for part in parts:
            final = final + part.astype(WIDE)
        return final
    while left > 1:
        total = total.reshape((left // 2, 2) + total.shape[1:])
        got = swap(total[:, 1].astype(LOW), "page", pages, mask)
        total = total[:, 0] + got.astype(WIDE)
        left //= 2
        mask *= 2
    return total[0]


def scatter_bits(values, axis, count, dim, order):
    index = lax.axis_index(axis)
    for mask in order:
        shape = values.shape
        values = values.reshape(shape[:dim] + (shape[dim] // 2, 2) + shape[dim + 1 :])
        bit = (index // mask) % 2
        keep = lax.dynamic_index_in_dim(values, bit, dim + 1, keepdims=False)
        send = lax.dynamic_index_in_dim(values, 1 - bit, dim + 1, keepdims=False)
        values = keep.astype(WIDE) + swap(send.astype(LOW), axis, count, mask).astype(WIDE)
    return values


def scatter_start(values, axis, count, dim, mask):
    index = lax.axis_index(axis)
    shape = values.shape
    values = values.reshape(shape[:dim] + (shape[dim] // 2, 2) + shape[dim + 1 :])
    bit = (index // mask) % 2
    keep = lax.dynamic_index_in_dim(values, bit, dim + 1, keepdims=False)
    send = lax.dynamic_index_in_dim(values, 1 - bit, dim + 1, keepdims=False)
    return keep.astype(WIDE), swap(send.astype(LOW), axis, count, mask)


def reorder(pieces, index):
    count = len(pieces)
    out = []
    for k in range(count):
        value = pieces[0]
        for rel in range(1, count):
            value = jnp.where(index ^ k == rel, pieces[rel], value)
        out.append(value)
    return out


def turn(values, seqs, index):
    mine = [lax.dynamic_index_in_dim(values, index ^ rel, 0, keepdims=False) for rel in range(seqs)]
    return [mine[0]] + [swap(mine[rel], "seq", seqs, rel) for rel in range(1, seqs)]


def after(values, *others):
    return lax.optimization_barrier((values, others))[0]


def to_near(values):
    return lax.all_to_all(values, "seq", 0, 0)


def fence(*values):
    return lax.optimization_barrier(values)


def to_all(values):
    return lax.all_to_all(values, ("page", "seq"), 0, 0)


def head_scores(qkv, h, span, depth, bias, same, mask):
    group = (h * depth) // 128
    lanes = lax.broadcasted_iota(jnp.int32, (1, 128), 1)
    mine = (lanes // depth) == (h % (128 // depth))
    q = qkv[:, group * 128 : group * 128 + 128]
    k = qkv[:, span + group * 128 : span + group * 128 + 128]
    raw = mul(jnp.where(mine, q, jnp.zeros_like(q)), k, NT)
    return raw * 0.125 + jnp.where(same, bias, 0.0) + mask, mine, group


def attend(pieces, block, spot, own_bias, inputs, vectors, column, row, mask, heads, depth):
    page_count, rows, width = inputs[0].shape
    seqs = len(inputs)
    slots = seqs * rows
    span = heads * depth
    arrays = [array for array, _ in pieces]
    rels = [rel for _, rel in pieces]
    n_arrays = len(arrays)

    blocks = sum(len(rel) for rel in rels)

    def body(spot_ref, bias_ref, *refs):
        weights = refs[:n_arrays]
        xs = refs[n_arrays : n_arrays + seqs]
        vec_ref, col_ref, row_ref, mask_ref = refs[n_arrays + seqs : n_arrays + seqs + 4]
        qkv_ref, lse_ref, full_ref = refs[n_arrays + seqs + 4 : n_arrays + seqs + 7]
        ctx_ref, x_all, sems = refs[n_arrays + seqs + 7 :]
        seq = spot_ref[1]
        page = spot_ref[0]
        step = pl.program_id(0)

        @pl.when(step == 0)
        def _():
            pairs = [(xs[r], x_all.at[r]) for r in range(seqs)]
            for ref, rel_list in zip(weights, rels):
                for k, rel in enumerate(rel_list):
                    start = pl.multiple_of((page ^ rel) * block, block)
                    for t in range(3):
                        source = ref.at[k, pl.ds(t * block, block), :]
                        pairs.append((source, full_ref.at[pl.ds(start, block), pl.ds(t * span, span)]))
            for copy in bring(pairs, sems):
                copy.wait()

        at_q = pl.multiple_of(spot_ref[1] * span, span)
        row_bias = jnp.concatenate(
            [vec_ref[0:1, pl.ds(at_q, span)], jnp.zeros((1, span), WIDE), vec_ref[1:2, pl.ds(at_q, span)]],
            axis=1,
        )
        for r in range(seqs):
            part = mul(x_all[r, step], full_ref[...]) + row_bias
            qkv_ref[0, r * rows : (r + 1) * rows, :] = part.astype(LOW)
        qkv = qkv_ref[0]
        same = col_ref[0] == row_ref[0]
        key_mask = mask_ref[0]
        lane = lax.broadcasted_iota(jnp.int32, (1, 128), 1)
        lse = jnp.zeros((slots, 128), WIDE)
        context = [None] * (span // 128)
        for h in range(heads):
            scores, mine, group = head_scores(qkv, h, span, depth, bias_ref[h], same, key_mask)
            peak = jnp.max(scores, axis=-1, keepdims=True)
            exponent = jnp.exp(scores - peak)
            total = jnp.sum(exponent, axis=-1, keepdims=True)
            lse = jnp.where(lane == h, peak + jnp.log(total), lse)
            low = (exponent * (1.0 / total)).astype(LOW)
            v = qkv[:, 2 * span + group * 128 : 2 * span + group * 128 + 128]
            out = mul(low, v)
            context[group] = out if context[group] is None else jnp.where(mine, out, context[group])
        lse_ref[0] = lse
        for group, value in enumerate(context):
            value = value.astype(LOW)
            for r in range(seqs):
                ctx_ref[seq ^ r, 0, :, group * 128 : group * 128 + 128] = value[r * rows : (r + 1) * rows]

    def per_page(shape):
        zeros = (0,) * len(shape)
        return pl.BlockSpec((1,) + shape, lambda i: (i,) + zeros)

    flops = page_count * (2 * slots * width * 3 * span + 8 * heads * slots * slots * depth)
    return pl.pallas_call(
        body,
        grid=(page_count,),
        out_shape=[
            kept((page_count, slots, 3 * span), LOW),
            kept((page_count, slots, 128), WIDE),
            kept((width, 3 * span), LOW),
        ]
        + [shaped((seqs, page_count, rows, span), LOW)],
        in_specs=[scalars(), scalars()]
        + [remote()] * (n_arrays + seqs)
        + [fixed(vectors.shape), per_page((slots, 1)), per_page((1, slots)), per_page((1, slots))],
        out_specs=[per_page((slots, 3 * span)), per_page((slots, 128)), fixed((width, 3 * span))]
        + [pl.BlockSpec((seqs, 1, rows, span), lambda i: (0, i, 0, 0))],
        scratch_shapes=[
            pltpu.VMEM((seqs, page_count, rows, width), LOW),
            pltpu.SemaphoreType.DMA((seqs + 3 * blocks,)),
        ],
        compiler_params=params(24),
        cost_estimate=cost(flops, 10 << 20, page_count * heads * slots * slots),
        name="attend",
    )(spot, own_bias, *outside(arrays), *outside(inputs), vectors, column, row, mask)


def attend_back(spot, own_bias, qkv, lse, grads, inputs, column, row, mask, heads, depth, pages):
    page_count, slots, triple = qkv.shape
    span = triple // 3
    seqs = grads.shape[0]
    rows = slots // seqs
    groups = span // 128
    width = inputs[0].shape[2]
    block = width // pages
    tile = 256 if width % 256 == 0 else width

    def body(spot_ref, bias_ref, qkv_ref, lse_ref, *refs):
        grad_ref, x_refs = refs[0], refs[1 : seqs + 1]
        col_ref, row_ref, mask_ref, out_ref, sum_ref, cell_ref, keep, send = refs[seqs + 1 : seqs + 9]
        full, x_all, g_all, sems = refs[seqs + 9 :]
        step = pl.program_id(0)

        @pl.when(step == 0)
        def _():
            pairs = []
            for k in range(seqs):
                start = pl.multiple_of((spot_ref[1] ^ k) * rows, rows)
                pairs.append((grad_ref.at[k], g_all.at[:, pl.ds(start, rows), :]))
            pairs += [(x_refs[r], x_all.at[:, pl.ds(r * rows, rows), :]) for r in range(seqs)]
            for copy in bring(pairs, sems):
                copy.wait()

        page = spot_ref[0]
        qkv = qkv_ref[0]
        same = col_ref[0] == row_ref[0]
        key_mask = mask_ref[0]
        lane = lax.broadcasted_iota(jnp.int32, (1, 128), 1)
        sub = lax.broadcasted_iota(jnp.int32, (128, 1), 0)
        lse = lse_ref[0]
        grad = g_all[step]
        cell = jnp.zeros((1, 128), WIDE)
        dq, dk, dv = [None] * groups, [None] * groups, [None] * groups
        for h in range(heads):
            scores, mine, group = head_scores(qkv, h, span, depth, bias_ref[h], same, key_mask)
            mine_sub = (sub // depth) == (h % (128 // depth))
            at = group * 128
            q = qkv[:, at : at + 128]
            k = qkv[:, span + at : span + at + 128]
            v = qkv[:, 2 * span + at : 2 * span + at + 128]
            g = grad[:, at : at + 128]
            weights = jnp.exp(scores - lse[:, h : h + 1])
            slope = mul(jnp.where(mine, g, jnp.zeros_like(g)), v, NT)
            inner = jnp.sum(weights * slope, axis=-1, keepdims=True)
            ds = weights * (slope - inner)
            same_sum = jnp.sum(jnp.where(same, ds, 0.0), axis=0, keepdims=True)
            cell = jnp.where(lane == h, jnp.sum(same_sum, axis=1, keepdims=True), cell)
            ds_low = ds.astype(LOW)
            part_q = mul(ds_low, k)
            part_k = mul(q, ds_low, TN)
            part_v = mul(g, weights.astype(LOW), TN)
            dq[group] = part_q if dq[group] is None else jnp.where(mine, part_q, dq[group])
            dk[group] = part_k if dk[group] is None else jnp.where(mine_sub, part_k, dk[group])
            dv[group] = part_v if dv[group] is None else jnp.where(mine_sub, part_v, dv[group])
        cell_ref[0] = jnp.broadcast_to(cell, (8, 128))
        for group in range(groups):
            at = group * 128
            value_q = dq[group] * 0.125
            value_v = dv[group].T
            out_ref[0, :, at : at + 128] = value_q.astype(LOW)
            out_ref[0, :, span + at : span + at + 128] = (dk[group] * 0.125).T.astype(LOW)
            out_ref[0, :, 2 * span + at : 2 * span + at + 128] = value_v.astype(LOW)
            sum_ref[0, 0:1, at : at + 128] = jnp.sum(value_q, axis=0, keepdims=True)
            sum_ref[0, 0:1, span + at : span + at + 128] = jnp.sum(value_v, axis=0, keepdims=True)
        grad_proj = out_ref[0]

        @pl.when(step == 0)
        def _():
            for at in range(0, width, tile):
                full[at : at + tile, :] = mul(x_all[step, :, at : at + tile], grad_proj, TN)

        @pl.when(step > 0)
        def _():
            for at in range(0, width, tile):
                full[at : at + tile, :] += mul(x_all[step, :, at : at + tile], grad_proj, TN)

        @pl.when(step == page_count - 1)
        def _():
            for rel in range(pages):
                start = pl.multiple_of((page ^ rel) * block, block)
                value = full[pl.ds(start, block), :]
                if rel % 2 == 0:
                    keep[rel // 2] = value
                else:
                    send[rel // 2] = value.astype(LOW)

    def per_page(shape):
        zeros = (0,) * len(shape)
        return pl.BlockSpec((1,) + shape, lambda i: (i,) + zeros)

    flops = page_count * (20 * heads * slots * slots * depth + 2 * slots * width * triple)
    return pl.pallas_call(
        body,
        grid=(page_count,),
        out_shape=[
            shaped((page_count, slots, triple), LOW),
            shaped((page_count, 8, 2 * span), WIDE),
            shaped((page_count, 8, 128), WIDE),
            shaped((pages // 2, block, triple), WIDE),
            shaped((pages // 2, block, triple), LOW),
        ],
        in_specs=[scalars(), scalars(), per_page((slots, triple)), per_page((slots, 128))]
        + [remote()] * (1 + seqs)
        + [per_page((slots, 1)), per_page((1, slots)), per_page((1, slots))],
        out_specs=[
            per_page((slots, triple)),
            per_page((8, 2 * span)),
            per_page((8, 128)),
            fixed((pages // 2, block, triple)),
            fixed((pages // 2, block, triple)),
        ],
        scratch_shapes=[
            pltpu.VMEM((width, triple), WIDE),
            pltpu.VMEM((page_count, slots, width), LOW),
            pltpu.VMEM((page_count, slots, span), LOW),
            pltpu.SemaphoreType.DMA((2 * seqs,)),
        ],
        compiler_params=params(28),
        cost_estimate=cost(flops, 10 << 20, page_count * heads * slots * slots),
        name="attend_back",
    )(spot, own_bias, *inside([qkv, lse]), *outside([grads]), *outside(inputs), column, row, mask)


def page_order(values, rels, page_index):
    pages = len(rels)
    shape = values.shape
    if rels != sorted(rels):
        values = jnp.stack([values[rels.index(rel)] for rel in range(pages)])
    for bit in bits_of(pages):
        folded = values.reshape((pages // (2 * bit), 2, bit) + shape[1:])
        values = jnp.where((page_index // bit) % 2 == 0, folded, folded[:, ::-1])
    return values.reshape(shape)


def assemble_mix(near_blocks, rels, spot, rows, width):
    seqs = len(near_blocks)
    span = near_blocks[0].shape[2]
    if rows % 16:
        ordered = reorder([array.reshape(len(rels), -1, rows, span) for array in near_blocks], spot[1])
        ordered = jnp.stack([array.transpose(0, 2, 1, 3).reshape(len(rels), rows, width) for array in ordered], axis=1)
        return page_order(ordered, rels, spot[0]).reshape(width, width)

    def body(spot_ref, *refs):
        out, held, sems = refs[-3:]
        page, seq = spot_ref[0], spot_ref[1]
        for copy in bring([(refs[r], held.at[r]) for r in range(seqs)], sems):
            copy.wait()
        for r in range(seqs):
            for k, rel in enumerate(rels):
                start = pl.multiple_of(((page ^ rel) * seqs + (seq ^ r)) * rows, rows)
                for t in range(width // span):
                    out[pl.ds(start, rows), t * span : (t + 1) * span] = held[r, k, t * rows : (t + 1) * rows, :]

    return pl.pallas_call(
        body,
        out_shape=kept((width, width), LOW),
        in_specs=[scalars()] + [remote()] * seqs,
        out_specs=near(),
        scratch_shapes=[pltpu.VMEM((seqs,) + near_blocks[0].shape, LOW), pltpu.SemaphoreType.DMA((seqs,))],
        compiler_params=params(8),
        cost_estimate=cost(0, 4 * width * width),
        name="assemble_mix",
    )(spot, *outside(near_blocks))


def mix(spot, contexts, w_mix, inputs, vectors):
    flat, width = inputs.shape
    seqs = contexts.shape[0]
    span = width // seqs

    def body(spot_ref, *refs):
        c_ref, w_ref, x_ref, vec_ref, wide_ref, low_ref, hat_ref, rstd_ref, c_all, x_here, sems = refs
        copies = bring([(c_ref.at[k], c_all.at[k]) for k in range(seqs)] + [(x_ref, x_here)], sems)
        for copy in copies:
            copy.wait()
        total = x_here[...].astype(WIDE) + vec_ref[2:3, :]
        for k in range(seqs):
            total = total + mul(c_all[k], w_ref[k * span : (k + 1) * span, :])
        center = total - jnp.mean(total, axis=-1, keepdims=True)
        spread = jnp.mean(center * center, axis=-1, keepdims=True)
        rstd = lax.rsqrt(spread + 1e-05)
        hat = center * rstd
        normed = hat * vec_ref[10:11, :] + vec_ref[4:5, :]
        wide_ref[...] = normed
        low_ref[...] = normed.astype(LOW)
        hat_ref[...] = hat
        rstd_ref[...] = jnp.broadcast_to(rstd, (flat, 128))

    return pl.pallas_call(
        body,
        out_shape=[
            kept((flat, width), WIDE),
            shaped((flat, width), LOW),
            kept((flat, width), WIDE),
            kept((flat, 128), WIDE),
        ],
        in_specs=[scalars()] + [remote(), near(), remote(), near()],
        out_specs=[near()] * 4,
        scratch_shapes=[
            pltpu.VMEM((seqs, flat, span), LOW),
            pltpu.VMEM((flat, width), LOW),
            pltpu.SemaphoreType.DMA((seqs + 1,)),
        ],
        compiler_params=params(12),
        cost_estimate=cost(2 * flat * width * width, 8 << 20),
        name="mix",
    )(spot, *outside([contexts]), *inside([w_mix]), *outside([inputs]), vectors)


def second_norm(normed, keep, close, far, vectors, cotangent):
    flat, width = normed.shape

    def body(h_ref, k_ref, n_ref, f_ref, vec_ref, cot_ref, out, wide, low, sums, n_here, f_here, c_here, sems):
        for copy in bring([(n_ref, n_here), (f_ref, f_here), (cot_ref, c_here)], sems):
            copy.wait()
        total = h_ref[...] + (k_ref[...] + n_here[...].astype(WIDE) + f_here[...].astype(WIDE)) + vec_ref[3:4, :]
        center = total - jnp.mean(total, axis=-1, keepdims=True)
        spread = jnp.mean(center * center, axis=-1, keepdims=True)
        rstd = lax.rsqrt(spread + 1e-05)
        hat = center * rstd
        out[...] = (hat * vec_ref[11:12, :] + vec_ref[5:6, :]).astype(LOW)
        cot = c_here[...].astype(WIDE)
        slope = cot * vec_ref[11:12, :]
        first = jnp.mean(slope, axis=-1, keepdims=True)
        second = jnp.mean(slope * hat, axis=-1, keepdims=True)
        grad = rstd * (slope - first - hat * second)
        wide[...] = grad
        low[...] = grad.astype(LOW)
        sums[0:1, :] = jnp.sum(cot * hat, axis=0, keepdims=True)
        sums[1:2, :] = jnp.sum(cot, axis=0, keepdims=True)
        sums[2:3, :] = jnp.sum(grad, axis=0, keepdims=True)

    return pl.pallas_call(
        body,
        out_shape=[
            shaped((flat, width), LOW),
            kept((flat, width), WIDE),
            shaped((flat, width), LOW),
            shaped((8, width), WIDE),
        ],
        in_specs=[near(), near(), remote(), remote(), near(), remote()],
        out_specs=[near()] * 4,
        scratch_shapes=[pltpu.VMEM((flat, width), LOW)] * 3 + [pltpu.SemaphoreType.DMA((3,))],
        compiler_params=params(12),
        cost_estimate=cost(flat * width * 30, 7 << 20),
        name="second_norm",
    )(*inside([normed]), keep, *outside([close, far]), vectors, *outside([cotangent]))


def first_norm_back(spot, grad_second, keep, close, far, hat, rstd, vectors, w_mix, seqs):
    flat, width = grad_second.shape
    span = width // seqs

    def body(spot_ref, d_ref, k_ref, n_ref, f_ref, hat_ref, rstd_ref, vec_ref, w_ref, wide, low, sums, *rest):
        outs, n_here, f_here, sems = rest
        for copy in bring([(n_ref, n_here), (f_ref, f_here)], sems):
            copy.wait()
        grad = d_ref[...] + (k_ref[...] + n_here[...].astype(WIDE) + f_here[...].astype(WIDE))
        hat = hat_ref[...]
        slope = grad * vec_ref[10:11, :]
        first = jnp.mean(slope, axis=-1, keepdims=True)
        second = jnp.mean(slope * hat, axis=-1, keepdims=True)
        result = rstd_ref[:, 0:1] * (slope - first - hat * second)
        wide[...] = result
        result_low = result.astype(LOW)
        low[...] = result_low
        for k in range(seqs):
            outs[k] = mul(result_low, w_ref[k * span : (k + 1) * span, :], NT).astype(LOW)
        sums[0:1, :] = jnp.sum(grad * hat, axis=0, keepdims=True)
        sums[1:2, :] = jnp.sum(grad, axis=0, keepdims=True)
        sums[2:3, :] = jnp.sum(result, axis=0, keepdims=True)

    return pl.pallas_call(
        body,
        out_shape=[shaped((flat, width), WIDE), shaped((flat, width), LOW), shaped((8, width), WIDE)]
        + [shaped((seqs, flat, span), LOW)],
        in_specs=[scalars(), near(), near(), remote(), remote()] + [near()] * 4,
        out_specs=[near()] * 4,
        scratch_shapes=[pltpu.VMEM((flat, width), LOW)] * 2 + [pltpu.SemaphoreType.DMA((2,))],
        compiler_params=params(12),
        cost_estimate=cost(2 * flat * width * width, 8 << 20),
        name="first_norm_back",
    )(spot, *inside([grad_second]), keep, *outside([close, far]), *inside([hat, rstd]), vectors, *inside([w_mix]))


def weight_grad(spot, lefts, rights, pages, split):
    count = len(lefts)
    tokens, height = lefts[0].shape
    width = rights[0].shape[1]
    rows = height // pages
    tile = 256 if height % 256 == 0 else height

    def body(spot_ref, *refs):
        left, right = refs[:count], refs[count : 2 * count]
        outs = refs[2 * count : -4]
        full, l_all, r_all, sems = refs[-4:]
        page = spot_ref[0]
        pairs = []
        for k in range(count):
            pairs.append((left[k], l_all.at[pl.ds(k * tokens, tokens), :]))
            pairs.append((right[k], r_all.at[pl.ds(k * tokens, tokens), :]))
        for copy in bring(pairs, sems):
            copy.wait()
        for at in range(0, height, tile):
            value = mul(l_all[:, at : at + tile], r_all[...], TN)
            if split:
                full[at : at + tile, :] = value
            else:
                outs[0][at : at + tile, :] = value.astype(LOW)
        if split:
            for rel in range(pages):
                start = pl.multiple_of((page ^ rel) * rows, rows)
                value = full[pl.ds(start, rows), :]
                if rel % 2 == 0:
                    outs[0][rel // 2] = value
                else:
                    outs[1][rel // 2] = value.astype(LOW)

    if split:
        outs = [shaped((pages // 2, rows, width), WIDE), shaped((pages // 2, rows, width), LOW)]
    else:
        outs = [shaped((height, width), LOW)]
    return pl.pallas_call(
        body,
        out_shape=outs,
        in_specs=[scalars()] + [remote()] * (2 * count),
        out_specs=[near()] * len(outs),
        scratch_shapes=[
            pltpu.VMEM((height, width) if split else (8, 128), WIDE),
            pltpu.VMEM((count * tokens, height), LOW),
            pltpu.VMEM((count * tokens, width), LOW),
            pltpu.SemaphoreType.DMA((2 * count,)),
        ],
        compiler_params=params(18),
        cost_estimate=cost(2 * count * tokens * height * width, 8 << 20),
        name="weight_grad",
    )(spot, *outside(lefts), *outside(rights))


def input_grad(grad_proj, w_proj, seqs):
    page_count, slots, triple = grad_proj.shape
    width = w_proj.shape[0]
    rows = slots // seqs

    def body(d_ref, w_ref, *outs):
        for rel in range(seqs):
            value = mul(d_ref[0, rel * rows : (rel + 1) * rows, :], w_ref[...], NT)
            outs[rel][0] = value.astype(outs[rel].dtype)

    per = pl.BlockSpec((1, rows, width), lambda i: (i, 0, 0))
    return pl.pallas_call(
        body,
        grid=(page_count,),
        out_shape=[shaped((page_count, rows, width), WIDE if rel % 2 == 0 else LOW) for rel in range(seqs)],
        in_specs=[pl.BlockSpec((1, slots, triple), lambda i: (i, 0, 0)), fixed(w_proj.shape)],
        out_specs=[per] * seqs,
        compiler_params=params(14),
        cost_estimate=cost(2 * page_count * slots * triple * width, 8 << 20),
        name="input_grad",
    )(grad_proj, *inside([w_proj]))


def local(counts, tokens, cells, lengths, cotangent, w_qkv, w_out, w_up, w_down, biases, gains, cell_bias):
    pages, seqs = counts
    page_count, row_count, width = tokens.shape
    slots = row_count * seqs
    heads = cell_bias.shape[0]
    depth = width // heads
    heads_here = heads // seqs
    span = heads_here * depth
    flat = page_count * row_count
    rows = w_qkv.shape[0]
    ff_rows = w_down.shape[0]
    ff_here = ff_rows * pages
    page_index = lax.axis_index("page")
    seq_index = lax.axis_index("seq")
    spot = jnp.stack([page_index, seq_index]).astype(jnp.int32)
    low_page = bits_of(pages)
    low_seq = bits_of(seqs)

    def scatter_near(keeps, sends):
        near_parts = [swap(send, "seq", seqs, 1) for send in sends]
        *result, sent = scatter_far_sent(keeps, near_parts)
        return (*result, sent)

    def scatter_far(keeps, nears):
        return scatter_far_sent(keeps, nears)[:3]

    def scatter_far_sent(totals, nears):
        far = jnp.zeros_like(nears[0])
        mask = 2
        while mask < seqs:
            half = [k for k in range(len(totals)) if (k * 2) & mask]
            ready = [(totals[k] + nears[k].astype(WIDE)).astype(LOW) for k in half]
            moved = [swap(value, "seq", seqs, mask) for value in ready]
            rest = [k for k in range(len(totals)) if not (k * 2) & mask]
            if mask * 2 >= seqs:
                far = moved[0]
                totals, nears = [totals[0]], [nears[0]]
            else:
                totals = [totals[k] + nears[k].astype(WIDE) for k in rest]
                nears = moved
            mask *= 2
        return totals[0], nears[0], far, ready[0]

    def small_table(sums_proj, cells_grad):
        owners = pages * seqs
        here = lax.broadcasted_iota(jnp.int32, (seqs, 1, 1), 0) == seq_index
        sums_proj = jnp.sum(sums_proj[:, 0], axis=0).reshape(2, 1, pages, lanes)

        def own(vector):
            return jnp.where(here, vector, 0.0).reshape(owners, 1, lanes)

        hidden_sum = functools.reduce(jnp.add, totals).reshape(pages, 1, ff_rows)
        hidden_sum = jnp.where(here.reshape(1, seqs, 1), hidden_sum, 0.0)
        hidden_sum = hidden_sum.reshape(-1, owners, lanes).transpose(1, 0, 2)
        cells_grad = jnp.sum(cells_grad[:, 0, :heads_here], axis=0)[None]
        cells_grad = jnp.where(here[:, 0], cells_grad, 0.0).reshape(heads)
        cells_grad = jnp.pad(cells_grad, (0, -heads % lanes)).reshape(1, -1, lanes)

        def row_of(sums, k):
            return sums[k].reshape(owners, 1, lanes)

        return to_all(
            jnp.concatenate(
                [
                    own(sums_proj[0]),
                    own(sums_proj[1]),
                    row_of(sums_one, 2),
                    row_of(sums_two, 2),
                    row_of(sums_one, 1),
                    row_of(sums_two, 1),
                    hidden_sum,
                    row_of(sums_one, 0),
                    row_of(sums_two, 0),
                    jnp.broadcast_to(cells_grad, (owners,) + cells_grad.shape[1:]),
                ],
                axis=1,
            )
        )

    def block_rows(values):
        return values.reshape(values.shape[0], -1, span)

    small = jnp.concatenate([biases, gains], axis=0).astype(LOW)
    small_rows, lanes = small.shape
    digits = jnp.concatenate([cells // 16, cells % 16], axis=0).astype(LOW)
    extra = jnp.concatenate(
        [jnp.pad(small, ((0, 0), (0, span - lanes))), jnp.pad(digits, ((0, 0), (0, span - row_count)))], axis=0
    )
    part_qkv = w_qkv.astype(LOW).reshape(rows, 3, seqs, span).transpose(2, 1, 0, 3)
    part_up = w_up.astype(LOW).reshape(rows, pages, seqs, ff_rows).transpose(2, 0, 1, 3)
    sent = jnp.concatenate(
        [
            part_qkv.reshape(seqs, 3 * rows, span),
            jnp.broadcast_to(extra, (seqs,) + extra.shape),
            part_up.reshape(seqs, pages * rows * ff_rows // span, span),
        ],
        axis=1,
    )
    turned = to_near(sent)
    part_qkv = turned[:, : 3 * rows].reshape(seqs, 3, rows, span).transpose(1, 0, 2, 3)
    extras = turned[:, 3 * rows : 3 * rows + extra.shape[0]]
    part_up = turned[:, 3 * rows + extra.shape[0] :].reshape(seqs * rows, ff_here)
    digits = extras[:, small_rows : small_rows + 2 * page_count, :row_count].astype(jnp.int32)
    cells_all = digits[:, :page_count] * 16 + digits[:, page_count:]
    cells_all = jnp.stack(reorder([cells_all[k] for k in range(seqs)], seq_index), axis=1)
    cells_all = cells_all.reshape(page_count, slots)

    part_mix = w_out.astype(LOW).reshape(rows, width // span, span).transpose(1, 0, 2)
    part_small = extras[:, :small_rows, :lanes].transpose(1, 0, 2).reshape(small_rows, seqs * lanes)
    part_small = jnp.pad(part_small, ((0, -small_rows % 16), (0, span - seqs * lanes)))
    block = seqs * rows
    part_both = jnp.concatenate(
        [part_qkv.reshape(3 * block, span), part_mix.reshape(-1, span), part_small], axis=0
    )
    split = low_page[1:3][::-1]
    stack, rels = part_both[None], [0]
    for bit in low_page[:0:-1][: len(low_page) - 1 - len(split)]:
        stack = jnp.concatenate([stack, swap(stack, "page", pages, bit)], axis=0)
        rels = rels + [rel | bit for rel in rels]
    jumps = [0]
    for bit in split:
        jumps = jumps + [jump | bit for jump in jumps]
    across = [swap(stack, "page", pages, jump) for jump in jumps[1:]]
    beside = [swap(stack, "page", pages, 1)]
    x_near = [tokens]
    x_far = swap(after(tokens, part_both), "seq", seqs, low_seq[-1])
    *across, part_up, first_beside, x_far, w_down_low, x_own = fence(
        *across, part_up, beside[0], x_far, w_down.astype(LOW), tokens
    )
    beside = [first_beside] + [swap(array, "page", pages, 1) for array in across]
    both_pieces = [(array, [rel ^ jump for rel in rels]) for array, jump in zip([stack] + across, jumps)]
    both_pieces += [(array, [rel ^ jump ^ 1 for rel in rels]) for array, jump in zip(beside, jumps)]
    inputs = {0: x_own, low_seq[-1]: x_far}
    for bit in low_seq[:-1][::-1]:
        for rel in list(inputs):
            inputs[rel | bit] = swap(inputs[rel], "seq", seqs, bit)
    inputs = [inputs[rel] for rel in range(seqs)]
    feed_both = lax.all_gather(jnp.concatenate([part_up, w_down_low], axis=0), "page", axis=0, tiled=False)
    w_expand = feed_both[:, :block].reshape(width, ff_here)
    w_reduce = feed_both[:, block:].reshape(ff_here, width)
    fenced = fence(*[array for array, _ in both_pieces], *inputs)
    inputs = list(fenced[len(both_pieces) :])
    both_pieces = [(array, rel) for array, (_, rel) in zip(fenced[: len(both_pieces)], both_pieces)]
    both_rels = [rel for _, rel_list in both_pieces for rel in rel_list]
    vectors = jnp.concatenate([array[:, 4 * block :, :] for array, _ in both_pieces], axis=0)
    vectors = page_order(vectors[:, :small_rows, : seqs * lanes], both_rels, page_index)
    vectors = vectors.reshape(pages, small_rows, seqs * lanes).transpose(1, 0, 2)
    vectors = vectors.reshape(small_rows, width).astype(WIDE)
    hidden_bias = vectors[6:10].reshape(pages, seqs, ff_rows)
    hidden_bias = lax.dynamic_index_in_dim(hidden_bias, seq_index, 1, keepdims=False).reshape(1, ff_here)

    position = lax.broadcasted_iota(jnp.int32, (1, slots), 1)
    position = ((position // row_count) ^ seq_index) * row_count + position % row_count
    mask = jnp.where(position < lengths[:, None], 0.0, -1e30).astype(WIDE)[:, None, :]
    column, row = cells_all[:, :, None], cells_all[:, None, :]
    own_bias = lax.dynamic_slice_in_dim(cell_bias, seq_index * heads_here, heads_here)
    mix_part = jnp.concatenate([array[:, 3 * block : 4 * block, :] for array, _ in both_pieces], axis=0)
    mix_far = swap(mix_part, "seq", seqs, low_seq[-1])
    qkv, lse, w_proj, contexts = attend(
        [(after(array, mix_part), rel_list) for array, rel_list in both_pieces],
        block,
        spot,
        own_bias,
        inputs,
        vectors,
        column,
        row,
        mask,
        heads_here,
        depth,
    )
    contexts, mix_part, mix_far, qkv, lse, w_proj = fence(contexts, mix_part, mix_far, qkv, lse, w_proj)
    mix_near = {0: mix_part, low_seq[-1]: mix_far}
    for bit in low_seq[:-1][::-1]:
        for rel in list(mix_near):
            mix_near[rel | bit] = swap(mix_near[rel], "seq", seqs, bit)
    contexts = to_near(contexts).reshape(seqs, flat, span)
    w_mix = assemble_mix([mix_near[rel] for rel in range(seqs)], both_rels, spot, rows, width)

    flat_inputs = tokens.reshape(flat, width)
    normed, normed_low, hat, rstd = mix(spot, contexts, w_mix, flat_inputs, vectors)
    hidden, active, parts = [], [], []

    def feed(pieces):
        for piece in pieces:
            value = jnp.dot(piece, w_expand, preferred_element_type=WIDE) + hidden_bias
            low = gelu_exact(value).astype(LOW)
            part = jnp.dot(low, w_reduce, preferred_element_type=WIDE)
            part = part.astype(LOW) if len(parts) % 2 else part
            hidden.append(value)
            active.append(low)
            parts.append(part)
        return tuple(parts)

    normed_all = gather_near(normed_low, seqs, feed)
    feed(normed_all[seqs // 2 :])
    keep, close, far, ready = scatter_near(parts[0::2], parts[1::2])
    slopes = [
        0.5 * (1.0 + lax.erf(u * 0.7071067811865476)) + u * jnp.exp(-0.5 * u * u) * 0.3989422804014327
        for u in after(hidden, ready)
    ]
    far, slopes = lax.optimization_barrier((far, slopes))
    output, grad_second, second_low, sums_two = second_norm(
        normed, keep, close, far, vectors, cotangent.reshape(flat, width)
    )

    expanded, parts, totals = [], [], []

    def feed_back(pieces):
        for piece in pieces:
            slope = slopes[len(parts)]
            value = jnp.einsum("td,fd->tf", piece, w_reduce, preferred_element_type=WIDE) * slope
            low = value.astype(LOW)
            part = jnp.einsum("tf,df->td", low, w_expand, preferred_element_type=WIDE)
            part = part.astype(LOW) if len(parts) % 2 else part
            expanded.append(low)
            totals.append(jnp.sum(value, axis=0))
            parts.append(part)
        return tuple(parts)

    second_all = gather_near(second_low, seqs, feed_back)
    feed_back(second_all[seqs // 2 :])
    keep, close, far, ready = scatter_near(parts[0::2], parts[1::2])
    down_keep, down_send = weight_grad(spot, after(active, ready), second_all, pages, True)
    up_keep, up_send = weight_grad(spot, after(normed_all, down_send), expanded, pages, True)
    far, down_send, up_send = lax.optimization_barrier((far, down_send, up_send))
    down_got = scatter_first(down_send, pages)
    grad_first, first_low, sums_one, grad_contexts = first_norm_back(
        spot, grad_second, keep, close, far, hat, rstd, vectors, w_mix, seqs
    )
    grad_contexts = to_near(grad_contexts)
    context = jnp.concatenate([contexts[k] for k in range(seqs)], axis=1)
    grad_mix = jnp.einsum("tc,td->cd", context, first_low, preferred_element_type=WIDE)
    grad_mix = scatter_bits(grad_mix.reshape(pages, seqs, rows, width), "seq", seqs, 1, low_seq[:1])
    grad_contexts, grad_mix, down_got, down_keep, up_send = fence(
        grad_contexts, grad_mix, down_got, down_keep, up_send
    )
    down_sum = Sum(down_keep + down_got.astype(WIDE), pages)
    up_got = scatter_first(up_send, pages)
    mix_keep, mix_parts = scatter_start(grad_mix, "seq", seqs, 1, low_seq[1])
    grad_contexts = after(grad_contexts, down_sum.ready)
    grad_contexts = grad_contexts.reshape(seqs, page_count, row_count, span)
    grad_proj, sums_proj, cells_grad, proj_keep, proj_send = attend_back(
        spot, own_bias, qkv, lse, grad_contexts, inputs, column, row, mask, heads_here, depth, pages
    )
    down_parts = down_sum.parts
    fenced = fence(
        grad_proj, sums_proj, cells_grad, proj_keep, proj_send, up_keep, up_got, mix_keep, mix_parts, *down_parts
    )
    grad_proj, sums_proj, cells_grad, proj_keep, proj_send, up_keep, up_got, mix_keep, mix_parts = fenced[:9]
    down_sum.parts = list(fenced[9:])
    proj_got = scatter_first(proj_send, pages)
    up_sum = Sum(up_keep + up_got.astype(WIDE), pages)
    grad_mix = mix_keep + mix_parts.astype(WIDE)
    mix_keep, mix_parts = scatter_start(grad_mix.reshape(pages, rows, width), "page", pages, 0, 1)
    fenced = fence(proj_got, proj_keep, mix_keep, mix_parts, grad_proj, sums_proj, cells_grad, *up_sum.parts)
    proj_got, proj_keep, mix_keep, mix_parts, grad_proj, sums_proj, cells_grad = fenced[:7]
    up_sum.parts = list(fenced[7:])
    proj_sum = Sum(proj_keep + proj_got.astype(WIDE), pages)
    small_sums = small_table(after(sums_proj, proj_sum.ready), after(cells_grad, proj_sum.ready))
    grad_mix = after(mix_keep, proj_sum.ready) + mix_parts.astype(WIDE)
    mix_keep, mix_parts = scatter_start(grad_mix, "page", pages, 0, 2)
    parts = input_grad(after(grad_proj, proj_sum.ready), w_proj, seqs)
    near_parts = [swap(part, "seq", seqs, 1) for part in parts[1::2]]
    grad_expand = up_sum.finish(proj_sum.ready)
    fenced = fence(small_sums, mix_keep, mix_parts, grad_expand, *proj_sum.parts, *near_parts)
    small_sums, mix_keep, mix_parts, grad_expand = fenced[:4]
    proj_sum.parts = list(fenced[4 : 4 + len(proj_sum.parts)])
    near_parts = list(fenced[4 + len(proj_sum.parts) :])
    grad_qkv = proj_sum.finish()
    grad_reduce = down_sum.finish(grad_qkv)
    grad_mix = mix_keep + mix_parts.astype(WIDE)
    grad_mix = scatter_bits(grad_mix, "page", pages, 0, low_page[2:]).reshape(rows, width)
    keep, close, far = scatter_far(parts[0::2], near_parts)
    sent = jnp.concatenate(
        [
            grad_qkv.reshape(seqs, rows, 3, span).transpose(0, 2, 1, 3).reshape(seqs, 3 * rows, span),
            grad_expand.reshape(seqs, -1, span),
        ],
        axis=1,
    ).astype(LOW)
    turned = to_near(sent)
    grad_qkv = turned[:, : 3 * rows].reshape(seqs, 3, rows, span).transpose(2, 1, 0, 3)
    grad_qkv = grad_qkv.reshape(rows, 3 * width).astype(WIDE)
    grad_expand = turned[:, 3 * rows :].reshape(seqs, rows, pages, ff_rows).transpose(1, 2, 0, 3)
    grad_expand = grad_expand.reshape(rows, seqs * ff_here).astype(WIDE)
    grad_inputs = grad_first.reshape(page_count, row_count, width) + (
        keep + close.astype(WIDE) + far.astype(WIDE)
    )

    summed = jnp.sum(small_sums, axis=0)
    return (
        output.reshape(page_count, row_count, width),
        grad_inputs,
        grad_qkv,
        grad_mix,
        grad_expand,
        grad_reduce,
        summed[:10],
        summed[10:12],
        summed[12:].reshape(-1)[:heads],
    )


def solution(mesh):
    counts = (mesh.shape["page"], mesh.shape["seq"])
    placed = (
        P("page", "seq", None),
        P("page", "seq"),
        P("page"),
        P("page", "seq", None),
        P(("page", "seq"), None),
        P(("page", "seq"), None),
        P(("page", "seq"), None),
        P(("page", "seq"), None),
        P(None, ("page", "seq")),
        P(None, ("page", "seq")),
        P(),
    )

    def step(*args):
        return local(counts, *args)

    return jax.shard_map(
        step,
        mesh=mesh,
        in_specs=placed,
        out_specs=(
            P("page", "seq", None),
            P("page", "seq", None),
            P(("page", "seq"), None),
            P(("page", "seq"), None),
            P(("page", "seq"), None),
            P(("page", "seq"), None),
            P(None, ("page", "seq")),
            P(None, ("page", "seq")),
            P(),
        ),
        check_vma=False,
    )
```

time: 507 us -> 373 us (0.74)
  local copies, waits for them, and re-layouts: 109 us -> 33.8 us
  Pallas kernels: 0 us -> 57.6 us
  other arithmetic: 66.7 us -> 25.4 us
  matrix products: 52.9 us -> 22.5 us
  waiting for transfers between devices: 166 us -> 139 us
  blocking collectives: 12.6 us -> 0 us
    pallas_call x0 -> x9, Pallas kernels: none -> 57.6 us  [the longest x1 14.7 us: attend_back(): pl.pallas_call(body, grid=(page_count,), out_shape=[shaped((page_count, s...]
    ppermute x40 -> x45, waiting for transfers between devices: 161 us -> 104 us  [swap(): return lax.ppermute(values, axis, [(i, i ^ mask) for i in range(count)])]
    dot_general x17 -> x16, matrix products: 52.2 us -> 20.8 us  [the longest x4 6.32 us: feed_back(): jnp.einsum('td,fd->tf', piece, w_reduce, preferred_element_type=WIDE)]
    dot_general x4 -> x0, local copies, waits for them, and re-layouts: 22.1 us -> none  [the longest x1 13.2 us: local(): jnp.einsum('tf,td->fd', activated_low, second_all, preferred_element_type...]
    another operation x33 -> x8, other arithmetic: 27.6 us -> 6.55 us  [the longest x30 24.8 us: gather_bits(): jnp.stack([jnp.where(first, values, other), jnp.where(first, other, value...]
    add x15 -> x1, other arithmetic: 20.7 us -> 1.9 us  [scatter_bits(): keep.astype(WIDE) + swap(send.astype(LOW), axis, count, mask).astype(WIDE)]
    all_gather x1, waiting for transfers between devices: 0.01 us -> 16.6 us  [local(): lax.all_gather(jnp.concatenate([part_up, w_down_low], axis=0), 'page', ax...]
    convert_element_type x8, local copies, waits for them, and re-layouts: 16.9 us -> 2.85 us  [the longest x2 1.1 us: local(): grad_qkv = grad_qkv.reshape(rows, 3 * width).astype(WIDE)]
  transfers between devices with their start and end apart: 47 -> 51, of which waited for: 21 -> 20; matrix products, arithmetic and copies ran while one was open for 36% -> 14% of each run, Pallas kernels for 0% -> 14%
where the time goes in v2:
time: 373 us; the launch traced here: 366 us
  waiting for transfers between devices  139 us (37%)
  starting transfers between devices  71.7 us (19%)
  Pallas kernels  57.6 us (15%)
  local copies, waits for them, and re-layouts  33.8 us (9%)
  other arithmetic  25.4 us (7%)
  matrix products  22.5 us (6%)
  between operations  16.3 us (4%)
    ppermute x45, waiting for transfers between devices, swap(): return lax.ppermute(values, axis, [(i, i ^ mask) for i in range(count)])  104 us
    ppermute x45, starting transfers between devices, swap(): return lax.ppermute(values, axis, [(i, i ^ mask) for i in range(count)])  51.3 us
    all_to_all x4, waiting for transfers between devices, to_near(): return lax.all_to_all(values, 'seq', 0, 0)  18.4 us
    unnamed x172, local copies, waits for them, and re-layouts  16.9 us
    all_gather x1, waiting for transfers between devices, local(): lax.all_gather(jnp.concatenate([part_up, w_down_low], axis=0), 'page', ax...  16.6 us
    all_to_all x4, starting transfers between devices, to_near(): return lax.all_to_all(values, 'seq', 0, 0)  15.6 us
    pallas_call x1, Pallas kernels, attend_back(): pl.pallas_call(body, grid=(page_count,), out_shape=[shaped((page_count, s...  14.7 us
    pallas_call x2, Pallas kernels, weight_grad(): pl.pallas_call(body, out_shape=outs, in_specs=[scalars()] + [remote()] *...  14 us
  transfers between devices with their start and end apart: 51, of which 20 were waited for; matrix products, arithmetic and copies ran while one was open for 14% of the time, Pallas kernels for 14%

profile of v2, /device:TPU:0, one launch (start us, length us, event | category | flops | bytes accessed | tf_op | source)
XLA Modules:
  0.0 366.3 jit_solution(7053063747862252271)
XLA Ops:
  11.8 4.2 %all-to-all-start = ((bf16[4,240,256]{2,1,0:T(8,128)(2,1)}), bf16[4,240,256]{2,1,0:T(8,128)(2,1)S(1)}, u32[]{:S(2)}, u32[]{:S(2)}) async-start(bf16[4,240,256]{2,1,0:T(8,128)(2,1)} %pad_maximum_fusion.1), calls=%async_computation | async-start | bytes 983040 | tf_op jit(solution)/shard_map/all_to_all | solution.py:225
  18.4 6.8 %all-to-all-done = bf16[4,240,256]{2,1,0:T(8,128)(2,1)S(1)} async-done(((bf16[4,240,256]{2,1,0:T(8,128)(2,1)}), bf16[4,240,256]{2,1,0:T(8,128)(2,1)S(1)}, u32[]{:S(2)}, u32[]{:S(2)}) %all-to-all-start) | async-done | bytes 491552 | tf_op jit(solution)/shard_map/all_to_all | solution.py:225
  32.1 3.8 %collective-permute-done.4.refs_10_.refs_3_ = bf16[2,128,1024]{2,1,0:T(8,128)(2,1)} collective-permute-done((bf16[2,128,1024]{2,1,0:T(8,128)(2,1)S(1)}, bf16[2,128,1024]{2,1,0:T(8,128)(2,1)}, u32[]{:S(2)}, u32[]{:S(2)}) %collective-permute-start.4) | collective-permute-done | bytes 524320 | tf_op jit(solution)/shard_map/ppermute | solution.py:79
  35.9 11.3 %collective-permute-done.refs_1_ = bf16[1,528,256]{2,1,0:T(8,128)(2,1)S(1)} collective-permute-done((bf16[1,528,256]{2,1,0:T(8,128)(2,1)S(1)}, bf16[1,528,256]{2,1,0:T(8,128)(2,1)S(1)}, u32[]{:S(2)}, u32[]{:S(2)}) %collective-permute-start) | collective-permute-done | bytes 270368 | tf_op jit(solution)/shard_map/ppermute | solution.py:79
  53.1 5.4 %collective-permute-done.5.refs_5_ = bf16[1,528,256]{2,1,0:T(8,128)(2,1)S(1)} collective-permute-done((bf16[1,528,256]{2,1,0:T(8,128)(2,1)S(1)}, bf16[1,528,256]{2,1,0:T(8,128)(2,1)S(1)}, u32[]{:S(2)}, u32[]{:S(2)}) %collective-permute-start.5) | collective-permute-done | bytes 270368 | tf_op jit(solution)/shard_map/ppermute | solution.py:79
  58.5 7.2 %collective-permute-done.6.refs_6_ = bf16[1,528,256]{2,1,0:T(8,128)(2,1)S(1)} collective-permute-done((bf16[1,528,256]{2,1,0:T(8,128)(2,1)S(1)}, bf16[1,528,256]{2,1,0:T(8,128)(2,1)S(1)}, u32[]{:S(2)}, u32[]{:S(2)}) %collective-permute-start.6) | collective-permute-done | bytes 270368 | tf_op jit(solution)/shard_map/ppermute | solution.py:79
  65.7 9.2 %collective-permute-done.7.refs_7_ = bf16[1,528,256]{2,1,0:T(8,128)(2,1)S(1)} collective-permute-done((bf16[1,528,256]{2,1,0:T(8,128)(2,1)S(1)}, bf16[1,528,256]{2,1,0:T(8,128)(2,1)S(1)}, u32[]{:S(2)}, u32[]{:S(2)}) %collective-permute-start.7) | collective-permute-done | bytes 270368 | tf_op jit(solution)/shard_map/ppermute | solution.py:79
  80.7 10.1 %attend.1 = (bf16[2,512,768]{2,1,0:T(8,128)(2,1)S(1)}, f32[2,512,128]{2,1,0:T(8,128)S(1)}, bf16[1024,768]{1,0:T(8,128)(2,1)S(1)}, bf16[4,2,128,256]{3,2,1,0:T(8,128)(2,1)}) custom-call(s32[2]{0:T(128)S(1)} %pad_add_fusion.1.spot_ref, f32[4]{0:T(128)S(1)} %dynamic_slice.34.bias_ref, bf16[1,528,256]{2,1,0:T(8,128)(2,1)} %copy-done.46, ...), custom_call_target="tpu_custom_call" | custom-call | flops 2684354560 | bytes 10485760 | tf_op jit(solution)/shard_map/attend/pallas_call | solution.py:314
  93.7 3.6 all-to-all-start.1
  100.5 5.7 %all-to-all-done.1 = bf16[4,2,128,256]{3,2,1,0:T(8,128)(2,1)S(1)} async-done(((bf16[4,2,128,256]{3,2,1,0:T(8,128)(2,1)}), bf16[4,2,128,256]{3,2,1,0:T(8,128)(2,1)S(1)}, u32[]{:S(2)}, u32[]{:S(2)}) %all-to-all-start.1) | async-done | bytes 524320 | tf_op jit(solution)/shard_map/all_to_all | solution.py:225
  107.0 3.7 %mix.1 = (f32[256,1024]{1,0:T(8,128)S(1)}, bf16[256,1024]{1,0:T(8,128)(2,1)}, f32[256,1024]{1,0:T(8,128)S(1)}, f32[256,128]{1,0:T(8,128)S(1)}) custom-call(s32[2]{0:T(128)S(1)} %pad_add_fusion.1.spot_ref, bf16[4,256,256]{2,1,0:T(8,128)(2,1)} %bitcast.181, bf16[1024,1024]{1,0:T(8,128)(2,1)S(1)} %assemble_mix.1.refs_1_.w_ref, bf16[256,1024]{1,0:T(8,128)(2,1)} %bitcast.199, ...), custom_call_target="tpu_custom_call" | custom-call | flops 536870912 | bytes 8388608 | tf_op jit(solution)/shard_map/mix/pallas_call | solution.py:529
  112.2 16.6 %all-gather.3.cloned.1.call-done = bf16[2048,1024]{1,0:T(8,128)(2,1)} async-done(((bf16[256,1024]{1,0:T(8,128)(2,1)}), bf16[2048,1024]{1,0:T(8,128)(2,1)}) %all-gather.3.cloned.1.call-update) | async-done | bytes 4194320 | tf_op jit(solution)/shard_map/all_gather | solution.py:840
  147.2 9.9 %collective-permute-done.18.f_ref = bf16[256,1024]{1,0:T(8,128)(2,1)S(1)} collective-permute-done((bf16[256,1024]{1,0:T(8,128)(2,1)S(1)}, bf16[256,1024]{1,0:T(8,128)(2,1)S(1)}, u32[]{:S(2)}, u32[]{:S(2)}) %collective-permute-start.18) | collective-permute-done | bytes 524320 | tf_op jit(solution)/shard_map/ppermute | solution.py:79
  158.2 3.3 second_norm.1
  168.1 8.0 %collective-permute-done.21.refs_6_ = bf16[256,1024]{1,0:T(8,128)(2,1)S(1)} collective-permute-done((bf16[256,1024]{1,0:T(8,128)(2,1)}, bf16[256,1024]{1,0:T(8,128)(2,1)S(1)}, u32[]{:S(2)}, u32[]{:S(2)}) %collective-permute-start.21) | collective-permute-done | bytes 524320 | tf_op jit(solution)/shard_map/ppermute | solution.py:79
  187.5 6.9 %weight_grad.2 = (f32[4,128,1024]{2,1,0:T(8,128)}, bf16[4,128,1024]{2,1,0:T(8,128)(2,1)}) custom-call(s32[2]{0:T(128)S(1)} %pad_add_fusion.1.spot_ref, bf16[256,1024]{1,0:T(8,128)(2,1)} %copy-done.30, bf16[256,1024]{1,0:T(8,128)(2,1)} %copy-done.71, bf16[256,1024]{1,0:T(8,128)(2,1)} %copy-done.73, bf16[256,1024]{1,0:T(8,128)(2,1)} %copy-done.72, ...), custom_call_target="tpu_custom_call" | custom-call | flops 2147483648 | bytes 8388608 | tf_op jit(solution)/shard_map/weight_grad/pallas_call | solution.py:663
  194.4 7.1 %weight_grad.3 = (f32[4,128,1024]{2,1,0:T(8,128)}, bf16[4,128,1024]{2,1,0:T(8,128)(2,1)}) custom-call(s32[2]{0:T(128)S(1)} %pad_add_fusion.1.spot_ref, bf16[256,1024]{1,0:T(8,128)(2,1)} %get-tuple-element.195.refs_0_, bf16[256,1024]{1,0:T(8,128)(2,1)} %collective-permute-done.13.refs_1_, bf16[256,1024]{1,0:T(8,128)(2,1)} %collective-permute-done.15.refs_2_, ...), custom_call_target="tpu_custom_call" | custom-call | flops 2147483648 | bytes 8388608 | tf_op jit(solution)/shard_map/weight_grad/pallas_call | solution.py:663
  202.5 4.5 %first_norm_back.1 = (f32[256,1024]{1,0:T(8,128)}, bf16[256,1024]{1,0:T(8,128)(2,1)}, f32[8,1024]{1,0:T(8,128)}, bf16[4,256,256]{2,1,0:T(8,128)(2,1)}) custom-call(s32[2]{0:T(128)S(1)} %pad_add_fusion.1.spot_ref, f32[256,1024]{1,0:T(8,128)S(1)} %copy-done.3, f32[256,1024]{1,0:T(8,128)S(1)} %fusion.60.k_ref, bf16[256,1024]{1,0:T(8,128)(2,1)} %copy-done.36, ...), custom_call_target="tpu_custom_call" | custom-call | flops 536870912 | bytes 8388608 | tf_op jit(solution)/shard_map/first_norm_back/pallas_call | solution.py:613
  213.2 4.2 %all-to-all-start.2 = ((bf16[4,256,256]{2,1,0:T(8,128)(2,1)}), bf16[4,256,256]{2,1,0:T(8,128)(2,1)}, u32[]{:S(2)}, u32[]{:S(2)}) async-start(bf16[4,256,256]{2,1,0:T(8,128)(2,1)} %get-tuple-element.206), calls=%async_computation.2 | async-start | bytes 1048576 | tf_op jit(solution)/shard_map/all_to_all | solution.py:225
  220.4 5.9 %all-to-all-done.2 = bf16[4,256,256]{2,1,0:T(8,128)(2,1)} async-done(((bf16[4,256,256]{2,1,0:T(8,128)(2,1)}), bf16[4,256,256]{2,1,0:T(8,128)(2,1)}, u32[]{:S(2)}, u32[]{:S(2)}) %all-to-all-start.2) | async-done | bytes 524320 | tf_op jit(solution)/shard_map/all_to_all | solution.py:225
  226.3 10.6 %collective-permute-done.26 = bf16[4,128,1024]{2,1,0:T(8,128)(2,1)} collective-permute-done((bf16[4,128,1024]{2,1,0:T(8,128)(2,1)}, bf16[4,128,1024]{2,1,0:T(8,128)(2,1)}, u32[]{:S(2)}, u32[]{:S(2)}) %collective-permute-start.26) | collective-permute-done | bytes 1048608 | tf_op jit(solution)/shard_map/ppermute | solution.py:79
  245.1 14.7 %attend_back.1 = (bf16[2,512,768]{2,1,0:T(8,128)(2,1)}, f32[2,8,512]{2,1,0:T(8,128)}, f32[2,8,128]{2,1,0:T(8,128)}, f32[4,128,768]{2,1,0:T(8,128)}, bf16[4,128,768]{2,1,0:T(8,128)(2,1)}) custom-call(s32[2]{0:T(128)S(1)} %pad_add_fusion.1.spot_ref, f32[4]{0:T(128)S(1)} %dynamic_slice.34.bias_ref, bf16[2,512,768]{2,1,0:T(8,128)(2,1)S(1)} %copy-done.12, ...), custom_call_target="tpu_custom_call" | custom-call | flops 4294967296 | bytes 10485760 | tf_op jit(solution)/shard_map/attend_back/pallas_call | solution.py:432
  265.1 4.0 %collective-permute-start.34 = (bf16[128,1024]{1,0:T(8,128)(2,1)S(1)}, bf16[128,1024]{1,0:T(8,128)(2,1)S(1)}, u32[]{:S(2)}, u32[]{:S(2)}) collective-permute-start(bf16[128,1024]{1,0:T(8,128)(2,1)S(1)} %get-tuple-element.291), channel_id=1, source_target_pairs={{0,8},{4,12},{8,0},{12,4},{16,24},{20,28},{24,16},{28,20},{1,9},{5... | collective-permute-start | bytes 786440 | tf_op jit(solution)/shard_map/ppermute | solution.py:79
  273.3 3.4 collective-permute-done.34
  276.7 12.8 %collective-permute-done.35 = bf16[128,1024]{1,0:T(8,128)(2,1)S(1)} collective-permute-done((bf16[128,1024]{1,0:T(8,128)(2,1)S(1)}, bf16[128,1024]{1,0:T(8,128)(2,1)S(1)}, u32[]{:S(2)}, u32[]{:S(2)}) %collective-permute-start.35) | collective-permute-done | bytes 262176 | tf_op jit(solution)/shard_map/ppermute | solution.py:79
  292.6 3.4 collective-permute-start.38
  300.4 4.8 %all-to-all-start.3 = ((f32[32,1,416]{2,1,0:T(1,128)}), f32[32,1,416]{2,1,0:T(1,128)S(1)}, u32[]{:S(2)}, u32[]{:S(2)}) async-start(f32[32,1,416]{2,1,0:T(1,128)} %reshape.641), calls=%async_computation.3 | async-start | bytes 131072 | tf_op jit(solution)/shard_map/all_to_all | solution.py:233
  305.3 5.0 %input_grad.1 = (f32[2,128,1024]{2,1,0:T(8,128)}, bf16[2,128,1024]{2,1,0:T(8,128)(2,1)}, f32[2,128,1024]{2,1,0:T(8,128)}, bf16[2,128,1024]{2,1,0:T(8,128)(2,1)}) custom-call(bf16[2,512,768]{2,1,0:T(8,128)(2,1)S(1)} %copy-done.10, bf16[1024,768]{1,0:T(8,128)(2,1)S(1)} %copy-done.9), custom_call_target="tpu_custom_call" | custom-call | flops 1610612736 | bytes 8388608 | tf_op jit(solution)/shard_map/input_grad/pallas_call | solution.py:691
  317.8 10.3 %collective-permute-done.39 = bf16[128,768]{1,0:T(8,128)(2,1)S(1)} collective-permute-done((bf16[128,768]{1,0:T(8,128)(2,1)}, bf16[128,768]{1,0:T(8,128)(2,1)S(1)}, u32[]{:S(2)}, u32[]{:S(2)}) %collective-permute-start.39) | collective-permute-done | bytes 196640 | tf_op jit(solution)/shard_map/ppermute | solution.py:79
  331.0 3.6 all-to-all-start.4
  334.7 6.3 %collective-permute-start.44 = (bf16[1,32,1024]{2,1,0:T(8,128)(2,1)S(1)}, bf16[1,32,1024]{2,1,0:T(8,128)(2,1)S(1)}, u32[]{:S(2)}, u32[]{:S(2)}) collective-permute-start(bf16[1,32,1024]{2,1,0:T(8,128)(2,1)S(1)} %dynamic-slice_convert_fusion.3), channel_id=1, source_target_pairs={{0,16},{4,20},{8,24},{12,28},{16,0},{20,4},{24,8},{28,12},{1,17},{... | collective-permute-start | bytes 196616 | tf_op jit(solution)/shard_map/ppermute | solution.py:79
  350.4 5.9 %collective-permute-done.43 = bf16[2,128,1024]{2,1,0:T(8,128)(2,1)} collective-permute-done((bf16[2,128,1024]{2,1,0:T(8,128)(2,1)}, bf16[2,128,1024]{2,1,0:T(8,128)(2,1)}, u32[]{:S(2)}, u32[]{:S(2)}) %collective-permute-start.43) | collective-permute-done | bytes 524320 | tf_op jit(solution)/shard_map/ppermute | solution.py:79
  (389 shorter events, 127.9 us)
Async XLA Ops:
  16.0 112.7 %all-gather.3.cloned.1.call-start = ((), (), s32[]{:S(2)}) async-start(), calls=%async_computation.5 | async-start | bytes 4718592 | tf_op jit(solution)/shard_map/all_gather | solution.py:840
  16.1 19.8 %collective-permute-start.4 = (bf16[2,128,1024]{2,1,0:T(8,128)(2,1)S(1)}, bf16[2,128,1024]{2,1,0:T(8,128)(2,1)}, u32[]{:S(2)}, u32[]{:S(2)}) collective-permute-start(bf16[2,128,1024]{2,1,0:T(8,128)(2,1)S(1)} %copy-done.43), channel_id=1, source_target_pairs={{0,2},{1,3},{2,0},{3,1},{4,6},{5,7},{6,4},{7,5},{8,10},{9,11},{10,... | collective-permute-start | bytes 1572872 | tf_op jit(solution)/shard_map/ppermute | solution.py:79
  25.4 21.8 %collective-permute-start = (bf16[1,528,256]{2,1,0:T(8,128)(2,1)S(1)}, bf16[1,528,256]{2,1,0:T(8,128)(2,1)S(1)}, u32[]{:S(2)}, u32[]{:S(2)}) collective-permute-start(bf16[1,528,256]{2,1,0:T(8,128)(2,1)S(1)} %fusion.48.refs_0_), channel_id=1, source_target_pairs={{0,16},{4,20},{8,24},{12,28},{16,0},{20,4},{24,8},{28,12},{1,17},{... | collective-permute-start | bytes 811016 | tf_op jit(solution)/shard_map/ppermute | solution.py:79
  28.5 18.7 %collective-permute-start.1 = (bf16[1,528,256]{2,1,0:T(8,128)(2,1)S(1)}, bf16[1,528,256]{2,1,0:T(8,128)(2,1)S(1)}, u32[]{:S(2)}, u32[]{:S(2)}) collective-permute-start(bf16[1,528,256]{2,1,0:T(8,128)(2,1)S(1)} %fusion.48.refs_0_), channel_id=1, source_target_pairs={{0,8},{4,12},{8,0},{12,4},{16,24},{20,28},{24,16},{28,20},{1,9},{5... | collective-permute-start | bytes 811016 | tf_op jit(solution)/shard_map/ppermute | solution.py:79
  30.1 17.1 %collective-permute-start.2 = (bf16[1,528,256]{2,1,0:T(8,128)(2,1)S(1)}, bf16[1,528,256]{2,1,0:T(8,128)(2,1)S(1)}, u32[]{:S(2)}, u32[]{:S(2)}) collective-permute-start(bf16[1,528,256]{2,1,0:T(8,128)(2,1)S(1)} %fusion.48.refs_0_), channel_id=1, source_target_pairs={{0,24},{4,28},{8,16},{12,20},{16,8},{20,12},{24,0},{28,4},{1,25},{... | collective-permute-start | bytes 811016 | tf_op jit(solution)/shard_map/ppermute | solution.py:79
  30.1 17.1 %collective-permute-start.3 = (bf16[1,528,256]{2,1,0:T(8,128)(2,1)S(1)}, bf16[1,528,256]{2,1,0:T(8,128)(2,1)S(1)}, u32[]{:S(2)}, u32[]{:S(2)}) collective-permute-start(bf16[1,528,256]{2,1,0:T(8,128)(2,1)S(1)} %fusion.48.refs_0_), channel_id=1, source_target_pairs={{0,4},{4,0},{8,12},{12,8},{16,20},{20,16},{24,28},{28,24},{1,5},{5... | collective-permute-start | bytes 811016 | tf_op jit(solution)/shard_map/ppermute | solution.py:79
  48.6 26.3 %collective-permute-start.8 = (bf16[2,128,1024]{2,1,0:T(8,128)(2,1)S(1)}, bf16[2,128,1024]{2,1,0:T(8,128)(2,1)}, u32[]{:S(2)}, u32[]{:S(2)}) collective-permute-start(bf16[2,128,1024]{2,1,0:T(8,128)(2,1)S(1)} %copy-done.43), channel_id=1, source_target_pairs={{0,1},{1,0},{2,3},{3,2},{4,5},{5,4},{6,7},{7,6},{8,9},{9,8},{10,11... | collective-permute-start | bytes 1572872 | tf_op jit(solution)/shard_map/ppermute | solution.py:79
  48.7 26.2 %collective-permute-start.9 = (bf16[2,128,1024]{2,1,0:T(8,128)(2,1)}, bf16[2,128,1024]{2,1,0:T(8,128)(2,1)}, u32[]{:S(2)}, u32[]{:S(2)}) collective-permute-start(bf16[2,128,1024]{2,1,0:T(8,128)(2,1)} %collective-permute-done.4.refs_10_.refs_3_), channel_id=1, source_target_pairs={{0,1},{1,0},{2,3},{3,2},{4,5},{5,4},{6,7},{7,6},{8,9},{9,8},{10,11... | collective-permute-start | bytes 1572872 | tf_op jit(solution)/shard_map/ppermute | solution.py:79
  50.7 15.0 %collective-permute-start.6 = (bf16[1,528,256]{2,1,0:T(8,128)(2,1)S(1)}, bf16[1,528,256]{2,1,0:T(8,128)(2,1)S(1)}, u32[]{:S(2)}, u32[]{:S(2)}) collective-permute-start(bf16[1,528,256]{2,1,0:T(8,128)(2,1)S(1)} %collective-permute-done.1.refs_2_), channel_id=1, source_target_pairs={{0,4},{4,0},{8,12},{12,8},{16,20},{20,16},{24,28},{28,24},{1,5},{5... | collective-permute-start | bytes 811016 | tf_op jit(solution)/shard_map/ppermute | solution.py:79
  51.2 23.6 %collective-permute-start.7 = (bf16[1,528,256]{2,1,0:T(8,128)(2,1)S(1)}, bf16[1,528,256]{2,1,0:T(8,128)(2,1)S(1)}, u32[]{:S(2)}, u32[]{:S(2)}) collective-permute-start(bf16[1,528,256]{2,1,0:T(8,128)(2,1)S(1)} %collective-permute-done.2.refs_3_), channel_id=1, source_target_pairs={{0,4},{4,0},{8,12},{12,8},{16,20},{20,16},{24,28},{28,24},{1,5},{5... | collective-permute-start | bytes 811016 | tf_op jit(solution)/shard_map/ppermute | solution.py:79
  111.8 20.6 %collective-permute-start.13 = (bf16[256,1024]{1,0:T(8,128)(2,1)}, bf16[256,1024]{1,0:T(8,128)(2,1)}, u32[]{:S(2)}, u32[]{:S(2)}) collective-permute-start(bf16[256,1024]{1,0:T(8,128)(2,1)} %get-tuple-element.195.refs_0_), channel_id=1, source_target_pairs={{0,1},{1,0},{2,3},{3,2},{4,5},{5,4},{6,7},{7,6},{8,9},{9,8},{10,11... | collective-permute-start | bytes 1572872 | tf_op jit(solution)/shard_map/ppermute | solution.py:79
  111.8 24.4 %collective-permute-start.15 = (bf16[256,1024]{1,0:T(8,128)(2,1)}, bf16[256,1024]{1,0:T(8,128)(2,1)}, u32[]{:S(2)}, u32[]{:S(2)}) collective-permute-start(bf16[256,1024]{1,0:T(8,128)(2,1)} %get-tuple-element.195.refs_0_), channel_id=1, source_target_pairs={{0,2},{1,3},{2,0},{3,1},{4,6},{5,7},{6,4},{7,5},{8,10},{9,11},{10,... | collective-permute-start | bytes 1572872 | tf_op jit(solution)/shard_map/ppermute | solution.py:79
  140.2 17.0 %collective-permute-start.14 = (bf16[256,1024]{1,0:T(8,128)(2,1)S(1)}, bf16[256,1024]{1,0:T(8,128)(2,1)S(1)}, u32[]{:S(2)}, u32[]{:S(2)}) collective-permute-start(bf16[256,1024]{1,0:T(8,128)(2,1)S(1)} %convolution_convert_fusion.3), channel_id=1, source_target_pairs={{0,1},{1,0},{2,3},{3,2},{4,5},{5,4},{6,7},{7,6},{8,9},{9,8},{10,11... | collective-permute-start | bytes 1572872 | tf_op jit(solution)/shard_map/ppermute | solution.py:79
  180.5 21.0 %collective-permute-start.20 = (bf16[256,1024]{1,0:T(8,128)(2,1)}, bf16[256,1024]{1,0:T(8,128)(2,1)S(1)}, u32[]{:S(2)}, u32[]{:S(2)}) collective-permute-start(bf16[256,1024]{1,0:T(8,128)(2,1)} %convolution_convert_fusion.1), channel_id=1, source_target_pairs={{0,1},{1,0},{2,3},{3,2},{4,5},{5,4},{6,7},{7,6},{8,9},{9,8},{10,11... | collective-permute-start | bytes 1572872 | tf_op jit(solution)/shard_map/ppermute | solution.py:79
  185.9 15.6 %collective-permute-start.24 = (bf16[256,1024]{1,0:T(8,128)(2,1)S(1)}, bf16[256,1024]{1,0:T(8,128)(2,1)S(1)}, u32[]{:S(2)}, u32[]{:S(2)}) collective-permute-start(bf16[256,1024]{1,0:T(8,128)(2,1)S(1)} %add_convert_fusion.1), channel_id=1, source_target_pairs={{0,2},{1,3},{2,0},{3,1},{4,6},{5,7},{6,4},{7,5},{8,10},{9,11},{10,... | collective-permute-start | bytes 1572872 | tf_op jit(solution)/shard_map/ppermute | solution.py:79
  211.1 25.8 %collective-permute-start.26 = (bf16[4,128,1024]{2,1,0:T(8,128)(2,1)}, bf16[4,128,1024]{2,1,0:T(8,128)(2,1)}, u32[]{:S(2)}, u32[]{:S(2)}) collective-permute-start(bf16[4,128,1024]{2,1,0:T(8,128)(2,1)} %get-tuple-element.208), channel_id=1, source_target_pairs={{0,4},{4,0},{8,12},{12,8},{16,20},{20,16},{24,28},{28,24},{1,5},{5... | collective-permute-start | bytes 3145736 | tf_op jit(solution)/shard_map/ppermute | solution.py:79
  236.9 26.0 %collective-permute-start.27 = (bf16[4,128,1024]{2,1,0:T(8,128)(2,1)}, bf16[4,128,1024]{2,1,0:T(8,128)(2,1)S(1)}, u32[]{:S(2)}, u32[]{:S(2)}) collective-permute-start(bf16[4,128,1024]{2,1,0:T(8,128)(2,1)} %get-tuple-element.221), channel_id=1, source_target_pairs={{0,4},{4,0},{8,12},{12,8},{16,20},{20,16},{24,28},{28,24},{1,5},{5... | collective-permute-start | bytes 3145736 | tf_op jit(solution)/shard_map/ppermute | solution.py:79
  240.0 20.9 %collective-permute-start.29 = (bf16[128,1024]{1,0:T(8,128)(2,1)S(1)}, bf16[128,1024]{1,0:T(8,128)(2,1)S(1)}, u32[]{:S(2)}, u32[]{:S(2)}) collective-permute-start(bf16[128,1024]{1,0:T(8,128)(2,1)S(1)} %get-tuple-element.294), channel_id=1, source_target_pairs={{0,8},{4,12},{8,0},{12,4},{16,24},{20,28},{24,16},{28,20},{1,9},{5... | collective-permute-start | bytes 786440 | tf_op jit(solution)/shard_map/ppermute | solution.py:79
  240.9 22.0 %collective-permute-start.28 = (bf16[8,1,32,1024]{3,2,0,1:T(8,128)(2,1)S(1)}, bf16[8,1,32,1024]{3,2,0,1:T(8,128)(2,1)S(1)}, u32[]{:S(2)}, u32[]{:S(2)}) collective-permute-start(bf16[8,1,32,1024]{3,2,0,1:T(8,128)(2,1)S(1)} %dynamic-slice_convert_fusion), channel_id=1, source_target_pairs={{0,2},{1,3},{2,0},{3,1},{4,6},{5,7},{6,4},{7,5},{8,10},{9,11},{10,... | collective-permute-start | bytes 1572872 | tf_op jit(solution)/shard_map/ppermute | solution.py:79
  241.5 21.4 %collective-permute-start.30 = (bf16[128,1024]{1,0:T(8,128)(2,1)S(1)}, bf16[128,1024]{1,0:T(8,128)(2,1)S(1)}, u32[]{:S(2)}, u32[]{:S(2)}) collective-permute-start(bf16[128,1024]{1,0:T(8,128)(2,1)S(1)} %get-tuple-element.293), channel_id=1, source_target_pairs={{0,16},{4,20},{8,24},{12,28},{16,0},{20,4},{24,8},{28,12},{1,17},{... | collective-permute-start | bytes 786440 | tf_op jit(solution)/shard_map/ppermute | solution.py:79
  242.9 20.1 %collective-permute-start.31 = (bf16[128,1024]{1,0:T(8,128)(2,1)S(1)}, bf16[128,1024]{1,0:T(8,128)(2,1)S(1)}, u32[]{:S(2)}, u32[]{:S(2)}) collective-permute-start(bf16[128,1024]{1,0:T(8,128)(2,1)S(1)} %get-tuple-element.292), channel_id=1, source_target_pairs={{0,24},{4,28},{8,16},{12,20},{16,8},{20,12},{24,0},{28,4},{1,25},{... | collective-permute-start | bytes 786440 | tf_op jit(solution)/shard_map/ppermute | solution.py:79
  263.0 27.3 %collective-permute-start.32 = (bf16[4,128,768]{2,1,0:T(8,128)(2,1)S(1)}, bf16[4,128,768]{2,1,0:T(8,128)(2,1)S(1)}, u32[]{:S(2)}, u32[]{:S(2)}) collective-permute-start(bf16[4,128,768]{2,1,0:T(8,128)(2,1)S(1)} %copy-done.67), channel_id=1, source_target_pairs={{0,4},{4,0},{8,12},{12,8},{16,20},{20,16},{24,28},{28,24},{1,5},{5... | collective-permute-start | bytes 2359304 | tf_op jit(solution)/shard_map/ppermute | solution.py:79
  269.1 20.4 %collective-permute-start.35 = (bf16[128,1024]{1,0:T(8,128)(2,1)S(1)}, bf16[128,1024]{1,0:T(8,128)(2,1)S(1)}, u32[]{:S(2)}, u32[]{:S(2)}) collective-permute-start(bf16[128,1024]{1,0:T(8,128)(2,1)S(1)} %get-tuple-element.290), channel_id=1, source_target_pairs={{0,16},{4,20},{8,24},{12,28},{16,0},{20,4},{24,8},{28,12},{1,17},{... | collective-permute-start | bytes 786440 | tf_op jit(solution)/shard_map/ppermute | solution.py:79
  269.9 19.5 %collective-permute-start.36 = (bf16[128,1024]{1,0:T(8,128)(2,1)S(1)}, bf16[128,1024]{1,0:T(8,128)(2,1)S(1)}, u32[]{:S(2)}, u32[]{:S(2)}) collective-permute-start(bf16[128,1024]{1,0:T(8,128)(2,1)S(1)} %get-tuple-element.289), channel_id=1, source_target_pairs={{0,24},{4,28},{8,16},{12,20},{16,8},{20,12},{24,0},{28,4},{1,25},{... | collective-permute-start | bytes 786440 | tf_op jit(solution)/shard_map/ppermute | solution.py:79
  271.7 17.8 %collective-permute-start.33 = (bf16[4,32,1024]{2,1,0:T(8,128)(2,1)S(1)}, bf16[4,32,1024]{2,1,0:T(8,128)(2,1)S(1)}, u32[]{:S(2)}, u32[]{:S(2)}) collective-permute-start(bf16[4,32,1024]{2,1,0:T(8,128)(2,1)S(1)} %fusion.27), channel_id=1, source_target_pairs={{0,4},{4,0},{8,12},{12,8},{16,20},{20,16},{24,28},{28,24},{1,5},{5... | collective-permute-start | bytes 786440 | tf_op jit(solution)/shard_map/ppermute | solution.py:79
  292.6 25.2 %collective-permute-start.38 = (bf16[128,768]{1,0:T(8,128)(2,1)}, bf16[128,768]{1,0:T(8,128)(2,1)}, u32[]{:S(2)}, u32[]{:S(2)}) collective-permute-start(bf16[128,768]{1,0:T(8,128)(2,1)} %get-tuple-element.297), channel_id=1, source_target_pairs={{0,8},{4,12},{8,0},{12,4},{16,24},{20,28},{24,16},{28,20},{1,9},{5... | collective-permute-start | bytes 589832 | tf_op jit(solution)/shard_map/ppermute | solution.py:79
  297.4 16.3 %collective-permute-start.37 = (bf16[2,32,1024]{2,1,0:T(8,128)(2,1)}, bf16[2,32,1024]{2,1,0:T(8,128)(2,1)S(1)}, u32[]{:S(2)}, u32[]{:S(2)}) collective-permute-start(bf16[2,32,1024]{2,1,0:T(8,128)(2,1)} %fusion.28), channel_id=1, source_target_pairs={{0,8},{4,12},{8,0},{12,4},{16,24},{20,28},{24,16},{28,20},{1,9},{5... | collective-permute-start | bytes 393224 | tf_op jit(solution)/shard_map/ppermute | solution.py:79
  300.4 15.9 %all-to-all-start.3 = ((f32[32,1,416]{2,1,0:T(1,128)}), f32[32,1,416]{2,1,0:T(1,128)S(1)}, u32[]{:S(2)}, u32[]{:S(2)}) async-start(f32[32,1,416]{2,1,0:T(1,128)} %reshape.641), calls=%async_computation.3 | async-start | bytes 131072 | tf_op jit(solution)/shard_map/all_to_all | solution.py:233
  310.3 17.8 %collective-permute-start.41 = (bf16[2,128,1024]{2,1,0:T(8,128)(2,1)}, bf16[2,128,1024]{2,1,0:T(8,128)(2,1)S(1)}, u32[]{:S(2)}, u32[]{:S(2)}) collective-permute-start(bf16[2,128,1024]{2,1,0:T(8,128)(2,1)} %get-tuple-element.251), channel_id=1, source_target_pairs={{0,1},{1,0},{2,3},{3,2},{4,5},{5,4},{6,7},{7,6},{8,9},{9,8},{10,11... | collective-permute-start | bytes 1572872 | tf_op jit(solution)/shard_map/ppermute | solution.py:79
  310.6 18.2 %collective-permute-start.42 = (bf16[2,128,1024]{2,1,0:T(8,128)(2,1)}, bf16[2,128,1024]{2,1,0:T(8,128)(2,1)S(1)}, u32[]{:S(2)}, u32[]{:S(2)}) collective-permute-start(bf16[2,128,1024]{2,1,0:T(8,128)(2,1)} %get-tuple-element.252), channel_id=1, source_target_pairs={{0,1},{1,0},{2,3},{3,2},{4,5},{5,4},{6,7},{7,6},{8,9},{9,8},{10,11... | collective-permute-start | bytes 1572872 | tf_op jit(solution)/shard_map/ppermute | solution.py:79
  310.8 17.3 %collective-permute-start.39 = (bf16[128,768]{1,0:T(8,128)(2,1)}, bf16[128,768]{1,0:T(8,128)(2,1)S(1)}, u32[]{:S(2)}, u32[]{:S(2)}) collective-permute-start(bf16[128,768]{1,0:T(8,128)(2,1)} %get-tuple-element.296), channel_id=1, source_target_pairs={{0,16},{4,20},{8,24},{12,28},{16,0},{20,4},{24,8},{28,12},{1,17},{... | collective-permute-start | bytes 589832 | tf_op jit(solution)/shard_map/ppermute | solution.py:79
  331.0 16.8 %all-to-all-start.4 = ((bf16[4,224,256]{2,1,0:T(8,128)(2,1)}), bf16[4,224,256]{2,1,0:T(8,128)(2,1)S(1)}, u32[]{:S(2)}, u32[]{:S(2)}) async-start(bf16[4,224,256]{2,1,0:T(8,128)(2,1)} %pad_maximum_fusion.2), calls=%async_computation.4 | async-start | bytes 917504 | tf_op jit(solution)/shard_map/all_to_all | solution.py:225
  (93 other events, 905.9 us)
Sparse Core Ops, SparseCore 0:
  48.4 80.3 all-gather.2

commit v3 on v2

--- a/solution.py
+++ b/solution.py
@@ -221,8 +221,9 @@
     return lax.optimization_barrier((values, others))[0]
 
 
-def to_near(values):
-    return lax.all_to_all(values, "seq", 0, 0)
+def exchange(pieces):
+    seqs = len(pieces)
+    return [pieces[0]] + [swap(pieces[rel], "seq", seqs, rel) for rel in range(1, seqs)]
 
 
 def fence(*values):
@@ -259,8 +260,8 @@
         xs = refs[n_arrays : n_arrays + seqs]
         vec_ref, col_ref, row_ref, mask_ref = refs[n_arrays + seqs : n_arrays + seqs + 4]
         qkv_ref, lse_ref, full_ref = refs[n_arrays + seqs + 4 : n_arrays + seqs + 7]
-        ctx_ref, x_all, sems = refs[n_arrays + seqs + 7 :]
-        seq = spot_ref[1]
+        ctx_refs = refs[n_arrays + seqs + 7 : n_arrays + 2 * seqs + 7]
+        x_all, sems = refs[n_arrays + 2 * seqs + 7 :]
         page = spot_ref[0]
         step = pl.program_id(0)
 
@@ -304,7 +305,7 @@
         for group, value in enumerate(context):
             value = value.astype(LOW)
             for r in range(seqs):
-                ctx_ref[seq ^ r, 0, :, group * 128 : group * 128 + 128] = value[r * rows : (r + 1) * rows]
+                ctx_refs[r][0, :, group * 128 : group * 128 + 128] = value[r * rows : (r + 1) * rows]
 
     def per_page(shape):
         zeros = (0,) * len(shape)
@@ -315,16 +316,16 @@
         body,
         grid=(page_count,),
         out_shape=[
-            kept((page_count, slots, 3 * span), LOW),
-            kept((page_count, slots, 128), WIDE),
-            kept((width, 3 * span), LOW),
+            shaped((page_count, slots, 3 * span), LOW),
+            shaped((page_count, slots, 128), WIDE),
+            shaped((width, 3 * span), LOW),
         ]
-        + [shaped((seqs, page_count, rows, span), LOW)],
+        + [shaped((page_count, rows, span), LOW)] * seqs,
         in_specs=[scalars(), scalars()]
         + [remote()] * (n_arrays + seqs)
         + [fixed(vectors.shape), per_page((slots, 1)), per_page((1, slots)), per_page((1, slots))],
         out_specs=[per_page((slots, 3 * span)), per_page((slots, 128)), fixed((width, 3 * span))]
-        + [pl.BlockSpec((seqs, 1, rows, span), lambda i: (0, i, 0, 0))],
+        + [per_page((rows, span))] * seqs,
         scratch_shapes=[
             pltpu.VMEM((seqs, page_count, rows, width), LOW),
             pltpu.SemaphoreType.DMA((seqs + 3 * blocks,)),
@@ -338,7 +339,7 @@
 def attend_back(spot, own_bias, qkv, lse, grads, inputs, column, row, mask, heads, depth, pages):
     page_count, slots, triple = qkv.shape
     span = triple // 3
-    seqs = grads.shape[0]
+    seqs = len(grads)
     rows = slots // seqs
     groups = span // 128
     width = inputs[0].shape[2]
@@ -346,17 +347,14 @@
     tile = 256 if width % 256 == 0 else width
 
     def body(spot_ref, bias_ref, qkv_ref, lse_ref, *refs):
-        grad_ref, x_refs = refs[0], refs[1 : seqs + 1]
-        col_ref, row_ref, mask_ref, out_ref, sum_ref, cell_ref, keep, send = refs[seqs + 1 : seqs + 9]
-        full, x_all, g_all, sems = refs[seqs + 9 :]
+        grad_refs, x_refs = refs[:seqs], refs[seqs : 2 * seqs]
+        col_ref, row_ref, mask_ref, out_ref, sum_ref, cell_ref, keep, send = refs[2 * seqs : 2 * seqs + 8]
+        full, x_all, g_all, sems = refs[2 * seqs + 8 :]
         step = pl.program_id(0)
 
         @pl.when(step == 0)
         def _():
-            pairs = []
-            for k in range(seqs):
-                start = pl.multiple_of((spot_ref[1] ^ k) * rows, rows)
-                pairs.append((grad_ref.at[k], g_all.at[:, pl.ds(start, rows), :]))
+            pairs = [(grad_refs[r], g_all.at[:, pl.ds(r * rows, rows), :]) for r in range(seqs)]
             pairs += [(x_refs[r], x_all.at[:, pl.ds(r * rows, rows), :]) for r in range(seqs)]
             for copy in bring(pairs, sems):
                 copy.wait()
@@ -416,13 +414,11 @@
 
         @pl.when(step == page_count - 1)
         def _():
-            for rel in range(pages):
-                start = pl.multiple_of((page ^ rel) * block, block)
-                value = full[pl.ds(start, block), :]
-                if rel % 2 == 0:
-                    keep[rel // 2] = value
-                else:
-                    send[rel // 2] = value.astype(LOW)
+            low = page % 2
+            for k in range(pages // 2):
+                keep[k] = full[pl.ds(pl.multiple_of((2 * k + low) * block, block), block), :]
+                start = pl.multiple_of((2 * k + 1 - low) * block, block)
+                send[k] = full[pl.ds(start, block), :].astype(LOW)
 
     def per_page(shape):
         zeros = (0,) * len(shape)
@@ -440,7 +436,7 @@
             shaped((pages // 2, block, triple), LOW),
         ],
         in_specs=[scalars(), scalars(), per_page((slots, triple)), per_page((slots, 128))]
-        + [remote()] * (1 + seqs)
+        + [remote()] * (2 * seqs)
         + [per_page((slots, 1)), per_page((1, slots)), per_page((1, slots))],
         out_specs=[
             per_page((slots, triple)),
@@ -458,7 +454,7 @@
         compiler_params=params(28),
         cost_estimate=cost(flops, 10 << 20, page_count * heads * slots * slots),
         name="attend_back",
-    )(spot, own_bias, *inside([qkv, lse]), *outside([grads]), *outside(inputs), column, row, mask)
+    )(spot, own_bias, *outside([qkv, lse]), *outside(grads), *outside(inputs), column, row, mask)
 
 
 def page_order(values, rels, page_index):
@@ -505,17 +501,19 @@
 
 def mix(spot, contexts, w_mix, inputs, vectors):
     flat, width = inputs.shape
-    seqs = contexts.shape[0]
+    seqs = len(contexts)
     span = width // seqs
 
     def body(spot_ref, *refs):
-        c_ref, w_ref, x_ref, vec_ref, wide_ref, low_ref, hat_ref, rstd_ref, c_all, x_here, sems = refs
-        copies = bring([(c_ref.at[k], c_all.at[k]) for k in range(seqs)] + [(x_ref, x_here)], sems)
+        c_refs = refs[:seqs]
+        w_ref, x_ref, vec_ref, wide_ref, low_ref, hat_ref, rstd_ref, c_all, x_here, sems = refs[seqs:]
+        copies = bring([(c_refs[r], c_all.at[r]) for r in range(seqs)] + [(x_ref, x_here)], sems)
         for copy in copies:
             copy.wait()
         total = x_here[...].astype(WIDE) + vec_ref[2:3, :]
-        for k in range(seqs):
-            total = total + mul(c_all[k], w_ref[k * span : (k + 1) * span, :])
+        for r in range(seqs):
+            start = pl.multiple_of((spot_ref[1] ^ r) * span, span)
+            total = total + mul(c_all[r], w_ref[pl.ds(start, span), :])
         center = total - jnp.mean(total, axis=-1, keepdims=True)
         spread = jnp.mean(center * center, axis=-1, keepdims=True)
         rstd = lax.rsqrt(spread + 1e-05)
@@ -531,10 +529,10 @@
         out_shape=[
             kept((flat, width), WIDE),
             shaped((flat, width), LOW),
-            kept((flat, width), WIDE),
-            kept((flat, 128), WIDE),
+            shaped((flat, width), WIDE),
+            shaped((flat, 128), WIDE),
         ],
-        in_specs=[scalars()] + [remote(), near(), remote(), near()],
+        in_specs=[scalars()] + [remote()] * seqs + [near(), remote(), near()],
         out_specs=[near()] * 4,
         scratch_shapes=[
             pltpu.VMEM((seqs, flat, span), LOW),
@@ -544,7 +542,7 @@
         compiler_params=params(12),
         cost_estimate=cost(2 * flat * width * width, 8 << 20),
         name="mix",
-    )(spot, *outside([contexts]), *inside([w_mix]), *outside([inputs]), vectors)
+    )(spot, *outside(contexts), *inside([w_mix]), *outside([inputs]), vectors)
 
 
 def second_norm(normed, keep, close, far, vectors, cotangent):
@@ -587,16 +585,27 @@
     )(*inside([normed]), keep, *outside([close, far]), vectors, *outside([cotangent]))
 
 
-def first_norm_back(spot, grad_second, keep, close, far, hat, rstd, vectors, w_mix, seqs):
+def first_norm_back(spot, grad_second, keep, close, far, hat, rstd, vectors, w_mix, contexts, pages):
     flat, width = grad_second.shape
+    seqs = len(contexts)
     span = width // seqs
-
-    def body(spot_ref, d_ref, k_ref, n_ref, f_ref, hat_ref, rstd_ref, vec_ref, w_ref, wide, low, sums, *rest):
-        outs, n_here, f_here, sems = rest
-        for copy in bring([(n_ref, n_here), (f_ref, f_here)], sems):
-            copy.wait()
+    rows = width // (pages * seqs)
+    with_mix = rows % 16 == 0
+
+    def body(spot_ref, d_ref, k_ref, n_ref, f_ref, hat_ref, rstd_ref, vec_ref, w_ref, *refs):
+        c_refs, (wide, low, sums) = refs[:seqs], refs[seqs : seqs + 3]
+        outs, rest = refs[seqs + 3 : 2 * seqs + 3], refs[2 * seqs + 3 :]
+        if with_mix:
+            mix_keep, mix_send, n_here, f_here, c_here, hat_here, full, sems = rest
+        else:
+            n_here, f_here, c_here, hat_here, full, sems = rest
+        pairs = [(n_ref, n_here), (f_ref, f_here), (hat_ref, hat_here)]
+        copies = bring(pairs + [(c_refs[r], c_here.at[r]) for r in range(seqs)], sems)
+        copies[0].wait()
+        copies[1].wait()
+        copies[2].wait()
         grad = d_ref[...] + (k_ref[...] + n_here[...].astype(WIDE) + f_here[...].astype(WIDE))
-        hat = hat_ref[...]
+        hat = hat_here[...]
         slope = grad * vec_ref[10:11, :]
         first = jnp.mean(slope, axis=-1, keepdims=True)
         second = jnp.mean(slope * hat, axis=-1, keepdims=True)
@@ -604,26 +613,61 @@
         wide[...] = result
         result_low = result.astype(LOW)
         low[...] = result_low
-        for k in range(seqs):
-            outs[k] = mul(result_low, w_ref[k * span : (k + 1) * span, :], NT).astype(LOW)
+        for r in range(seqs):
+            start = pl.multiple_of((spot_ref[1] ^ r) * span, span)
+            outs[r][...] = mul(result_low, w_ref[pl.ds(start, span), :], NT).astype(LOW)
         sums[0:1, :] = jnp.sum(grad * hat, axis=0, keepdims=True)
         sums[1:2, :] = jnp.sum(grad, axis=0, keepdims=True)
         sums[2:3, :] = jnp.sum(result, axis=0, keepdims=True)
-
+        for copy in copies[3:]:
+            copy.wait()
+        if with_mix:
+            for r in range(seqs):
+                start = pl.multiple_of((spot_ref[1] ^ r) * span, span)
+                full[pl.ds(start, span), :] = mul(c_here[r], result_low, TN)
+            bit = spot_ref[1] % 2
+            for p in range(pages):
+                for k in range(seqs // 2):
+                    start = pl.multiple_of((p * seqs + 2 * k + bit) * rows, rows)
+                    mix_keep[p, k] = full[pl.ds(start, rows), :]
+                    start = pl.multiple_of((p * seqs + 2 * k + 1 - bit) * rows, rows)
+                    mix_send[p, k] = full[pl.ds(start, rows), :].astype(LOW)
+
+    mix_shape = (pages, seqs // 2, rows, width)
     return pl.pallas_call(
         body,
-        out_shape=[shaped((flat, width), WIDE), shaped((flat, width), LOW), shaped((8, width), WIDE)]
-        + [shaped((seqs, flat, span), LOW)],
-        in_specs=[scalars(), near(), near(), remote(), remote()] + [near()] * 4,
-        out_specs=[near()] * 4,
-        scratch_shapes=[pltpu.VMEM((flat, width), LOW)] * 2 + [pltpu.SemaphoreType.DMA((2,))],
-        compiler_params=params(12),
+        out_shape=[
+            shaped((flat, width), WIDE),
+            shaped((flat, width), LOW),
+            shaped((8, width), WIDE),
+        ]
+        + [shaped((flat, span), LOW)] * seqs
+        + ([shaped(mix_shape, WIDE), shaped(mix_shape, LOW)] if with_mix else []),
+        in_specs=[scalars(), near(), near(), remote(), remote(), remote()] + [near()] * 3 + [remote()] * seqs,
+        out_specs=[near()] * (3 + seqs + 2 * with_mix),
+        scratch_shapes=[pltpu.VMEM((flat, width), LOW)] * 2
+        + [
+            pltpu.VMEM((seqs, flat, span), LOW),
+            pltpu.VMEM((flat, width), WIDE),
+            pltpu.VMEM((width, width), WIDE),
+            pltpu.SemaphoreType.DMA((3 + seqs,)),
+        ],
+        compiler_params=params(20),
         cost_estimate=cost(2 * flat * width * width, 8 << 20),
         name="first_norm_back",
-    )(spot, *inside([grad_second]), keep, *outside([close, far]), *inside([hat, rstd]), vectors, *inside([w_mix]))
-
-
-def weight_grad(spot, lefts, rights, pages, split):
+    )(
+        spot,
+        *inside([grad_second]),
+        keep,
+        *outside([close, far]),
+        *outside([hat, rstd]),
+        vectors,
+        *inside([w_mix]),
+        *outside(contexts),
+    )
+
+
+def weight_grad(spot, lefts, rights, pages, split, base=None):
     count = len(lefts)
     tokens, height = lefts[0].shape
     width = rights[0].shape[1]
@@ -632,7 +676,8 @@
 
     def body(spot_ref, *refs):
         left, right = refs[:count], refs[count : 2 * count]
-        outs = refs[2 * count : -4]
+        base_ref = refs[2 * count] if base is not None else None
+        outs = refs[2 * count + (base is not None) : -4]
         full, l_all, r_all, sems = refs[-4:]
         page = spot_ref[0]
         pairs = []
@@ -643,27 +688,24 @@
             copy.wait()
         for at in range(0, height, tile):
             value = mul(l_all[:, at : at + tile], r_all[...], TN)
-            if split:
-                full[at : at + tile, :] = value
-            else:
-                outs[0][at : at + tile, :] = value.astype(LOW)
+            if base is not None:
+                value = value + base_ref[at : at + tile, :]
+            (full if split else outs[0])[at : at + tile, :] = value
         if split:
-            for rel in range(pages):
-                start = pl.multiple_of((page ^ rel) * rows, rows)
-                value = full[pl.ds(start, rows), :]
-                if rel % 2 == 0:
-                    outs[0][rel // 2] = value
-                else:
-                    outs[1][rel // 2] = value.astype(LOW)
+            low = page % 2
+            for k in range(pages // 2):
+                outs[0][k] = full[pl.ds(pl.multiple_of((2 * k + low) * rows, rows), rows), :]
+                start = pl.multiple_of((2 * k + 1 - low) * rows, rows)
+                outs[1][k] = full[pl.ds(start, rows), :].astype(LOW)
 
     if split:
         outs = [shaped((pages // 2, rows, width), WIDE), shaped((pages // 2, rows, width), LOW)]
     else:
-        outs = [shaped((height, width), LOW)]
+        outs = [kept((height, width), WIDE)]
     return pl.pallas_call(
         body,
         out_shape=outs,
-        in_specs=[scalars()] + [remote()] * (2 * count),
+        in_specs=[scalars()] + [remote()] * (2 * count) + [near()] * (base is not None),
         out_specs=[near()] * len(outs),
         scratch_shapes=[
             pltpu.VMEM((height, width) if split else (8, 128), WIDE),
@@ -674,7 +716,22 @@
         compiler_params=params(18),
         cost_estimate=cost(2 * count * tokens * height * width, 8 << 20),
         name="weight_grad",
-    )(spot, *outside(lefts), *outside(rights))
+    )(spot, *outside(lefts), *outside(rights), *(inside([base]) if base is not None else []))
+
+
+def widen(values):
+    def body(in_ref, out_ref):
+        out_ref[...] = in_ref[...].astype(WIDE)
+
+    return pl.pallas_call(
+        body,
+        out_shape=shaped(values.shape, WIDE),
+        in_specs=[near()],
+        out_specs=near(),
+        compiler_params=params(4),
+        cost_estimate=cost(values.size, 6 * values.size),
+        name="widen",
+    )(values)
 
 
 def input_grad(grad_proj, w_proj, seqs):
@@ -697,7 +754,7 @@
         compiler_params=params(14),
         cost_estimate=cost(2 * page_count * slots * triple * width, 8 << 20),
         name="input_grad",
-    )(grad_proj, *inside([w_proj]))
+    )(*outside([grad_proj, w_proj]))
 
 
 def local(counts, tokens, cells, lengths, cotangent, w_qkv, w_out, w_up, w_down, biases, gains, cell_bias):
@@ -743,6 +800,15 @@
             mask *= 2
         return totals[0], nears[0], far, ready[0]
 
+    groups = [[page for page in range(pages) if page % 2 == low] for low in range(2)]
+
+    def halved(keep, *got):
+        got = jnp.concatenate(got, axis=1) if len(got) > 1 else got[0]
+        return (keep + got.astype(WIDE)).astype(LOW).reshape(-1, keep.shape[-1])
+
+    def scatter_same(values):
+        return lax.psum_scatter(values, "page", scatter_dimension=0, tiled=True, axis_index_groups=groups)
+
     def small_table(sums_proj, cells_grad):
         owners = pages * seqs
         here = lax.broadcasted_iota(jnp.int32, (seqs, 1, 1), 0) == seq_index
@@ -798,7 +864,7 @@
         ],
         axis=1,
     )
-    turned = to_near(sent)
+    turned = jnp.stack(reorder(turn(sent, seqs, seq_index), seq_index))
     part_qkv = turned[:, : 3 * rows].reshape(seqs, 3, rows, span).transpose(1, 0, 2, 3)
     extras = turned[:, 3 * rows : 3 * rows + extra.shape[0]]
     part_up = turned[:, 3 * rows + extra.shape[0] :].reshape(seqs * rows, ff_here)
@@ -858,7 +924,7 @@
     own_bias = lax.dynamic_slice_in_dim(cell_bias, seq_index * heads_here, heads_here)
     mix_part = jnp.concatenate([array[:, 3 * block : 4 * block, :] for array, _ in both_pieces], axis=0)
     mix_far = swap(mix_part, "seq", seqs, low_seq[-1])
-    qkv, lse, w_proj, contexts = attend(
+    qkv, lse, w_proj, *contexts = attend(
         [(after(array, mix_part), rel_list) for array, rel_list in both_pieces],
         block,
         spot,
@@ -871,36 +937,40 @@
         heads_here,
         depth,
     )
-    contexts, mix_part, mix_far, qkv, lse, w_proj = fence(contexts, mix_part, mix_far, qkv, lse, w_proj)
+    mix_part, mix_far, qkv, lse, w_proj, *contexts = fence(mix_part, mix_far, qkv, lse, w_proj, *contexts)
     mix_near = {0: mix_part, low_seq[-1]: mix_far}
     for bit in low_seq[:-1][::-1]:
         for rel in list(mix_near):
             mix_near[rel | bit] = swap(mix_near[rel], "seq", seqs, bit)
-    contexts = to_near(contexts).reshape(seqs, flat, span)
+    contexts = exchange([context.reshape(flat, span) for context in contexts])
     w_mix = assemble_mix([mix_near[rel] for rel in range(seqs)], both_rels, spot, rows, width)
 
     flat_inputs = tokens.reshape(flat, width)
     normed, normed_low, hat, rstd = mix(spot, contexts, w_mix, flat_inputs, vectors)
-    hidden, active, parts = [], [], []
-
-    def feed(pieces):
-        for piece in pieces:
+    hidden, active, parts = {}, {}, {}
+
+    def feed(rels, *others):
+        for rel in rels:
+            piece = after(normed_all[rel], *others)
             value = jnp.dot(piece, w_expand, preferred_element_type=WIDE) + hidden_bias
-            low = gelu_exact(value).astype(LOW)
-            part = jnp.dot(low, w_reduce, preferred_element_type=WIDE)
-            part = part.astype(LOW) if len(parts) % 2 else part
-            hidden.append(value)
-            active.append(low)
-            parts.append(part)
-        return tuple(parts)
-
-    normed_all = gather_near(normed_low, seqs, feed)
-    feed(normed_all[seqs // 2 :])
-    keep, close, far, ready = scatter_near(parts[0::2], parts[1::2])
+            active[rel] = gelu_exact(value).astype(LOW)
+            part = jnp.dot(active[rel], w_reduce, preferred_element_type=WIDE)
+            parts[rel] = part.astype(LOW) if rel % 2 else part
+            hidden[rel] = value
+
+    normed_all = gather_near(normed_low, seqs)
+    feed(range(seqs // 2, seqs))
+    far_parts = [swap(parts[rel], "seq", seqs, 1) for rel in range(seqs // 2 + 1, seqs, 2)]
+    far_sums = [parts[rel] + part.astype(WIDE) for rel, part in zip(range(seqs // 2, seqs, 2), far_parts)]
+    ready = far_sums[0].astype(LOW)
+    far = swap(ready, "seq", seqs, seqs // 2)
+    feed(range(seqs // 2), ready)
+    keep, close = parts[0], swap(parts[1], "seq", seqs, 1)
     slopes = [
         0.5 * (1.0 + lax.erf(u * 0.7071067811865476)) + u * jnp.exp(-0.5 * u * u) * 0.3989422804014327
-        for u in after(hidden, ready)
+        for u in after([hidden[rel] for rel in range(seqs)], ready)
     ]
+    active = [active[rel] for rel in range(seqs)]
     far, slopes = lax.optimization_barrier((far, slopes))
     output, grad_second, second_low, sums_two = second_norm(
         normed, keep, close, far, vectors, cotangent.reshape(flat, width)
@@ -918,62 +988,74 @@
             expanded.append(low)
             totals.append(jnp.sum(value, axis=0))
             parts.append(part)
-        return tuple(parts)
-
+        if len(parts) == len(pieces):
+            bases.extend(weight_grad(spot, active[: len(pieces)], pieces, pages, False))
+        return tuple(parts + bases)
+
+    bases = []
     second_all = gather_near(second_low, seqs, feed_back)
     feed_back(second_all[seqs // 2 :])
     keep, close, far, ready = scatter_near(parts[0::2], parts[1::2])
-    down_keep, down_send = weight_grad(spot, after(active, ready), second_all, pages, True)
-    up_keep, up_send = weight_grad(spot, after(normed_all, down_send), expanded, pages, True)
-    far, down_send, up_send = lax.optimization_barrier((far, down_send, up_send))
+    half = seqs // 2
+    down_keep, down_send = weight_grad(
+        spot, after(active[half:], ready), second_all[half:], pages, True, bases[0]
+    )
+    up_base = weight_grad(spot, after(normed_all[:half], down_send), expanded[:half], pages, False)[0]
+    far, up_base = fence(far, up_base)
     down_got = scatter_first(down_send, pages)
-    grad_first, first_low, sums_one, grad_contexts = first_norm_back(
-        spot, grad_second, keep, close, far, hat, rstd, vectors, w_mix, seqs
-    )
-    grad_contexts = to_near(grad_contexts)
-    context = jnp.concatenate([contexts[k] for k in range(seqs)], axis=1)
-    grad_mix = jnp.einsum("tc,td->cd", context, first_low, preferred_element_type=WIDE)
-    grad_mix = scatter_bits(grad_mix.reshape(pages, seqs, rows, width), "seq", seqs, 1, low_seq[:1])
-    grad_contexts, grad_mix, down_got, down_keep, up_send = fence(
-        grad_contexts, grad_mix, down_got, down_keep, up_send
-    )
-    down_sum = Sum(down_keep + down_got.astype(WIDE), pages)
+    grad_first, first_low, sums_one, *mix_grads = first_norm_back(
+        spot, grad_second, keep, close, far, hat, rstd, vectors, w_mix, contexts, pages
+    )
+    grad_contexts, mix_grads = mix_grads[:seqs], mix_grads[seqs:]
+    up_keep, up_send = weight_grad(
+        spot, after(normed_all[half:], first_low), expanded[half:], pages, True, up_base
+    )
+    grad_contexts = exchange(grad_contexts)
+    if mix_grads:
+        mix_keep, mix_send = mix_grads
+        mix_parts = swap(mix_send, "seq", seqs, 1)
+    else:
+        context = jnp.concatenate(reorder(contexts, seq_index), axis=1)
+        grad_mix = jnp.einsum("tc,td->cd", context, first_low, preferred_element_type=WIDE)
+        mix_keep, mix_parts = scatter_start(grad_mix.reshape(pages, seqs, rows, width), "seq", seqs, 1, 1)
+    mix_keep, mix_parts, down_got, down_keep, *others = fence(
+        mix_keep, mix_parts, down_got, down_keep, *grad_contexts, up_send
+    )
+    grad_contexts, up_send = others[:seqs], others[seqs]
+    down_half = halved(down_keep, down_got)
     up_got = scatter_first(up_send, pages)
-    mix_keep, mix_parts = scatter_start(grad_mix, "seq", seqs, 1, low_seq[1])
-    grad_contexts = after(grad_contexts, down_sum.ready)
-    grad_contexts = grad_contexts.reshape(seqs, page_count, row_count, span)
+    mix_total = (mix_keep + mix_parts.astype(WIDE)).reshape(pages, seqs // 2, rows, width)
+    mix_keep, mix_parts = scatter_start(mix_total, "seq", seqs, 1, low_seq[1])
+    grad_contexts = after(grad_contexts, down_half)
+    grad_reduce = scatter_same(down_half)
+    grad_contexts = [grad.reshape(page_count, row_count, span) for grad in grad_contexts]
     grad_proj, sums_proj, cells_grad, proj_keep, proj_send = attend_back(
         spot, own_bias, qkv, lse, grad_contexts, inputs, column, row, mask, heads_here, depth, pages
     )
-    down_parts = down_sum.parts
-    fenced = fence(
-        grad_proj, sums_proj, cells_grad, proj_keep, proj_send, up_keep, up_got, mix_keep, mix_parts, *down_parts
-    )
-    grad_proj, sums_proj, cells_grad, proj_keep, proj_send, up_keep, up_got, mix_keep, mix_parts = fenced[:9]
-    down_sum.parts = list(fenced[9:])
+    grad_proj, sums_proj, cells_grad, proj_keep, proj_send, up_keep, mix_keep, mix_parts = fence(
+        grad_proj, sums_proj, cells_grad, proj_keep, proj_send, up_keep, mix_keep, mix_parts
+    )
     proj_got = scatter_first(proj_send, pages)
-    up_sum = Sum(up_keep + up_got.astype(WIDE), pages)
-    grad_mix = mix_keep + mix_parts.astype(WIDE)
-    mix_keep, mix_parts = scatter_start(grad_mix.reshape(pages, rows, width), "page", pages, 0, 1)
-    fenced = fence(proj_got, proj_keep, mix_keep, mix_parts, grad_proj, sums_proj, cells_grad, *up_sum.parts)
-    proj_got, proj_keep, mix_keep, mix_parts, grad_proj, sums_proj, cells_grad = fenced[:7]
-    up_sum.parts = list(fenced[7:])
-    proj_sum = Sum(proj_keep + proj_got.astype(WIDE), pages)
-    small_sums = small_table(after(sums_proj, proj_sum.ready), after(cells_grad, proj_sum.ready))
-    grad_mix = after(mix_keep, proj_sum.ready) + mix_parts.astype(WIDE)
-    mix_keep, mix_parts = scatter_start(grad_mix, "page", pages, 0, 2)
-    parts = input_grad(after(grad_proj, proj_sum.ready), w_proj, seqs)
+    grad_mix = (mix_keep + mix_parts.astype(WIDE)).reshape(pages, rows, width)
+    mix_keep, mix_parts = scatter_start(grad_mix, "page", pages, 0, 1)
+    grad_expand = scatter_same(halved(up_keep, up_got))
+    parts = input_grad(after(grad_proj, proj_send), w_proj, seqs)
     near_parts = [swap(part, "seq", seqs, 1) for part in parts[1::2]]
-    grad_expand = up_sum.finish(proj_sum.ready)
-    fenced = fence(small_sums, mix_keep, mix_parts, grad_expand, *proj_sum.parts, *near_parts)
-    small_sums, mix_keep, mix_parts, grad_expand = fenced[:4]
-    proj_sum.parts = list(fenced[4 : 4 + len(proj_sum.parts)])
-    near_parts = list(fenced[4 + len(proj_sum.parts) :])
-    grad_qkv = proj_sum.finish()
-    grad_reduce = down_sum.finish(grad_qkv)
+    proj_got, proj_keep, sums_proj, cells_grad, mix_keep, mix_parts, grad_expand, grad_reduce, *near_parts = fence(
+        proj_got, proj_keep, sums_proj, cells_grad, mix_keep, mix_parts, grad_expand, grad_reduce, *near_parts
+    )
+    proj_half = halved(proj_keep, proj_got)
+    grad_qkv = scatter_same(proj_half)
+    grad_reduce = widen(after(grad_reduce, proj_half))
+    near_parts, sums_proj, cells_grad, mix_keep, mix_parts = after(
+        (near_parts, sums_proj, cells_grad, mix_keep, mix_parts), grad_reduce
+    )
+    keep, close, far = scatter_far(parts[0::2], near_parts)
+    small_sums = small_table(sums_proj, cells_grad)
+    mix_keep, mix_parts = scatter_start(mix_keep + mix_parts.astype(WIDE), "page", pages, 0, 2)
+    grad_qkv, far, small_sums, mix_keep, mix_parts = fence(grad_qkv, far, small_sums, mix_keep, mix_parts)
     grad_mix = mix_keep + mix_parts.astype(WIDE)
     grad_mix = scatter_bits(grad_mix, "page", pages, 0, low_page[2:]).reshape(rows, width)
-    keep, close, far = scatter_far(parts[0::2], near_parts)
     sent = jnp.concatenate(
         [
             grad_qkv.reshape(seqs, rows, 3, span).transpose(0, 2, 1, 3).reshape(seqs, 3 * rows, span),
@@ -981,7 +1063,7 @@
         ],
         axis=1,
     ).astype(LOW)
-    turned = to_near(sent)
+    turned = jnp.stack(reorder(turn(sent, seqs, seq_index), seq_index))
     grad_qkv = turned[:, : 3 * rows].reshape(seqs, 3, rows, span).transpose(2, 1, 0, 3)
     grad_qkv = grad_qkv.reshape(rows, 3 * width).astype(WIDE)
     grad_expand = turned[:, 3 * rows :].reshape(seqs, rows, pages, ff_rows).transpose(1, 2, 0, 3)

time: 373 us -> 311 us (0.83)
  starting transfers between devices: 71.7 us -> 39.3 us
  waiting for transfers between devices: 139 us -> 123 us
  Pallas kernels: 57.6 us -> 68.7 us
  local copies, waits for them, and re-layouts: 33.8 us -> 23.2 us
  matrix products: 22.5 us -> 15.7 us
  other arithmetic: 25.4 us -> 21.4 us
    all_to_all x4 -> x0, waiting for transfers between devices: 18.4 us -> none  [to_near(): return lax.all_to_all(values, 'seq', 0, 0)]
    ppermute x45 -> x48, starting transfers between devices: 51.3 us -> 35.6 us  [swap(): return lax.ppermute(values, axis, [(i, i ^ mask) for i in range(count)])]
    all_to_all x4 -> x0, starting transfers between devices: 15.6 us -> none  [to_near(): return lax.all_to_all(values, 'seq', 0, 0)]
    all_to_all x1, waiting for transfers between devices: 0.01 us -> 8.21 us  [to_all(): return lax.all_to_all(values, ('page', 'seq'), 0, 0)]
    unnamed x172 -> x142, local copies, waits for them, and re-layouts: 16.9 us -> 8.78 us
    all_gather x1, waiting for transfers between devices: 16.6 us -> 9.2 us  [local(): lax.all_gather(jnp.concatenate([part_up, w_down_low], axis=0), 'page', ax...]
    convert_element_type x0 -> x4, other arithmetic: none -> 6.46 us  [the longest x3 6.44 us: halved(): return (keep + got.astype(WIDE)).astype(LOW).reshape(-1, keep.shape[-1])]
    add x5 -> x3, other arithmetic: 5.18 us -> 0.49 us  [the longest x2 0.36 us: local(): mix_keep + mix_parts.astype(WIDE)]
  transfers between devices with their start and end apart: 51 -> 53, of which waited for: 20 -> 26; matrix products, arithmetic and copies ran while one was open for 14% -> 11% of each run, Pallas kernels for 14% -> 21%
where the time goes in v3:
time: 311 us; the launch traced here: 307 us
  waiting for transfers between devices  123 us (40%)
  Pallas kernels  68.7 us (22%)
  starting transfers between devices  39.3 us (13%)
  local copies, waits for them, and re-layouts  23.2 us (7%)
  other arithmetic  21.4 us (7%)
  matrix products  15.7 us (5%)
  between operations  15.5 us (5%)
    ppermute x48, waiting for transfers between devices, swap(): return lax.ppermute(values, axis, [(i, i ^ mask) for i in range(count)])  105 us
    ppermute x48, starting transfers between devices, swap(): return lax.ppermute(values, axis, [(i, i ^ mask) for i in range(count)])  35.6 us
    pallas_call x4, Pallas kernels, weight_grad(): pl.pallas_call(body, out_shape=outs, in_specs=[scalars()] + [remote()] *...  17.9 us
    pallas_call x1, Pallas kernels, attend_back(): pl.pallas_call(body, grid=(page_count,), out_shape=[shaped((page_count, s...  15.3 us
    pallas_call x1, Pallas kernels, attend(): pl.pallas_call(body, grid=(page_count,), out_shape=[shaped((page_count, s...  10.8 us
    all_gather x1, waiting for transfers between devices, local(): lax.all_gather(jnp.concatenate([part_up, w_down_low], axis=0), 'page', ax...  9.2 us
    unnamed x142, local copies, waits for them, and re-layouts  8.78 us
    all_to_all x1, waiting for transfers between devices, to_all(): return lax.all_to_all(values, ('page', 'seq'), 0, 0)  8.21 us
  transfers between devices with their start and end apart: 53, of which 26 were waited for; matrix products, arithmetic and copies ran while one was open for 11% of the time, Pallas kernels for 21%

profile of v3, /device:TPU:0, one launch (start us, length us, event | category | flops | bytes accessed | tf_op | source)
XLA Modules:
  0.0 306.8 jit_solution(16785681828234772982)
XLA Ops:
  11.1 2.5 collective-permute-start
  17.3 3.4 %collective-permute-done.1 = bf16[240,256]{1,0:T(8,128)(2,1)S(1)} collective-permute-done((bf16[240,256]{1,0:T(8,128)(2,1)S(1)}, bf16[240,256]{1,0:T(8,128)(2,1)S(1)}, u32[]{:S(2)}, u32[]{:S(2)}) %collective-permute-start.1) | collective-permute-done | bytes 122912 | tf_op jit(solution)/shard_map/ppermute | solution.py:79
  21.1 2.9 collective-permute-start.3
  27.6 10.2 %collective-permute-done.3.refs_1_ = bf16[1,528,256]{2,1,0:T(8,128)(2,1)S(1)} collective-permute-done((bf16[1,528,256]{2,1,0:T(8,128)(2,1)S(1)}, bf16[1,528,256]{2,1,0:T(8,128)(2,1)S(1)}, u32[]{:S(2)}, u32[]{:S(2)}) %collective-permute-start.3) | collective-permute-done | bytes 270368 | tf_op jit(solution)/shard_map/ppermute | solution.py:79
  37.9 5.5 %collective-permute-done.5.refs_3_ = bf16[1,528,256]{2,1,0:T(8,128)(2,1)S(1)} collective-permute-done((bf16[1,528,256]{2,1,0:T(8,128)(2,1)S(1)}, bf16[1,528,256]{2,1,0:T(8,128)(2,1)S(1)}, u32[]{:S(2)}, u32[]{:S(2)}) %collective-permute-start.5) | collective-permute-done | bytes 270368 | tf_op jit(solution)/shard_map/ppermute | solution.py:79
  49.1 5.4 %collective-permute-done.10.refs_7_ = bf16[1,528,256]{2,1,0:T(8,128)(2,1)S(1)} collective-permute-done((bf16[1,528,256]{2,1,0:T(8,128)(2,1)S(1)}, bf16[1,528,256]{2,1,0:T(8,128)(2,1)S(1)}, u32[]{:S(2)}, u32[]{:S(2)}) %collective-permute-start.10) | collective-permute-done | bytes 270368 | tf_op jit(solution)/shard_map/ppermute | solution.py:79
  54.5 5.9 %collective-permute-done.8.refs_5_ = bf16[1,528,256]{2,1,0:T(8,128)(2,1)S(1)} collective-permute-done((bf16[1,528,256]{2,1,0:T(8,128)(2,1)S(1)}, bf16[1,528,256]{2,1,0:T(8,128)(2,1)S(1)}, u32[]{:S(2)}, u32[]{:S(2)}) %collective-permute-start.8) | collective-permute-done | bytes 270368 | tf_op jit(solution)/shard_map/ppermute | solution.py:79
  60.5 10.4 %collective-permute-done.9.refs_6_ = bf16[1,528,256]{2,1,0:T(8,128)(2,1)S(1)} collective-permute-done((bf16[1,528,256]{2,1,0:T(8,128)(2,1)S(1)}, bf16[1,528,256]{2,1,0:T(8,128)(2,1)S(1)}, u32[]{:S(2)}, u32[]{:S(2)}) %collective-permute-start.9) | collective-permute-done | bytes 270368 | tf_op jit(solution)/shard_map/ppermute | solution.py:79
  74.4 10.8 %attend.1 = (bf16[2,512,768]{2,1,0:T(8,128)(2,1)}, f32[2,512,128]{2,1,0:T(8,128)}, bf16[1024,768]{1,0:T(8,128)(2,1)}, bf16[2,128,256]{2,1,0:T(8,128)(2,1)}, bf16...) custom-call(s32[2]{0:T(128)S(1)} %pad_add_fusion.1.spot_ref, ...), custom_call_target="tpu_custom_call" | custom-call | flops 2684354560 | bytes 10485760 | tf_op jit(solution)/shard_map/attend/pallas_call | solution.py:315
  95.0 4.1 %mix.1 = (f32[256,1024]{1,0:T(8,128)S(1)}, bf16[256,1024]{1,0:T(8,128)(2,1)}, f32[256,1024]{1,0:T(8,128)}, f32[256,128]{1,0:T(8,128)}) custom-call(s32[2]{0:T(128)S(1)} %pad_add_fusion.1.spot_ref, bf16[256,256]{1,0:T(8,128)(2,1)} %bitcast.238, bf16[256,256]{1,0:T(8,128)(2,1)} %copy-done.36, bf16[256,256]{1,0:T(8,128)(2,1)} %copy-done.37, ...), custom_call_target="tpu_custom_call" | custom-call | flops 536870912 | bytes 8388608 | tf_op jit(solution)/shard_map/mix/pallas_call | solution.py:527
  99.8 14.1 %collective-permute-done.19.refs_0_ = bf16[256,1024]{1,0:T(8,128)(2,1)S(1)} collective-permute-done((bf16[256,1024]{1,0:T(8,128)(2,1)}, bf16[256,1024]{1,0:T(8,128)(2,1)S(1)}, u32[]{:S(2)}, u32[]{:S(2)}) %collective-permute-start.19) | collective-permute-done | bytes 524320 | tf_op jit(solution)/shard_map/ppermute | solution.py:79
  116.8 9.2 %all-gather.3.cloned.1.call-done = bf16[2048,1024]{1,0:T(8,128)(2,1)} async-done(((bf16[256,1024]{1,0:T(8,128)(2,1)}), bf16[2048,1024]{1,0:T(8,128)(2,1)}) %all-gather.3.cloned.1.call-update) | async-done | bytes 4194320 | tf_op jit(solution)/shard_map/all_gather | solution.py:906
  126.0 2.7 fusion.61
  140.7 7.4 %collective-permute-done.24.f_ref = bf16[256,1024]{1,0:T(8,128)(2,1)S(1)} collective-permute-done((bf16[256,1024]{1,0:T(8,128)(2,1)S(1)}, bf16[256,1024]{1,0:T(8,128)(2,1)S(1)}, u32[]{:S(2)}, u32[]{:S(2)}) %collective-permute-start.24) | collective-permute-done | bytes 524320 | tf_op jit(solution)/shard_map/ppermute | solution.py:79
  149.0 3.2 %second_norm.1 = (bf16[256,1024]{1,0:T(8,128)(2,1)}, f32[256,1024]{1,0:T(8,128)S(1)}, bf16[256,1024]{1,0:T(8,128)(2,1)}, f32[8,1024]{1,0:T(8,128)}) custom-call(f32[256,1024]{1,0:T(8,128)S(1)} %get-tuple-element.187.h_ref, f32[256,1024]{1,0:T(8,128)S(1)} %fusion.67.k_ref, bf16[256,1024]{1,0:T(8,128)(2,1)} %copy-done.29, bf16[256,1024]{1,0:T(8,128)(2,1)} %copy-done.28, ...), custom_call_target="tpu_custom_call" | custom-call | flops 7864320 | bytes 7340032 | tf_op jit(solution)/shard_map/second_norm/pallas_call | solution.py:571
  157.3 3.4 %weight_grad.4.refs_4_ = f32[1024,1024]{1,0:T(8,128)S(1)} custom-call(s32[2]{0:T(128)S(1)} %pad_add_fusion.1.spot_ref, bf16[256,1024]{1,0:T(8,128)(2,1)} %copy-done.8, bf16[256,1024]{1,0:T(8,128)(2,1)} %copy-done.26, bf16[256,1024]{1,0:T(8,128)(2,1)} %get-tuple-element.200.refs_2_, bf16[256,1024]{1,0:T(8,128)(2,1)} %copy-done.10), custom_call_target="tpu_custom_call" | custom-call | flops 1073741824 | bytes 8388608 | tf_op jit(solution)/shard_map/weight_grad/pallas_call | solution.py:705
  163.4 3.5 %collective-permute-done.27.refs_2_ = bf16[256,1024]{1,0:T(8,128)(2,1)S(1)} collective-permute-done((bf16[256,1024]{1,0:T(8,128)(2,1)}, bf16[256,1024]{1,0:T(8,128)(2,1)S(1)}, u32[]{:S(2)}, u32[]{:S(2)}) %collective-permute-start.27) | collective-permute-done | bytes 524320 | tf_op jit(solution)/shard_map/ppermute | solution.py:79
  174.8 5.5 %weight_grad.5 = (f32[4,128,1024]{2,1,0:T(8,128)}, bf16[4,128,1024]{2,1,0:T(8,128)(2,1)}) custom-call(s32[2]{0:T(128)S(1)} %pad_add_fusion.1.spot_ref, bf16[256,1024]{1,0:T(8,128)(2,1)} %copy-done.25, bf16[256,1024]{1,0:T(8,128)(2,1)} %copy-done.22, bf16[256,1024]{1,0:T(8,128)(2,1)} %copy-done.6, bf16[256,1024]{1,0:T(8,128)(2,1)} %copy-done.9, ...), custom_call_target="tpu_custom_call" | custom-call | flops 1073741824 | bytes 8388608 | tf_op jit(solution)/shard_map/weight_grad/pallas_call | solution.py:705
  181.0 3.4 %weight_grad.6.refs_4_ = f32[1024,1024]{1,0:T(8,128)S(1)} custom-call(s32[2]{0:T(128)S(1)} %pad_add_fusion.1.spot_ref, bf16[256,1024]{1,0:T(8,128)(2,1)} %get-tuple-element.209.refs_0_, bf16[256,1024]{1,0:T(8,128)(2,1)} %copy-done.21, bf16[256,1024]{1,0:T(8,128)(2,1)} %copy-done.3, bf16[256,1024]{1,0:T(8,128)(2,1)} %copy-done.7), custom_call_target="tpu_custom_call" | custom-call | flops 1073741824 | bytes 8388608 | tf_op jit(solution)/shard_map/weight_grad/pallas_call | solution.py:705
  184.4 2.9 collective-permute-done.30.f_ref
  188.3 7.2 %first_norm_back.1 = (f32[256,1024]{1,0:T(8,128)}, bf16[256,1024]{1,0:T(8,128)(2,1)}, f32[8,1024]{1,0:T(8,128)}, bf16[256,256]{1,0:T(8,128)(2,1)}, bf16[256,256]...) custom-call(s32[2]{0:T(128)S(1)} %pad_add_fusion.1.spot_ref, ...), custom_call_target="tpu_custom_call" | custom-call | flops 536870912 | bytes 8388608 | tf_op jit(solution)/shard_map/first_norm_back/pallas_call | solution.py:637
  197.5 5.6 %weight_grad.7 = (f32[4,128,1024]{2,1,0:T(8,128)}, bf16[4,128,1024]{2,1,0:T(8,128)(2,1)}) custom-call(s32[2]{0:T(128)S(1)} %pad_add_fusion.1.spot_ref, bf16[256,1024]{1,0:T(8,128)(2,1)} %copy-done.18, bf16[256,1024]{1,0:T(8,128)(2,1)} %collective-permute-done.20.refs_1_, bf16[256,1024]{1,0:T(8,128)(2,1)} %copy-done.5, bf16[256,1024]{1,0:T(8,128)(2,1)} %copy-done.4, ...), custom_call_target="tpu_custom_call" | custom-call | flops 1073741824 | bytes 8388608 | tf_op jit(solution)/shard_map/weight_grad/pallas_call | solution.py:705
  203.7 2.5 collective-permute-done.32
  209.7 15.3 %attend_back.1 = (bf16[2,512,768]{2,1,0:T(8,128)(2,1)}, f32[2,8,512]{2,1,0:T(8,128)}, f32[2,8,128]{2,1,0:T(8,128)}, f32[4,128,768]{2,1,0:T(8,128)}, bf16[4,128,768]{2,1,0:T(8,128)(2,1)}) custom-call(s32[2]{0:T(128)S(1)} %pad_add_fusion.1.spot_ref, f32[4]{0:T(128)S(1)} %dynamic_slice.57.bias_ref, bf16[2,512,768]{2,1,0:T(8,128)(2,1)} %get-tuple-element.215.qkv_ref, ...), custom_call_target="tpu_custom_call" | custom-call | flops 4294967296 | bytes 10485760 | tf_op jit(solution)/shard_map/attend_back/pallas_call | solution.py:428
  225.1 7.8 %collective-permute-done.39 = bf16[4,128,1024]{2,1,0:T(8,128)(2,1)} collective-permute-done((bf16[4,128,1024]{2,1,0:T(8,128)(2,1)}, bf16[4,128,1024]{2,1,0:T(8,128)(2,1)}, u32[]{:S(2)}, u32[]{:S(2)}) %collective-permute-start.39) | collective-permute-done | bytes 1048608 | tf_op jit(solution)/shard_map/ppermute | solution.py:79
  232.9 2.6 add_convert_fusion
  238.0 7.0 %input_grad.1 = (f32[2,128,1024]{2,1,0:T(8,128)}, bf16[2,128,1024]{2,1,0:T(8,128)(2,1)}, f32[2,128,1024]{2,1,0:T(8,128)}, bf16[2,128,1024]{2,1,0:T(8,128)(2,1)}) custom-call(bf16[2,512,768]{2,1,0:T(8,128)(2,1)} %get-tuple-element.248.d_ref, bf16[1024,768]{1,0:T(8,128)(2,1)} %get-tuple-element.249.w_ref), custom_call_target="tpu_custom_call" | custom-call | flops 1610612736 | bytes 8388608 | tf_op jit(solution)/shard_map/input_grad/pallas_call | solution.py:748
  249.0 12.5 %collective-permute-done.38 = bf16[4,32,1024]{2,1,0:T(8,128)(2,1)S(1)} collective-permute-done((bf16[4,32,1024]{2,1,0:T(8,128)(2,1)S(1)}, bf16[4,32,1024]{2,1,0:T(8,128)(2,1)S(1)}, u32[]{:S(2)}, u32[]{:S(2)}) %collective-permute-start.38) | collective-permute-done | bytes 262176 | tf_op jit(solution)/shard_map/ppermute | solution.py:79
  261.6 2.5 add_convert_fusion.2
  272.1 3.5 %all-to-all-start = ((f32[32,1,416]{2,1,0:T(1,128)}), f32[32,1,416]{2,1,0:T(1,128)S(1)}, u32[]{:S(2)}, u32[]{:S(2)}) async-start(f32[32,1,416]{2,1,0:T(1,128)} %reshape.656), calls=%async_computation.3 | async-start | bytes 131072 | tf_op jit(solution)/shard_map/all_to_all | solution.py:234
  275.9 8.2 %all-to-all-done = f32[32,1,416]{2,1,0:T(1,128)S(1)} async-done(((f32[32,1,416]{2,1,0:T(1,128)}), f32[32,1,416]{2,1,0:T(1,128)S(1)}, u32[]{:S(2)}, u32[]{:S(2)}) %all-to-all-start) | async-done | bytes 53280 | tf_op jit(solution)/shard_map/all_to_all | solution.py:234
  293.9 2.7 collective-permute-done.47
  (363 shorter events, 97.1 us)
Async XLA Ops:
  7.2 118.8 %all-gather.3.cloned.1.call-start = ((), (), s32[]{:S(2)}) async-start(), calls=%async_computation.7 | async-start | bytes 4718592 | tf_op jit(solution)/shard_map/all_gather | solution.py:906
  14.3 29.1 %collective-permute-start.7 = (bf16[2,128,1024]{2,1,0:T(8,128)(2,1)S(1)}, bf16[2,128,1024]{2,1,0:T(8,128)(2,1)}, u32[]{:S(2)}, u32[]{:S(2)}) collective-permute-start(bf16[2,128,1024]{2,1,0:T(8,128)(2,1)S(1)} %copy-done.33), channel_id=1, source_target_pairs={{0,2},{1,3},{2,0},{3,1},{4,6},{5,7},{6,4},{7,5},{8,10},{9,11},{10,... | collective-permute-start | bytes 1572872 | tf_op jit(solution)/shard_map/ppermute | solution.py:79
  21.1 16.8 %collective-permute-start.3 = (bf16[1,528,256]{2,1,0:T(8,128)(2,1)S(1)}, bf16[1,528,256]{2,1,0:T(8,128)(2,1)S(1)}, u32[]{:S(2)}, u32[]{:S(2)}) collective-permute-start(bf16[1,528,256]{2,1,0:T(8,128)(2,1)S(1)} %fusion.59.refs_0_), channel_id=1, source_target_pairs={{0,16},{4,20},{8,24},{12,28},{16,0},{20,4},{24,8},{28,12},{1,17},{... | collective-permute-start | bytes 811016 | tf_op jit(solution)/shard_map/ppermute | solution.py:79
  24.0 13.9 %collective-permute-start.4 = (bf16[1,528,256]{2,1,0:T(8,128)(2,1)S(1)}, bf16[1,528,256]{2,1,0:T(8,128)(2,1)S(1)}, u32[]{:S(2)}, u32[]{:S(2)}) collective-permute-start(bf16[1,528,256]{2,1,0:T(8,128)(2,1)S(1)} %fusion.59.refs_0_), channel_id=1, source_target_pairs={{0,8},{4,12},{8,0},{12,4},{16,24},{20,28},{24,16},{28,20},{1,9},{5... | collective-permute-start | bytes 811016 | tf_op jit(solution)/shard_map/ppermute | solution.py:79
  25.6 17.8 %collective-permute-start.5 = (bf16[1,528,256]{2,1,0:T(8,128)(2,1)S(1)}, bf16[1,528,256]{2,1,0:T(8,128)(2,1)S(1)}, u32[]{:S(2)}, u32[]{:S(2)}) collective-permute-start(bf16[1,528,256]{2,1,0:T(8,128)(2,1)S(1)} %fusion.59.refs_0_), channel_id=1, source_target_pairs={{0,24},{4,28},{8,16},{12,20},{16,8},{20,12},{24,0},{28,4},{1,25},{... | collective-permute-start | bytes 811016 | tf_op jit(solution)/shard_map/ppermute | solution.py:79
  25.6 17.8 %collective-permute-start.6 = (bf16[1,528,256]{2,1,0:T(8,128)(2,1)S(1)}, bf16[1,528,256]{2,1,0:T(8,128)(2,1)}, u32[]{:S(2)}, u32[]{:S(2)}) collective-permute-start(bf16[1,528,256]{2,1,0:T(8,128)(2,1)S(1)} %fusion.59.refs_0_), channel_id=1, source_target_pairs={{0,4},{4,0},{8,12},{12,8},{16,20},{20,16},{24,28},{28,24},{1,5},{5... | collective-permute-start | bytes 811016 | tf_op jit(solution)/shard_map/ppermute | solution.py:79
  44.3 217.3 %reduce-scatter.6.cloned.1.call-start = ((), (), s32[]{:S(2)}) async-start(), calls=%async_computation.5 | async-start | bytes 1310720 | tf_op jit(solution)/shard_map/reduce_scatter | solution.py:810
  44.6 26.3 %collective-permute-start.11 = (bf16[2,128,1024]{2,1,0:T(8,128)(2,1)S(1)}, bf16[2,128,1024]{2,1,0:T(8,128)(2,1)}, u32[]{:S(2)}, u32[]{:S(2)}) collective-permute-start(bf16[2,128,1024]{2,1,0:T(8,128)(2,1)S(1)} %copy-done.33), channel_id=1, source_target_pairs={{0,1},{1,0},{2,3},{3,2},{4,5},{5,4},{6,7},{7,6},{8,9},{9,8},{10,11... | collective-permute-start | bytes 1572872 | tf_op jit(solution)/shard_map/ppermute | solution.py:79
  44.7 26.2 %collective-permute-start.12 = (bf16[2,128,1024]{2,1,0:T(8,128)(2,1)}, bf16[2,128,1024]{2,1,0:T(8,128)(2,1)}, u32[]{:S(2)}, u32[]{:S(2)}) collective-permute-start(bf16[2,128,1024]{2,1,0:T(8,128)(2,1)} %collective-permute-done.7.refs_10_.refs_6_), channel_id=1, source_target_pairs={{0,1},{1,0},{2,3},{3,2},{4,5},{5,4},{6,7},{7,6},{8,9},{9,8},{10,11... | collective-permute-start | bytes 1572872 | tf_op jit(solution)/shard_map/ppermute | solution.py:79
  45.2 9.3 %collective-permute-start.10 = (bf16[1,528,256]{2,1,0:T(8,128)(2,1)S(1)}, bf16[1,528,256]{2,1,0:T(8,128)(2,1)S(1)}, u32[]{:S(2)}, u32[]{:S(2)}) collective-permute-start(bf16[1,528,256]{2,1,0:T(8,128)(2,1)S(1)} %collective-permute-done.5.refs_3_), channel_id=1, source_target_pairs={{0,4},{4,0},{8,12},{12,8},{16,20},{20,16},{24,28},{28,24},{1,5},{5... | collective-permute-start | bytes 811016 | tf_op jit(solution)/shard_map/ppermute | solution.py:79
  46.7 13.8 %collective-permute-start.8 = (bf16[1,528,256]{2,1,0:T(8,128)(2,1)S(1)}, bf16[1,528,256]{2,1,0:T(8,128)(2,1)S(1)}, u32[]{:S(2)}, u32[]{:S(2)}) collective-permute-start(bf16[1,528,256]{2,1,0:T(8,128)(2,1)S(1)} %collective-permute-done.3.refs_1_), channel_id=1, source_target_pairs={{0,4},{4,0},{8,12},{12,8},{16,20},{20,16},{24,28},{28,24},{1,5},{5... | collective-permute-start | bytes 811016 | tf_op jit(solution)/shard_map/ppermute | solution.py:79
  47.2 23.6 %collective-permute-start.9 = (bf16[1,528,256]{2,1,0:T(8,128)(2,1)S(1)}, bf16[1,528,256]{2,1,0:T(8,128)(2,1)S(1)}, u32[]{:S(2)}, u32[]{:S(2)}) collective-permute-start(bf16[1,528,256]{2,1,0:T(8,128)(2,1)S(1)} %collective-permute-done.4.refs_2_), channel_id=1, source_target_pairs={{0,4},{4,0},{8,12},{12,8},{16,20},{20,16},{24,28},{28,24},{1,5},{5... | collective-permute-start | bytes 811016 | tf_op jit(solution)/shard_map/ppermute | solution.py:79
  72.7 12.6 %collective-permute-start.13 = (bf16[8,128,256]{2,1,0:T(8,128)(2,1)S(1)}, bf16[8,128,256]{2,1,0:T(8,128)(2,1)S(1)}, u32[]{:S(2)}, u32[]{:S(2)}) collective-permute-start(bf16[8,128,256]{2,1,0:T(8,128)(2,1)S(1)} %slice_dynamic-update-slice_fusion.refs_0_), channel_id=1, source_target_pairs={{0,2},{1,3},{2,0},{3,1},{4,6},{5,7},{6,4},{7,5},{8,10},{9,11},{10,... | collective-permute-start | bytes 1572872 | tf_op jit(solution)/shard_map/ppermute | solution.py:79
  99.2 14.8 %collective-permute-start.19 = (bf16[256,1024]{1,0:T(8,128)(2,1)}, bf16[256,1024]{1,0:T(8,128)(2,1)S(1)}, u32[]{:S(2)}, u32[]{:S(2)}) collective-permute-start(bf16[256,1024]{1,0:T(8,128)(2,1)} %get-tuple-element.209.refs_0_), channel_id=1, source_target_pairs={{0,2},{1,3},{2,0},{3,1},{4,6},{5,7},{6,4},{7,5},{8,10},{9,11},{10,... | collective-permute-start | bytes 1572872 | tf_op jit(solution)/shard_map/ppermute | solution.py:79
  134.0 14.0 %collective-permute-start.24 = (bf16[256,1024]{1,0:T(8,128)(2,1)S(1)}, bf16[256,1024]{1,0:T(8,128)(2,1)S(1)}, u32[]{:S(2)}, u32[]{:S(2)}) collective-permute-start(bf16[256,1024]{1,0:T(8,128)(2,1)S(1)} %add_convert_fusion.5), channel_id=1, source_target_pairs={{0,2},{1,3},{2,0},{3,1},{4,6},{5,7},{6,4},{7,5},{8,10},{9,11},{10,... | collective-permute-start | bytes 1572872 | tf_op jit(solution)/shard_map/ppermute | solution.py:79
  138.0 10.1 %collective-permute-start.23 = (bf16[256,1024]{1,0:T(8,128)(2,1)S(1)}, bf16[256,1024]{1,0:T(8,128)(2,1)S(1)}, u32[]{:S(2)}, u32[]{:S(2)}) collective-permute-start(bf16[256,1024]{1,0:T(8,128)(2,1)S(1)} %convolution_convert_fusion.2), channel_id=1, source_target_pairs={{0,1},{1,0},{2,3},{3,2},{4,5},{5,4},{6,7},{7,6},{8,9},{9,8},{10,11... | collective-permute-start | bytes 1572872 | tf_op jit(solution)/shard_map/ppermute | solution.py:79
  152.3 14.6 %collective-permute-start.27 = (bf16[256,1024]{1,0:T(8,128)(2,1)}, bf16[256,1024]{1,0:T(8,128)(2,1)S(1)}, u32[]{:S(2)}, u32[]{:S(2)}) collective-permute-start(bf16[256,1024]{1,0:T(8,128)(2,1)} %get-tuple-element.200.refs_2_), channel_id=1, source_target_pairs={{0,2},{1,3},{2,0},{3,1},{4,6},{5,7},{6,4},{7,5},{8,10},{9,11},{10,... | collective-permute-start | bytes 1572872 | tf_op jit(solution)/shard_map/ppermute | solution.py:79
  173.3 14.0 %collective-permute-start.30 = (bf16[256,1024]{1,0:T(8,128)(2,1)S(1)}, bf16[256,1024]{1,0:T(8,128)(2,1)S(1)}, u32[]{:S(2)}, u32[]{:S(2)}) collective-permute-start(bf16[256,1024]{1,0:T(8,128)(2,1)S(1)} %add_convert_fusion.4), channel_id=1, source_target_pairs={{0,2},{1,3},{2,0},{3,1},{4,6},{5,7},{6,4},{7,5},{8,10},{9,11},{10,... | collective-permute-start | bytes 1572872 | tf_op jit(solution)/shard_map/ppermute | solution.py:79
  174.8 12.5 %collective-permute-start.26 = (bf16[256,1024]{1,0:T(8,128)(2,1)S(1)}, bf16[256,1024]{1,0:T(8,128)(2,1)S(1)}, u32[]{:S(2)}, u32[]{:S(2)}) collective-permute-start(bf16[256,1024]{1,0:T(8,128)(2,1)S(1)} %convolution_convert_fusion.1), channel_id=1, source_target_pairs={{0,1},{1,0},{2,3},{3,2},{4,5},{5,4},{6,7},{7,6},{8,9},{9,8},{10,11... | collective-permute-start | bytes 1572872 | tf_op jit(solution)/shard_map/ppermute | solution.py:79
  180.4 25.9 %collective-permute-start.32 = (bf16[4,128,1024]{2,1,0:T(8,128)(2,1)}, bf16[4,128,1024]{2,1,0:T(8,128)(2,1)S(1)}, u32[]{:S(2)}, u32[]{:S(2)}) collective-permute-start(bf16[4,128,1024]{2,1,0:T(8,128)(2,1)} %get-tuple-element.208), channel_id=1, source_target_pairs={{0,4},{4,0},{8,12},{12,8},{16,20},{20,16},{24,28},{28,24},{1,5},{5... | collective-permute-start | bytes 3145736 | tf_op jit(solution)/shard_map/ppermute | solution.py:79
  195.5 10.8 %collective-permute-start.31 = (bf16[8,2,32,1024]{3,2,1,0:T(8,128)(2,1)}, bf16[8,2,32,1024]{3,2,1,0:T(8,128)(2,1)S(1)}, u32[]{:S(2)}, u32[]{:S(2)}) collective-permute-start(bf16[8,2,32,1024]{3,2,1,0:T(8,128)(2,1)} %get-tuple-element.218), channel_id=1, source_target_pairs={{0,1},{1,0},{2,3},{3,2},{4,5},{5,4},{6,7},{7,6},{8,9},{9,8},{10,11... | collective-permute-start | bytes 3145736 | tf_op jit(solution)/shard_map/ppermute | solution.py:79
  207.7 54.0 %reduce-scatter.4.cloned.1.call-start = ((), (), s32[]{:S(2)}) async-start(), calls=%async_computation.4 | async-start | bytes 1310720 | tf_op jit(solution)/shard_map/reduce_scatter | solution.py:810
  207.7 25.2 %collective-permute-start.39 = (bf16[4,128,1024]{2,1,0:T(8,128)(2,1)}, bf16[4,128,1024]{2,1,0:T(8,128)(2,1)}, u32[]{:S(2)}, u32[]{:S(2)}) collective-permute-start(bf16[4,128,1024]{2,1,0:T(8,128)(2,1)} %get-tuple-element.257), channel_id=1, source_target_pairs={{0,4},{4,0},{8,12},{12,8},{16,20},{20,16},{24,28},{28,24},{1,5},{5... | collective-permute-start | bytes 3145736 | tf_op jit(solution)/shard_map/ppermute | solution.py:79
  208.8 16.3 %collective-permute-start.36 = (bf16[8,1,32,1024]{3,2,1,0:T(8,128)(2,1)S(1)}, bf16[8,1,32,1024]{3,2,1,0:T(8,128)(2,1)S(1)}, u32[]{:S(2)}, u32[]{:S(2)}) collective-permute-start(bf16[8,1,32,1024]{3,2,1,0:T(8,128)(2,1)S(1)} %dynamic-slice_convert_fusion), channel_id=1, source_target_pairs={{0,2},{1,3},{2,0},{3,1},{4,6},{5,7},{6,4},{7,5},{8,10},{9,11},{10,... | collective-permute-start | bytes 1572872 | tf_op jit(solution)/shard_map/ppermute | solution.py:79
  235.5 50.8 %reduce-scatter.8.cloned.1.call-start = ((), (), s32[]{:S(2)}) async-start(), calls=%async_computation.6 | async-start | bytes 983040 | tf_op jit(solution)/shard_map/reduce_scatter | solution.py:810
  237.4 24.2 %collective-permute-start.37 = (bf16[4,128,768]{2,1,0:T(8,128)(2,1)}, bf16[4,128,768]{2,1,0:T(8,128)(2,1)S(1)}, u32[]{:S(2)}, u32[]{:S(2)}) collective-permute-start(bf16[4,128,768]{2,1,0:T(8,128)(2,1)} %get-tuple-element.247), channel_id=1, source_target_pairs={{0,4},{4,0},{8,12},{12,8},{16,20},{20,16},{24,28},{28,24},{1,5},{5... | collective-permute-start | bytes 2359304 | tf_op jit(solution)/shard_map/ppermute | solution.py:79
  245.0 16.6 %collective-permute-start.40 = (bf16[2,128,1024]{2,1,0:T(8,128)(2,1)}, bf16[2,128,1024]{2,1,0:T(8,128)(2,1)}, u32[]{:S(2)}, u32[]{:S(2)}) collective-permute-start(bf16[2,128,1024]{2,1,0:T(8,128)(2,1)} %get-tuple-element.258), channel_id=1, source_target_pairs={{0,1},{1,0},{2,3},{3,2},{4,5},{5,4},{6,7},{7,6},{8,9},{9,8},{10,11... | collective-permute-start | bytes 1572872 | tf_op jit(solution)/shard_map/ppermute | solution.py:79
  245.0 16.6 %collective-permute-start.41 = (bf16[2,128,1024]{2,1,0:T(8,128)(2,1)}, bf16[2,128,1024]{2,1,0:T(8,128)(2,1)}, u32[]{:S(2)}, u32[]{:S(2)}) collective-permute-start(bf16[2,128,1024]{2,1,0:T(8,128)(2,1)} %get-tuple-element.259), channel_id=1, source_target_pairs={{0,1},{1,0},{2,3},{3,2},{4,5},{5,4},{6,7},{7,6},{8,9},{9,8},{10,11... | collective-permute-start | bytes 1572872 | tf_op jit(solution)/shard_map/ppermute | solution.py:79
  245.7 15.9 %collective-permute-start.38 = (bf16[4,32,1024]{2,1,0:T(8,128)(2,1)S(1)}, bf16[4,32,1024]{2,1,0:T(8,128)(2,1)S(1)}, u32[]{:S(2)}, u32[]{:S(2)}) collective-permute-start(bf16[4,32,1024]{2,1,0:T(8,128)(2,1)S(1)} %fusion.18), channel_id=1, source_target_pairs={{0,4},{4,0},{8,12},{12,8},{16,20},{20,16},{24,28},{28,24},{1,5},{5... | collective-permute-start | bytes 786440 | tf_op jit(solution)/shard_map/ppermute | solution.py:79
  265.8 19.8 %collective-permute-start.43 = (bf16[2,32,1024]{2,1,0:T(8,128)(2,1)}, bf16[2,32,1024]{2,1,0:T(8,128)(2,1)S(1)}, u32[]{:S(2)}, u32[]{:S(2)}) collective-permute-start(bf16[2,32,1024]{2,1,0:T(8,128)(2,1)} %fusion.20), channel_id=1, source_target_pairs={{0,8},{4,12},{8,0},{12,4},{16,24},{20,28},{24,16},{28,20},{1,9},{5... | collective-permute-start | bytes 393224 | tf_op jit(solution)/shard_map/ppermute | solution.py:79
  270.3 15.2 %collective-permute-start.42 = (bf16[2,128,1024]{2,1,0:T(8,128)(2,1)}, bf16[2,128,1024]{2,1,0:T(8,128)(2,1)}, u32[]{:S(2)}, u32[]{:S(2)}) collective-permute-start(bf16[2,128,1024]{2,1,0:T(8,128)(2,1)} %add_convert_fusion.3), channel_id=1, source_target_pairs={{0,2},{1,3},{2,0},{3,1},{4,6},{5,7},{6,4},{7,5},{8,10},{9,11},{10,... | collective-permute-start | bytes 1572872 | tf_op jit(solution)/shard_map/ppermute | solution.py:79
  272.1 12.0 %all-to-all-start = ((f32[32,1,416]{2,1,0:T(1,128)}), f32[32,1,416]{2,1,0:T(1,128)S(1)}, u32[]{:S(2)}, u32[]{:S(2)}) async-start(f32[32,1,416]{2,1,0:T(1,128)} %reshape.656), calls=%async_computation.3 | async-start | bytes 131072 | tf_op jit(solution)/shard_map/all_to_all | solution.py:234
  (80 other events, 617.9 us)
Sparse Core Ops, SparseCore 0:
  44.5 81.4 all-gather.2
  207.8 24.4 reduce-scatter.5
  235.6 24.9 reduce-scatter.3
  264.3 21.9 reduce-scatter.7

commit v4 on v3

--- a/solution.py
+++ b/solution.py
@@ -240,8 +240,8 @@
     mine = (lanes // depth) == (h % (128 // depth))
     q = qkv[:, group * 128 : group * 128 + 128]
     k = qkv[:, span + group * 128 : span + group * 128 + 128]
-    raw = mul(jnp.where(mine, q, jnp.zeros_like(q)), k, NT)
-    return raw * 0.125 + jnp.where(same, bias, 0.0) + mask, mine, group
+    raw = mul(jnp.where(mine, q * 0.125, jnp.zeros_like(q)), k, NT)
+    return raw + jnp.where(same, mask + bias, mask), mine, group
 
 
 def attend(pieces, block, spot, own_bias, inputs, vectors, column, row, mask, heads, depth):
@@ -477,26 +477,23 @@
         return page_order(ordered, rels, spot[0]).reshape(width, width)
 
     def body(spot_ref, *refs):
-        out, held, sems = refs[-3:]
+        out = refs[-1]
         page, seq = spot_ref[0], spot_ref[1]
-        for copy in bring([(refs[r], held.at[r]) for r in range(seqs)], sems):
-            copy.wait()
         for r in range(seqs):
             for k, rel in enumerate(rels):
                 start = pl.multiple_of(((page ^ rel) * seqs + (seq ^ r)) * rows, rows)
                 for t in range(width // span):
-                    out[pl.ds(start, rows), t * span : (t + 1) * span] = held[r, k, t * rows : (t + 1) * rows, :]
+                    out[pl.ds(start, rows), t * span : (t + 1) * span] = refs[r][k, t * rows : (t + 1) * rows, :]
 
     return pl.pallas_call(
         body,
         out_shape=kept((width, width), LOW),
-        in_specs=[scalars()] + [remote()] * seqs,
+        in_specs=[scalars()] + [near()] * seqs,
         out_specs=near(),
-        scratch_shapes=[pltpu.VMEM((seqs,) + near_blocks[0].shape, LOW), pltpu.SemaphoreType.DMA((seqs,))],
         compiler_params=params(8),
         cost_estimate=cost(0, 4 * width * width),
         name="assemble_mix",
-    )(spot, *outside(near_blocks))
+    )(spot, *inside(near_blocks))
 
 
 def mix(spot, contexts, w_mix, inputs, vectors):
@@ -507,13 +504,13 @@
     def body(spot_ref, *refs):
         c_refs = refs[:seqs]
         w_ref, x_ref, vec_ref, wide_ref, low_ref, hat_ref, rstd_ref, c_all, x_here, sems = refs[seqs:]
-        copies = bring([(c_refs[r], c_all.at[r]) for r in range(seqs)] + [(x_ref, x_here)], sems)
+        copies = bring([(c_refs[0], c_all), (x_ref, x_here)], sems)
         for copy in copies:
             copy.wait()
         total = x_here[...].astype(WIDE) + vec_ref[2:3, :]
         for r in range(seqs):
             start = pl.multiple_of((spot_ref[1] ^ r) * span, span)
-            total = total + mul(c_all[r], w_ref[pl.ds(start, span), :])
+            total = total + mul((c_refs[r] if r else c_all)[...], w_ref[pl.ds(start, span), :])
         center = total - jnp.mean(total, axis=-1, keepdims=True)
         spread = jnp.mean(center * center, axis=-1, keepdims=True)
         rstd = lax.rsqrt(spread + 1e-05)
@@ -532,26 +529,26 @@
             shaped((flat, width), WIDE),
             shaped((flat, 128), WIDE),
         ],
-        in_specs=[scalars()] + [remote()] * seqs + [near(), remote(), near()],
+        in_specs=[scalars()] + [remote()] + [near()] * seqs + [remote(), near()],
         out_specs=[near()] * 4,
         scratch_shapes=[
-            pltpu.VMEM((seqs, flat, span), LOW),
+            pltpu.VMEM((flat, span), LOW),
             pltpu.VMEM((flat, width), LOW),
-            pltpu.SemaphoreType.DMA((seqs + 1,)),
+            pltpu.SemaphoreType.DMA((2,)),
         ],
         compiler_params=params(12),
         cost_estimate=cost(2 * flat * width * width, 8 << 20),
         name="mix",
-    )(spot, *outside(contexts), *inside([w_mix]), *outside([inputs]), vectors)
+    )(spot, *outside(contexts[:1]), *inside(contexts[1:]), *inside([w_mix]), *outside([inputs]), vectors)
 
 
 def second_norm(normed, keep, close, far, vectors, cotangent):
     flat, width = normed.shape
 
-    def body(h_ref, k_ref, n_ref, f_ref, vec_ref, cot_ref, out, wide, low, sums, n_here, f_here, c_here, sems):
-        for copy in bring([(n_ref, n_here), (f_ref, f_here), (cot_ref, c_here)], sems):
+    def body(h_ref, k_ref, n_ref, f_ref, vec_ref, cot_ref, out, wide, low, sums, c_here, sems):
+        for copy in bring([(cot_ref, c_here)], sems):
             copy.wait()
-        total = h_ref[...] + (k_ref[...] + n_here[...].astype(WIDE) + f_here[...].astype(WIDE)) + vec_ref[3:4, :]
+        total = h_ref[...] + (k_ref[...] + n_ref[...].astype(WIDE) + f_ref[...].astype(WIDE)) + vec_ref[3:4, :]
         center = total - jnp.mean(total, axis=-1, keepdims=True)
         spread = jnp.mean(center * center, axis=-1, keepdims=True)
         rstd = lax.rsqrt(spread + 1e-05)
@@ -572,17 +569,17 @@
         body,
         out_shape=[
             shaped((flat, width), LOW),
-            kept((flat, width), WIDE),
+            shaped((flat, width), WIDE),
             shaped((flat, width), LOW),
             shaped((8, width), WIDE),
         ],
-        in_specs=[near(), near(), remote(), remote(), near(), remote()],
+        in_specs=[near()] * 5 + [remote()],
         out_specs=[near()] * 4,
-        scratch_shapes=[pltpu.VMEM((flat, width), LOW)] * 3 + [pltpu.SemaphoreType.DMA((3,))],
+        scratch_shapes=[pltpu.VMEM((flat, width), LOW), pltpu.SemaphoreType.DMA((1,))],
         compiler_params=params(12),
         cost_estimate=cost(flat * width * 30, 7 << 20),
         name="second_norm",
-    )(*inside([normed]), keep, *outside([close, far]), vectors, *outside([cotangent]))
+    )(*inside([normed]), keep, *inside([close, far]), vectors, *outside([cotangent]))
 
 
 def first_norm_back(spot, grad_second, keep, close, far, hat, rstd, vectors, w_mix, contexts, pages):
@@ -596,15 +593,14 @@
         c_refs, (wide, low, sums) = refs[:seqs], refs[seqs : seqs + 3]
         outs, rest = refs[seqs + 3 : 2 * seqs + 3], refs[2 * seqs + 3 :]
         if with_mix:
-            mix_keep, mix_send, n_here, f_here, c_here, hat_here, full, sems = rest
+            mix_keep, mix_send, c_here, hat_here, d_here, n_here, f_here, full, sems = rest
         else:
-            n_here, f_here, c_here, hat_here, full, sems = rest
-        pairs = [(n_ref, n_here), (f_ref, f_here), (hat_ref, hat_here)]
+            c_here, hat_here, d_here, n_here, f_here, full, sems = rest
+        pairs = [(d_ref, d_here), (n_ref, n_here), (f_ref, f_here), (hat_ref, hat_here)]
         copies = bring(pairs + [(c_refs[r], c_here.at[r]) for r in range(seqs)], sems)
-        copies[0].wait()
-        copies[1].wait()
-        copies[2].wait()
-        grad = d_ref[...] + (k_ref[...] + n_here[...].astype(WIDE) + f_here[...].astype(WIDE))
+        for copy in copies[:4]:
+            copy.wait()
+        grad = d_here[...] + (k_ref[...] + n_here[...].astype(WIDE) + f_here[...].astype(WIDE))
         hat = hat_here[...]
         slope = grad * vec_ref[10:11, :]
         first = jnp.mean(slope, axis=-1, keepdims=True)
@@ -619,7 +615,7 @@
         sums[0:1, :] = jnp.sum(grad * hat, axis=0, keepdims=True)
         sums[1:2, :] = jnp.sum(grad, axis=0, keepdims=True)
         sums[2:3, :] = jnp.sum(result, axis=0, keepdims=True)
-        for copy in copies[3:]:
+        for copy in copies[4:]:
             copy.wait()
         if with_mix:
             for r in range(seqs):
@@ -643,21 +639,23 @@
         ]
         + [shaped((flat, span), LOW)] * seqs
         + ([shaped(mix_shape, WIDE), shaped(mix_shape, LOW)] if with_mix else []),
-        in_specs=[scalars(), near(), near(), remote(), remote(), remote()] + [near()] * 3 + [remote()] * seqs,
+        in_specs=[scalars(), remote(), near(), remote(), remote(), remote()] + [near()] * 3 + [remote()] * seqs,
         out_specs=[near()] * (3 + seqs + 2 * with_mix),
-        scratch_shapes=[pltpu.VMEM((flat, width), LOW)] * 2
-        + [
+        scratch_shapes=[
             pltpu.VMEM((seqs, flat, span), LOW),
             pltpu.VMEM((flat, width), WIDE),
+            pltpu.VMEM((flat, width), WIDE),
+            pltpu.VMEM((flat, width), LOW),
+            pltpu.VMEM((flat, width), LOW),
             pltpu.VMEM((width, width), WIDE),
-            pltpu.SemaphoreType.DMA((3 + seqs,)),
+            pltpu.SemaphoreType.DMA((4 + seqs,)),
         ],
         compiler_params=params(20),
         cost_estimate=cost(2 * flat * width * width, 8 << 20),
         name="first_norm_back",
     )(
         spot,
-        *inside([grad_second]),
+        *outside([grad_second]),
         keep,
         *outside([close, far]),
         *outside([hat, rstd]),
@@ -677,20 +675,24 @@
     def body(spot_ref, *refs):
         left, right = refs[:count], refs[count : 2 * count]
         base_ref = refs[2 * count] if base is not None else None
-        outs = refs[2 * count + (base is not None) : -4]
-        full, l_all, r_all, sems = refs[-4:]
+        outs = refs[2 * count + (base is not None) : -5]
+        full, l_all, r_all, base_here, sems = refs[-5:]
         page = spot_ref[0]
         pairs = []
         for k in range(count):
             pairs.append((left[k], l_all.at[pl.ds(k * tokens, tokens), :]))
             pairs.append((right[k], r_all.at[pl.ds(k * tokens, tokens), :]))
-        for copy in bring(pairs, sems):
+        copies = bring(pairs + ([(base_ref, base_here)] if base is not None else []), sems)
+        for copy in copies:
             copy.wait()
         for at in range(0, height, tile):
             value = mul(l_all[:, at : at + tile], r_all[...], TN)
             if base is not None:
-                value = value + base_ref[at : at + tile, :]
-            (full if split else outs[0])[at : at + tile, :] = value
+                value = value + base_here[at : at + tile, :]
+            if split:
+                full[at : at + tile, :] = value
+            else:
+                outs[0][at : at + tile, :] = value.astype(outs[0].dtype)
         if split:
             low = page % 2
             for k in range(pages // 2):
@@ -701,37 +703,117 @@
     if split:
         outs = [shaped((pages // 2, rows, width), WIDE), shaped((pages // 2, rows, width), LOW)]
     else:
-        outs = [kept((height, width), WIDE)]
+        outs = [shaped((height, width), WIDE if base is None else LOW)]
     return pl.pallas_call(
         body,
         out_shape=outs,
-        in_specs=[scalars()] + [remote()] * (2 * count) + [near()] * (base is not None),
+        in_specs=[scalars()] + [remote()] * (2 * count) + [remote()] * (base is not None),
         out_specs=[near()] * len(outs),
         scratch_shapes=[
             pltpu.VMEM((height, width) if split else (8, 128), WIDE),
             pltpu.VMEM((count * tokens, height), LOW),
             pltpu.VMEM((count * tokens, width), LOW),
-            pltpu.SemaphoreType.DMA((2 * count,)),
+            pltpu.VMEM((height, width) if base is not None else (8, 128), WIDE),
+            pltpu.SemaphoreType.DMA((2 * count + 1,)),
         ],
-        compiler_params=params(18),
+        compiler_params=params(22),
         cost_estimate=cost(2 * count * tokens * height * width, 8 << 20),
         name="weight_grad",
-    )(spot, *outside(lefts), *outside(rights), *(inside([base]) if base is not None else []))
-
-
-def widen(values):
-    def body(in_ref, out_ref):
-        out_ref[...] = in_ref[...].astype(WIDE)
-
+    )(spot, *outside(lefts), *outside(rights), *(outside([base]) if base is not None else []))
+
+
+def weight_grad_pair(first, base, second):
+    count = len(first)
+    tokens, height = first[0][0].shape
+    width = first[0][1].shape[1]
+    tile = 256 if height % 256 == 0 else height
+
+    def body(*refs):
+        base_ref, out, wide, l_one, r_one, l_two, r_two, base_here, sems = refs[4 * count :]
+        pairs = []
+        for k in range(count):
+            at = pl.ds(k * tokens, tokens)
+            pairs += [(refs[2 * k], l_one.at[at, :]), (refs[2 * k + 1], r_one.at[at, :])]
+        for k in range(count):
+            at = pl.ds(k * tokens, tokens)
+            pairs += [(refs[2 * count + 2 * k], l_two.at[at, :]), (refs[2 * count + 2 * k + 1], r_two.at[at, :])]
+        pairs.insert(2 * count, (base_ref, base_here))
+        copies = bring(pairs, sems)
+        for copy in copies[: 2 * count + 1]:
+            copy.wait()
+        for at in range(0, height, tile):
+            value = mul(l_one[:, at : at + tile], r_one[...], TN) + base_here[at : at + tile, :]
+            out[at : at + tile, :] = value.astype(LOW)
+        for copy in copies[2 * count + 1 :]:
+            copy.wait()
+        for at in range(0, height, tile):
+            wide[at : at + tile, :] = mul(l_two[:, at : at + tile], r_two[...], TN)
+
+    flat = [array for pair in first + second for array in pair]
     return pl.pallas_call(
         body,
-        out_shape=shaped(values.shape, WIDE),
-        in_specs=[near()],
+        out_shape=[shaped((height, width), LOW), shaped((height, width), WIDE)],
+        in_specs=[remote()] * (4 * count + 1),
+        out_specs=[near()] * 2,
+        scratch_shapes=[pltpu.VMEM((count * tokens, height), LOW), pltpu.VMEM((count * tokens, width), LOW)] * 2
+        + [pltpu.VMEM((height, width), WIDE), pltpu.SemaphoreType.DMA((4 * count + 1,))],
+        compiler_params=params(20),
+        cost_estimate=cost(4 * count * tokens * height * width, 12 << 20),
+        name="weight_grad_pair",
+    )(*outside(flat), *outside([base]))
+
+
+def pack_small(spot, sums_proj, cells_grad, sums_one, sums_two, hidden_sum, pages, seqs):
+    width = sums_one.shape[1]
+    span = sums_proj.shape[2] // 2
+    hidden = hidden_sum.shape[1] // pages
+    owners = pages * seqs
+    lanes = width // owners
+
+    def body(spot_ref, proj_ref, cell_ref, one_ref, two_ref, hid_ref, out, rows):
+        seq = spot_ref[1]
+        rows[...] = jnp.zeros_like(rows)
+        proj = jnp.sum(proj_ref[:, 0, :], axis=0, keepdims=True)
+        at = pl.multiple_of(seq * span, span)
+        rows[0:1, pl.ds(at, span)] = proj[:, :span]
+        rows[1:2, pl.ds(at, span)] = proj[:, span:]
+        for row, ref, k in ((2, one_ref, 2), (3, two_ref, 2), (4, one_ref, 1), (5, two_ref, 1), (10, one_ref, 0), (11, two_ref, 0)):
+            rows[row : row + 1, :] = ref[k : k + 1, :]
+        for p in range(pages):
+            first = p * seqs * hidden
+            at = pl.multiple_of(first % width + seq * hidden, hidden)
+            row = 6 + first // width
+            rows[row : row + 1, pl.ds(at, hidden)] = hid_ref[0:1, p * hidden : (p + 1) * hidden]
+        cell = jnp.sum(cell_ref[:, 0, :], axis=0, keepdims=True)
+        for o in range(owners):
+            out[o] = rows[:, o * lanes : (o + 1) * lanes]
+            out[o, 12:13, :] = cell[:, :lanes]
+
+    return pl.pallas_call(
+        body,
+        out_shape=shaped((owners, 16, lanes), WIDE),
+        in_specs=[scalars()] + [near()] * 5,
+        out_specs=near(),
+        scratch_shapes=[pltpu.VMEM((16, width), WIDE)],
+        compiler_params=params(6),
+        cost_estimate=cost(32 * width, 1 << 20),
+        name="pack_small",
+    )(spot, sums_proj, cells_grad, sums_one, sums_two, hidden_sum)
+
+
+def add_wide(keep, got):
+    def body(keep_ref, got_ref, out_ref):
+        out_ref[...] = keep_ref[...].astype(WIDE) + got_ref[...].astype(WIDE)
+
+    return pl.pallas_call(
+        body,
+        out_shape=shaped(keep.shape, WIDE),
+        in_specs=[near(), near()],
         out_specs=near(),
         compiler_params=params(4),
-        cost_estimate=cost(values.size, 6 * values.size),
-        name="widen",
-    )(values)
+        cost_estimate=cost(keep.size, 8 * keep.size),
+        name="add_wide",
+    )(keep, got)
 
 
 def input_grad(grad_proj, w_proj, seqs):
@@ -808,6 +890,12 @@
 
     def scatter_same(values):
         return lax.psum_scatter(values, "page", scatter_dimension=0, tiled=True, axis_index_groups=groups)
+
+    def split_low(values):
+        values = values.reshape(2, -1, values.shape[-1])
+        low = page_index % 2
+        mine = lax.dynamic_index_in_dim(values, low, 0, keepdims=False)
+        return mine, swap(lax.dynamic_index_in_dim(values, 1 - low, 0, keepdims=False), "page", pages, 1)
 
     def small_table(sums_proj, cells_grad):
         owners = pages * seqs
@@ -997,12 +1085,14 @@
     feed_back(second_all[seqs // 2 :])
     keep, close, far, ready = scatter_near(parts[0::2], parts[1::2])
     half = seqs // 2
-    down_keep, down_send = weight_grad(
-        spot, after(active[half:], ready), second_all[half:], pages, True, bases[0]
-    )
-    up_base = weight_grad(spot, after(normed_all[:half], down_send), expanded[:half], pages, False)[0]
-    far, up_base = fence(far, up_base)
-    down_got = scatter_first(down_send, pages)
+    if ff_here == width:
+        first = list(zip(after(active[half:], ready, close), second_all[half:]))
+        down_part, up_base = weight_grad_pair(first, bases[0], list(zip(normed_all[:half], expanded[:half])))
+    else:
+        down_part = weight_grad(spot, active[half:], second_all[half:], pages, False, bases[0])[0]
+        up_base = weight_grad(spot, normed_all[:half], expanded[:half], pages, False)[0]
+    far, down_part, up_base = fence(far, down_part, up_base)
+    down_sum = scatter_same(down_part)
     grad_first, first_low, sums_one, *mix_grads = first_norm_back(
         spot, grad_second, keep, close, far, hat, rstd, vectors, w_mix, contexts, pages
     )
@@ -1018,16 +1108,11 @@
         context = jnp.concatenate(reorder(contexts, seq_index), axis=1)
         grad_mix = jnp.einsum("tc,td->cd", context, first_low, preferred_element_type=WIDE)
         mix_keep, mix_parts = scatter_start(grad_mix.reshape(pages, seqs, rows, width), "seq", seqs, 1, 1)
-    mix_keep, mix_parts, down_got, down_keep, *others = fence(
-        mix_keep, mix_parts, down_got, down_keep, *grad_contexts, up_send
-    )
+    mix_keep, mix_parts, *others = fence(mix_keep, mix_parts, *grad_contexts, up_send)
     grad_contexts, up_send = others[:seqs], others[seqs]
-    down_half = halved(down_keep, down_got)
     up_got = scatter_first(up_send, pages)
     mix_total = (mix_keep + mix_parts.astype(WIDE)).reshape(pages, seqs // 2, rows, width)
     mix_keep, mix_parts = scatter_start(mix_total, "seq", seqs, 1, low_seq[1])
-    grad_contexts = after(grad_contexts, down_half)
-    grad_reduce = scatter_same(down_half)
     grad_contexts = [grad.reshape(page_count, row_count, span) for grad in grad_contexts]
     grad_proj, sums_proj, cells_grad, proj_keep, proj_send = attend_back(
         spot, own_bias, qkv, lse, grad_contexts, inputs, column, row, mask, heads_here, depth, pages
@@ -1036,43 +1121,51 @@
         grad_proj, sums_proj, cells_grad, proj_keep, proj_send, up_keep, mix_keep, mix_parts
     )
     proj_got = scatter_first(proj_send, pages)
-    grad_mix = (mix_keep + mix_parts.astype(WIDE)).reshape(pages, rows, width)
+    up_half = halved(up_keep, after(up_got, down_sum))
+    up_sum = scatter_same(up_half)
+    parts = input_grad(after(grad_proj, up_half), w_proj, seqs)
+    packed = lanes % 32 == 0 and span % 128 == 0 and ff_rows % 128 == 0 and width % (seqs * ff_rows) == 0
+    if packed:
+        hidden_sum = functools.reduce(jnp.add, totals)[None]
+        table = pack_small(
+            spot, *after((sums_proj, cells_grad), parts), sums_one, sums_two, hidden_sum, pages, seqs
+        )
+        small_sums = to_all(table)
+    else:
+        small_sums = small_table(*after((sums_proj, cells_grad), parts))
+    proj_got, proj_keep, mix_keep, mix_parts, small_sums, *parts = fence(
+        proj_got, proj_keep, mix_keep, mix_parts, small_sums, *parts
+    )
+    proj_half = halved(proj_keep, proj_got)
+    near_parts = [swap(part, "seq", seqs, 1) for part in after(parts[1::2], proj_half)]
+    keep, close, far = scatter_far(parts[0::2], near_parts)
+    proj_half = after(proj_half, up_sum)
+    proj_sum = scatter_same(proj_half)
+    grad_mix = add_wide(after(mix_keep, proj_half), mix_parts).reshape(pages, rows, width)
+    up_sum, down_sum = after((up_sum, down_sum), grad_mix)
     mix_keep, mix_parts = scatter_start(grad_mix, "page", pages, 0, 1)
-    grad_expand = scatter_same(halved(up_keep, up_got))
-    parts = input_grad(after(grad_proj, proj_send), w_proj, seqs)
-    near_parts = [swap(part, "seq", seqs, 1) for part in parts[1::2]]
-    proj_got, proj_keep, sums_proj, cells_grad, mix_keep, mix_parts, grad_expand, grad_reduce, *near_parts = fence(
-        proj_got, proj_keep, sums_proj, cells_grad, mix_keep, mix_parts, grad_expand, grad_reduce, *near_parts
-    )
-    proj_half = halved(proj_keep, proj_got)
-    grad_qkv = scatter_same(proj_half)
-    grad_reduce = widen(after(grad_reduce, proj_half))
-    near_parts, sums_proj, cells_grad, mix_keep, mix_parts = after(
-        (near_parts, sums_proj, cells_grad, mix_keep, mix_parts), grad_reduce
-    )
-    keep, close, far = scatter_far(parts[0::2], near_parts)
-    small_sums = small_table(sums_proj, cells_grad)
+    down_keep, down_got = split_low(down_sum)
+    up_rows = turn(up_sum.reshape(seqs, rows, ff_here), seqs, seq_index)
     mix_keep, mix_parts = scatter_start(mix_keep + mix_parts.astype(WIDE), "page", pages, 0, 2)
-    grad_qkv, far, small_sums, mix_keep, mix_parts = fence(grad_qkv, far, small_sums, mix_keep, mix_parts)
+    grad_reduce = down_keep.astype(WIDE) + down_got.astype(WIDE)
+    proj_sum, far, mix_keep, mix_parts, *up_rows = fence(proj_sum, far, mix_keep, mix_parts, *up_rows)
+    proj_rows = turn(proj_sum.reshape(seqs, rows, 3 * span), seqs, seq_index)
+    grad_expand = jnp.stack(reorder(up_rows, seq_index)).reshape(seqs, rows, pages, ff_rows).transpose(1, 2, 0, 3)
+    grad_expand = grad_expand.reshape(rows, seqs * ff_here).astype(WIDE)
     grad_mix = mix_keep + mix_parts.astype(WIDE)
     grad_mix = scatter_bits(grad_mix, "page", pages, 0, low_page[2:]).reshape(rows, width)
-    sent = jnp.concatenate(
-        [
-            grad_qkv.reshape(seqs, rows, 3, span).transpose(0, 2, 1, 3).reshape(seqs, 3 * rows, span),
-            grad_expand.reshape(seqs, -1, span),
-        ],
-        axis=1,
-    ).astype(LOW)
-    turned = jnp.stack(reorder(turn(sent, seqs, seq_index), seq_index))
-    grad_qkv = turned[:, : 3 * rows].reshape(seqs, 3, rows, span).transpose(2, 1, 0, 3)
+    grad_qkv = jnp.stack(reorder(proj_rows, seq_index)).reshape(seqs, rows, 3, span).transpose(1, 2, 0, 3)
     grad_qkv = grad_qkv.reshape(rows, 3 * width).astype(WIDE)
-    grad_expand = turned[:, 3 * rows :].reshape(seqs, rows, pages, ff_rows).transpose(1, 2, 0, 3)
-    grad_expand = grad_expand.reshape(rows, seqs * ff_here).astype(WIDE)
     grad_inputs = grad_first.reshape(page_count, row_count, width) + (
         keep + close.astype(WIDE) + far.astype(WIDE)
     )
 
     summed = jnp.sum(small_sums, axis=0)
+    if packed:
+        cell_total = small_sums[:, 12, :heads_here].reshape(pages, seqs, heads_here)
+        cell_total = jnp.sum(cell_total, axis=0).reshape(heads)
+    else:
+        cell_total = summed[12:].reshape(-1)[:heads]
     return (
         output.reshape(page_count, row_count, width),
         grad_inputs,
@@ -1082,7 +1175,7 @@
         grad_reduce,
         summed[:10],
         summed[10:12],
-        summed[12:].reshape(-1)[:heads],
+        cell_total,
     )
 
 

time: 311 us -> 309 us (level)
  blocking collectives: 0 us -> 11.9 us
  waiting for transfers between devices: 123 us -> 117 us
  local copies, waits for them, and re-layouts: 23.2 us -> 17.9 us
  other arithmetic: 21.4 us -> 18.2 us
    all_to_all x0 -> x1, blocking collectives: none -> 11.9 us  [to_all(): return lax.all_to_all(values, ('page', 'seq'), 0, 0)]
    pallas_call x2 -> x4, Pallas kernels: 4.06 us -> 13.3 us  [the longest x1 7.52 us: weight_grad_pair(): pl.pallas_call(body, out_shape=[shaped((height, width), LOW), shaped((hei...]
    all_to_all x1 -> x0, waiting for transfers between devices: 8.21 us -> none  [to_all(): return lax.all_to_all(values, ('page', 'seq'), 0, 0)]
    pallas_call x4 -> x2, Pallas kernels: 17.9 us -> 12.4 us  [weight_grad(): pl.pallas_call(body, out_shape=outs, in_specs=[scalars()] + [remote()] *...]
    all_to_all x1 -> x0, starting transfers between devices: 3.51 us -> none  [to_all(): return lax.all_to_all(values, ('page', 'seq'), 0, 0)]
    ppermute x48 -> x51, starting transfers between devices: 35.6 us -> 38.6 us  [swap(): return lax.ppermute(values, axis, [(i, i ^ mask) for i in range(count)])]
    unnamed x142 -> x121, local copies, waits for them, and re-layouts: 8.78 us -> 7.17 us
    convert_element_type x3 -> x2, other arithmetic: 6.44 us -> 5.35 us  [halved(): return (keep + got.astype(WIDE)).astype(LOW).reshape(-1, keep.shape[-1])]
  transfers between devices with their start and end apart: 53 -> 55, of which waited for: 26 -> 28; matrix products, arithmetic and copies ran while one was open for 11% -> 11% of each run, Pallas kernels for 21% -> 22%
where the time goes in v4:
time: 309 us; the launch traced here: 305 us
  waiting for transfers between devices  117 us (38%)
  Pallas kernels  70.2 us (23%)
  starting transfers between devices  39.2 us (13%)
  other arithmetic  18.2 us (6%)
  local copies, waits for them, and re-layouts  17.9 us (6%)
  matrix products  15.7 us (5%)
  between operations  15.5 us (5%)
  blocking collectives  11.9 us (4%)
    ppermute x51, waiting for transfers between devices, swap(): return lax.ppermute(values, axis, [(i, i ^ mask) for i in range(count)])  105 us
    ppermute x51, starting transfers between devices, swap(): return lax.ppermute(values, axis, [(i, i ^ mask) for i in range(count)])  38.6 us
    pallas_call x1, Pallas kernels, attend_back(): pl.pallas_call(body, grid=(page_count,), out_shape=[shaped((page_count, s...  15 us
    pallas_call x2, Pallas kernels, weight_grad(): pl.pallas_call(body, out_shape=outs, in_specs=[scalars()] + [remote()] *...  12.4 us
    all_to_all x1, blocking collectives, to_all(): return lax.all_to_all(values, ('page', 'seq'), 0, 0)  11.9 us
    pallas_call x1, Pallas kernels, attend(): pl.pallas_call(body, grid=(page_count,), out_shape=[shaped((page_count, s...  11 us
    all_gather x1, waiting for transfers between devices, local(): lax.all_gather(jnp.concatenate([part_up, w_down_low], axis=0), 'page', ax...  9.29 us
    pallas_call x1, Pallas kernels, weight_grad_pair(): pl.pallas_call(body, out_shape=[shaped((height, width), LOW), shaped((hei...  7.52 us
  transfers between devices with their start and end apart: 55, of which 28 were waited for; matrix products, arithmetic and copies ran while one was open for 11% of the time, Pallas kernels for 22%

profile of v4, /device:TPU:0, one launch (start us, length us, event | category | flops | bytes accessed | tf_op | source)
XLA Modules:
  0.0 305.2 jit_solution(9362016752714174682)
XLA Ops:
  11.1 2.5 collective-permute-start
  17.3 3.4 %collective-permute-done.1 = bf16[240,256]{1,0:T(8,128)(2,1)S(1)} collective-permute-done((bf16[240,256]{1,0:T(8,128)(2,1)S(1)}, bf16[240,256]{1,0:T(8,128)(2,1)S(1)}, u32[]{:S(2)}, u32[]{:S(2)}) %collective-permute-start.1) | collective-permute-done | bytes 122912 | tf_op jit(solution)/shard_map/ppermute | solution.py:79
  21.1 2.9 collective-permute-start.3
  27.6 10.2 %collective-permute-done.3.refs_1_ = bf16[1,528,256]{2,1,0:T(8,128)(2,1)S(1)} collective-permute-done((bf16[1,528,256]{2,1,0:T(8,128)(2,1)S(1)}, bf16[1,528,256]{2,1,0:T(8,128)(2,1)S(1)}, u32[]{:S(2)}, u32[]{:S(2)}) %collective-permute-start.3) | collective-permute-done | bytes 270368 | tf_op jit(solution)/shard_map/ppermute | solution.py:79
  37.9 5.6 %collective-permute-done.5.refs_3_ = bf16[1,528,256]{2,1,0:T(8,128)(2,1)S(1)} collective-permute-done((bf16[1,528,256]{2,1,0:T(8,128)(2,1)S(1)}, bf16[1,528,256]{2,1,0:T(8,128)(2,1)S(1)}, u32[]{:S(2)}, u32[]{:S(2)}) %collective-permute-start.5) | collective-permute-done | bytes 270368 | tf_op jit(solution)/shard_map/ppermute | solution.py:79
  49.0 5.4 %collective-permute-done.10.refs_7_ = bf16[1,528,256]{2,1,0:T(8,128)(2,1)S(1)} collective-permute-done((bf16[1,528,256]{2,1,0:T(8,128)(2,1)S(1)}, bf16[1,528,256]{2,1,0:T(8,128)(2,1)S(1)}, u32[]{:S(2)}, u32[]{:S(2)}) %collective-permute-start.10) | collective-permute-done | bytes 270368 | tf_op jit(solution)/shard_map/ppermute | solution.py:79
  54.5 5.9 %collective-permute-done.8.refs_5_ = bf16[1,528,256]{2,1,0:T(8,128)(2,1)S(1)} collective-permute-done((bf16[1,528,256]{2,1,0:T(8,128)(2,1)S(1)}, bf16[1,528,256]{2,1,0:T(8,128)(2,1)S(1)}, u32[]{:S(2)}, u32[]{:S(2)}) %collective-permute-start.8) | collective-permute-done | bytes 270368 | tf_op jit(solution)/shard_map/ppermute | solution.py:79
  60.4 10.4 %collective-permute-done.9.refs_6_ = bf16[1,528,256]{2,1,0:T(8,128)(2,1)S(1)} collective-permute-done((bf16[1,528,256]{2,1,0:T(8,128)(2,1)S(1)}, bf16[1,528,256]{2,1,0:T(8,128)(2,1)S(1)}, u32[]{:S(2)}, u32[]{:S(2)}) %collective-permute-start.9) | collective-permute-done | bytes 270368 | tf_op jit(solution)/shard_map/ppermute | solution.py:79
  74.4 11.0 %attend.1 = (bf16[2,512,768]{2,1,0:T(8,128)(2,1)}, f32[2,512,128]{2,1,0:T(8,128)}, bf16[1024,768]{1,0:T(8,128)(2,1)}, bf16[2,128,256]{2,1,0:T(8,128)(2,1)}, bf16...) custom-call(s32[2]{0:T(128)S(1)} %pad_add_fusion.1.spot_ref, ...), custom_call_target="tpu_custom_call" | custom-call | flops 2684354560 | bytes 10485760 | tf_op jit(solution)/shard_map/attend/pallas_call | solution.py:315
  89.1 3.5 %collective-permute-done.15.refs_2_ = bf16[256,256]{1,0:T(8,128)(2,1)S(1)} collective-permute-done((bf16[256,256]{1,0:T(8,128)(2,1)}, bf16[256,256]{1,0:T(8,128)(2,1)S(1)}, u32[]{:S(2)}, u32[]{:S(2)}) %collective-permute-start.15) | collective-permute-done | bytes 131104 | tf_op jit(solution)/shard_map/ppermute | solution.py:79
  94.5 3.9 %mix.1 = (f32[256,1024]{1,0:T(8,128)S(1)}, bf16[256,1024]{1,0:T(8,128)(2,1)}, f32[256,1024]{1,0:T(8,128)}, f32[256,128]{1,0:T(8,128)}) custom-call(s32[2]{0:T(128)S(1)} %pad_add_fusion.1.spot_ref, bf16[256,256]{1,0:T(8,128)(2,1)} %bitcast.261, bf16[256,256]{1,0:T(8,128)(2,1)S(1)} %collective-permute-done.14.refs_1_, ...), custom_call_target="tpu_custom_call" | custom-call | flops 536870912 | bytes 8388608 | tf_op jit(solution)/shard_map/mix/pallas_call | solution.py:524
  99.5 14.3 %collective-permute-done.19.refs_0_ = bf16[256,1024]{1,0:T(8,128)(2,1)S(1)} collective-permute-done((bf16[256,1024]{1,0:T(8,128)(2,1)}, bf16[256,1024]{1,0:T(8,128)(2,1)S(1)}, u32[]{:S(2)}, u32[]{:S(2)}) %collective-permute-start.19) | collective-permute-done | bytes 524320 | tf_op jit(solution)/shard_map/ppermute | solution.py:79
  116.7 9.3 %all-gather.3.cloned.1.call-done = bf16[2048,1024]{1,0:T(8,128)(2,1)} async-done(((bf16[256,1024]{1,0:T(8,128)(2,1)}), bf16[2048,1024]{1,0:T(8,128)(2,1)}) %all-gather.3.cloned.1.call-update) | async-done | bytes 4194320 | tf_op jit(solution)/shard_map/all_gather | solution.py:994
  125.9 2.7 fusion.59
  140.7 7.4 %collective-permute-done.24.f_ref = bf16[256,1024]{1,0:T(8,128)(2,1)S(1)} collective-permute-done((bf16[256,1024]{1,0:T(8,128)(2,1)S(1)}, bf16[256,1024]{1,0:T(8,128)(2,1)S(1)}, u32[]{:S(2)}, u32[]{:S(2)}) %collective-permute-start.24) | collective-permute-done | bytes 524320 | tf_op jit(solution)/shard_map/ppermute | solution.py:79
  148.1 3.3 %second_norm.1 = (bf16[256,1024]{1,0:T(8,128)(2,1)}, f32[256,1024]{1,0:T(8,128)}, bf16[256,1024]{1,0:T(8,128)(2,1)}, f32[8,1024]{1,0:T(8,128)}) custom-call(f32[256,1024]{1,0:T(8,128)S(1)} %get-tuple-element.184.h_ref, f32[256,1024]{1,0:T(8,128)S(1)} %fusion.64.k_ref, bf16[256,1024]{1,0:T(8,128)(2,1)S(1)} %collective-permute-done.23.n_ref, ...), custom_call_target="tpu_custom_call" | custom-call | flops 7864320 | bytes 7340032 | tf_op jit(solution)/shard_map/second_norm/pallas_call | solution.py:568
  156.5 5.4 %weight_grad.2.refs_8_ = f32[1024,1024]{1,0:T(8,128)} custom-call(s32[2]{0:T(128)S(1)} %pad_add_fusion.1.spot_ref, bf16[256,1024]{1,0:T(8,128)(2,1)} %copy-done.15, bf16[256,1024]{1,0:T(8,128)(2,1)} %copy-done.29, bf16[256,1024]{1,0:T(8,128)(2,1)} %get-tuple-element.197.refs_2_, bf16[256,1024]{1,0:T(8,128)(2,1)} %copy-done.17), custom_call_target="tpu_custom_call" | custom-call | flops 1073741824 | bytes 8388608 | tf_op jit(solution)/shard_map/weight_grad/pallas_call | solution.py:707
  173.8 7.5 %weight_grad_pair.1 = (bf16[1024,1024]{1,0:T(8,128)(2,1)}, f32[1024,1024]{1,0:T(8,128)}) custom-call(bf16[256,1024]{1,0:T(8,128)(2,1)} %copy-done.28, bf16[256,1024]{1,0:T(8,128)(2,1)} %copy-done.13, bf16[256,1024]{1,0:T(8,128)(2,1)} %copy-done.26, bf16[256,1024]{1,0:T(8,128)(2,1)} %copy-done.16, bf16[256,1024]{1,0:T(8,128)(2,1)} %get-tuple-element.188.refs_4_, ...), custom_call_target="tpu_custom_call" | custom-call | flops 2147483648 | bytes 12582912 | tf_op jit(solution)/shard_map/weight_grad_pair/pallas_call | solution.py:753
  181.3 5.0 %collective-permute-done.30.f_ref = bf16[256,1024]{1,0:T(8,128)(2,1)S(1)} collective-permute-done((bf16[256,1024]{1,0:T(8,128)(2,1)S(1)}, bf16[256,1024]{1,0:T(8,128)(2,1)S(1)}, u32[]{:S(2)}, u32[]{:S(2)}) %collective-permute-start.30) | collective-permute-done | bytes 524320 | tf_op jit(solution)/shard_map/ppermute | solution.py:79
  187.4 7.1 %first_norm_back.1 = (f32[256,1024]{1,0:T(8,128)}, bf16[256,1024]{1,0:T(8,128)(2,1)}, f32[8,1024]{1,0:T(8,128)}, bf16[256,256]{1,0:T(8,128)(2,1)}, bf16[256,256]...) custom-call(s32[2]{0:T(128)S(1)} %pad_add_fusion.1.spot_ref, ...), custom_call_target="tpu_custom_call" | custom-call | flops 536870912 | bytes 8388608 | tf_op jit(solution)/shard_map/first_norm_back/pallas_call | solution.py:633
  196.5 7.0 %weight_grad.3 = (f32[4,128,1024]{2,1,0:T(8,128)}, bf16[4,128,1024]{2,1,0:T(8,128)(2,1)}) custom-call(s32[2]{0:T(128)S(1)} %pad_add_fusion.1.spot_ref, bf16[256,1024]{1,0:T(8,128)(2,1)} %copy-done.23, bf16[256,1024]{1,0:T(8,128)(2,1)} %collective-permute-done.20.refs_1_, bf16[256,1024]{1,0:T(8,128)(2,1)} %copy-done.12, bf16[256,1024]{1,0:T(8,128)(2,1)} %copy-done.11, ...), custom_call_target="tpu_custom_call" | custom-call | flops 1073741824 | bytes 8388608 | tf_op jit(solution)/shard_map/weight_grad/pallas_call | solution.py:707
  207.0 15.0 %attend_back.1 = (bf16[2,512,768]{2,1,0:T(8,128)(2,1)}, f32[2,8,512]{2,1,0:T(8,128)}, f32[2,8,128]{2,1,0:T(8,128)}, f32[4,128,768]{2,1,0:T(8,128)}, bf16[4,128,768]{2,1,0:T(8,128)(2,1)}) custom-call(s32[2]{0:T(128)S(1)} %pad_add_fusion.1.spot_ref, f32[4]{0:T(128)S(1)} %dynamic_slice.77.bias_ref, bf16[2,512,768]{2,1,0:T(8,128)(2,1)} %get-tuple-element.211.qkv_ref, ...), custom_call_target="tpu_custom_call" | custom-call | flops 4294967296 | bytes 10485760 | tf_op jit(solution)/shard_map/attend_back/pallas_call | solution.py:428
  222.0 8.2 %collective-permute-done.37 = bf16[4,128,1024]{2,1,0:T(8,128)(2,1)} collective-permute-done((bf16[4,128,1024]{2,1,0:T(8,128)(2,1)}, bf16[4,128,1024]{2,1,0:T(8,128)(2,1)}, u32[]{:S(2)}, u32[]{:S(2)}) %collective-permute-start.37) | collective-permute-done | bytes 1048608 | tf_op jit(solution)/shard_map/ppermute | solution.py:79
  230.2 3.2 %add_convert_fusion = bf16[4,128,1024]{2,1,0:T(8,128)(2,1)} fusion(f32[4,128,1024]{2,1,0:T(8,128)} %get-tuple-element.242, bf16[4,128,1024]{2,1,0:T(8,128)(2,1)} %collective-permute-done.37), kind=kLoop, calls=%fused_computation | loop fusion | flops 1572864 | bytes 4194304 | tf_op jit(solution)/shard_map/convert_element_type | solution.py:889
  234.5 6.8 %input_grad.1 = (f32[2,128,1024]{2,1,0:T(8,128)}, bf16[2,128,1024]{2,1,0:T(8,128)(2,1)}, f32[2,128,1024]{2,1,0:T(8,128)}, bf16[2,128,1024]{2,1,0:T(8,128)(2,1)}) custom-call(bf16[2,512,768]{2,1,0:T(8,128)(2,1)} %get-tuple-element.246.d_ref, bf16[1024,768]{1,0:T(8,128)(2,1)} %get-tuple-element.247.w_ref), custom_call_target="tpu_custom_call" | custom-call | flops 1610612736 | bytes 8388608 | tf_op jit(solution)/shard_map/input_grad/pallas_call | solution.py:830
  243.8 11.9 %all_to_all.5 = f32[32,1,512]{2,1,0:T(1,128)S(1)} all-to-all(f32[32,1,512]{2,1,0:T(1,128)S(1)} %reshape.519), channel_id=1, replica_groups=mesh['page'=8,'seq'=4] {'page','seq'}, dimensions={0} | all-to-all | bytes 131072 | tf_op jit(solution)/shard_map/all_to_all | solution.py:234
  257.1 2.2 add_convert_fusion.1
  268.5 4.7 %collective-permute-done.41 = bf16[4,32,1024]{2,1,0:T(8,128)(2,1)S(1)} collective-permute-done((bf16[4,32,1024]{2,1,0:T(8,128)(2,1)S(1)}, bf16[4,32,1024]{2,1,0:T(8,128)(2,1)S(1)}, u32[]{:S(2)}, u32[]{:S(2)}) %collective-permute-start.41) | collective-permute-done | bytes 262176 | tf_op jit(solution)/shard_map/ppermute | solution.py:79
  273.3 4.2 %collective-permute-done.50 = bf16[128,1024]{1,0:T(8,128)(2,1)S(1)} collective-permute-done((bf16[128,1024]{1,0:T(8,128)(2,1)S(1)}, bf16[128,1024]{1,0:T(8,128)(2,1)S(1)}, u32[]{:S(2)}, u32[]{:S(2)}) %collective-permute-start.50) | collective-permute-done | bytes 262176 | tf_op jit(solution)/shard_map/ppermute | solution.py:79
  281.0 3.7 %collective-permute-done.42 = bf16[2,32,1024]{2,1,0:T(8,128)(2,1)S(1)} collective-permute-done((bf16[2,32,1024]{2,1,0:T(8,128)(2,1)S(1)}, bf16[2,32,1024]{2,1,0:T(8,128)(2,1)S(1)}, u32[]{:S(2)}, u32[]{:S(2)}) %collective-permute-start.42) | collective-permute-done | bytes 131104 | tf_op jit(solution)/shard_map/ppermute | solution.py:79
  284.7 2.2 reduce-scatter.8.cloned.1.call-done
  292.3 2.3 add_add_fusion
  (323 shorter events, 91.7 us)
Async XLA Ops:
  7.2 118.8 %all-gather.3.cloned.1.call-start = ((), (), s32[]{:S(2)}) async-start(), calls=%async_computation.7 | async-start | bytes 4718592 | tf_op jit(solution)/shard_map/all_gather | solution.py:994
  14.3 29.1 %collective-permute-start.7 = (bf16[2,128,1024]{2,1,0:T(8,128)(2,1)S(1)}, bf16[2,128,1024]{2,1,0:T(8,128)(2,1)}, u32[]{:S(2)}, u32[]{:S(2)}) collective-permute-start(bf16[2,128,1024]{2,1,0:T(8,128)(2,1)S(1)} %copy-done.32), channel_id=1, source_target_pairs={{0,2},{1,3},{2,0},{3,1},{4,6},{5,7},{6,4},{7,5},{8,10},{9,11},{10,... | collective-permute-start | bytes 1572872 | tf_op jit(solution)/shard_map/ppermute | solution.py:79
  21.1 16.8 %collective-permute-start.3 = (bf16[1,528,256]{2,1,0:T(8,128)(2,1)S(1)}, bf16[1,528,256]{2,1,0:T(8,128)(2,1)S(1)}, u32[]{:S(2)}, u32[]{:S(2)}) collective-permute-start(bf16[1,528,256]{2,1,0:T(8,128)(2,1)S(1)} %fusion.58.refs_0_), channel_id=1, source_target_pairs={{0,16},{4,20},{8,24},{12,28},{16,0},{20,4},{24,8},{28,12},{1,17},{... | collective-permute-start | bytes 811016 | tf_op jit(solution)/shard_map/ppermute | solution.py:79
  24.0 13.9 %collective-permute-start.4 = (bf16[1,528,256]{2,1,0:T(8,128)(2,1)S(1)}, bf16[1,528,256]{2,1,0:T(8,128)(2,1)S(1)}, u32[]{:S(2)}, u32[]{:S(2)}) collective-permute-start(bf16[1,528,256]{2,1,0:T(8,128)(2,1)S(1)} %fusion.58.refs_0_), channel_id=1, source_target_pairs={{0,8},{4,12},{8,0},{12,4},{16,24},{20,28},{24,16},{28,20},{1,9},{5... | collective-permute-start | bytes 811016 | tf_op jit(solution)/shard_map/ppermute | solution.py:79
  25.6 17.8 %collective-permute-start.5 = (bf16[1,528,256]{2,1,0:T(8,128)(2,1)S(1)}, bf16[1,528,256]{2,1,0:T(8,128)(2,1)S(1)}, u32[]{:S(2)}, u32[]{:S(2)}) collective-permute-start(bf16[1,528,256]{2,1,0:T(8,128)(2,1)S(1)} %fusion.58.refs_0_), channel_id=1, source_target_pairs={{0,24},{4,28},{8,16},{12,20},{16,8},{20,12},{24,0},{28,4},{1,25},{... | collective-permute-start | bytes 811016 | tf_op jit(solution)/shard_map/ppermute | solution.py:79
  25.6 17.8 %collective-permute-start.6 = (bf16[1,528,256]{2,1,0:T(8,128)(2,1)S(1)}, bf16[1,528,256]{2,1,0:T(8,128)(2,1)}, u32[]{:S(2)}, u32[]{:S(2)}) collective-permute-start(bf16[1,528,256]{2,1,0:T(8,128)(2,1)S(1)} %fusion.58.refs_0_), channel_id=1, source_target_pairs={{0,4},{4,0},{8,12},{12,8},{16,20},{20,16},{24,28},{28,24},{1,5},{5... | collective-permute-start | bytes 811016 | tf_op jit(solution)/shard_map/ppermute | solution.py:79
  44.3 185.9 %reduce-scatter.4.cloned.1.call-start = ((), (), s32[]{:S(2)}) async-start(), calls=%async_computation.4 | async-start | bytes 2621440 | tf_op jit(solution)/shard_map/reduce_scatter | solution.py:892
  44.6 26.3 %collective-permute-start.11 = (bf16[2,128,1024]{2,1,0:T(8,128)(2,1)S(1)}, bf16[2,128,1024]{2,1,0:T(8,128)(2,1)}, u32[]{:S(2)}, u32[]{:S(2)}) collective-permute-start(bf16[2,128,1024]{2,1,0:T(8,128)(2,1)S(1)} %copy-done.32), channel_id=1, source_target_pairs={{0,1},{1,0},{2,3},{3,2},{4,5},{5,4},{6,7},{7,6},{8,9},{9,8},{10,11... | collective-permute-start | bytes 1572872 | tf_op jit(solution)/shard_map/ppermute | solution.py:79
  44.6 26.2 %collective-permute-start.12 = (bf16[2,128,1024]{2,1,0:T(8,128)(2,1)}, bf16[2,128,1024]{2,1,0:T(8,128)(2,1)}, u32[]{:S(2)}, u32[]{:S(2)}) collective-permute-start(bf16[2,128,1024]{2,1,0:T(8,128)(2,1)} %collective-permute-done.7.refs_10_.refs_6_), channel_id=1, source_target_pairs={{0,1},{1,0},{2,3},{3,2},{4,5},{5,4},{6,7},{7,6},{8,9},{9,8},{10,11... | collective-permute-start | bytes 1572872 | tf_op jit(solution)/shard_map/ppermute | solution.py:79
  45.1 9.3 %collective-permute-start.10 = (bf16[1,528,256]{2,1,0:T(8,128)(2,1)S(1)}, bf16[1,528,256]{2,1,0:T(8,128)(2,1)S(1)}, u32[]{:S(2)}, u32[]{:S(2)}) collective-permute-start(bf16[1,528,256]{2,1,0:T(8,128)(2,1)S(1)} %collective-permute-done.5.refs_3_), channel_id=1, source_target_pairs={{0,4},{4,0},{8,12},{12,8},{16,20},{20,16},{24,28},{28,24},{1,5},{5... | collective-permute-start | bytes 811016 | tf_op jit(solution)/shard_map/ppermute | solution.py:79
  46.6 13.8 %collective-permute-start.8 = (bf16[1,528,256]{2,1,0:T(8,128)(2,1)S(1)}, bf16[1,528,256]{2,1,0:T(8,128)(2,1)S(1)}, u32[]{:S(2)}, u32[]{:S(2)}) collective-permute-start(bf16[1,528,256]{2,1,0:T(8,128)(2,1)S(1)} %collective-permute-done.3.refs_1_), channel_id=1, source_target_pairs={{0,4},{4,0},{8,12},{12,8},{16,20},{20,16},{24,28},{28,24},{1,5},{5... | collective-permute-start | bytes 811016 | tf_op jit(solution)/shard_map/ppermute | solution.py:79
  47.2 23.6 %collective-permute-start.9 = (bf16[1,528,256]{2,1,0:T(8,128)(2,1)S(1)}, bf16[1,528,256]{2,1,0:T(8,128)(2,1)S(1)}, u32[]{:S(2)}, u32[]{:S(2)}) collective-permute-start(bf16[1,528,256]{2,1,0:T(8,128)(2,1)S(1)} %collective-permute-done.4.refs_2_), channel_id=1, source_target_pairs={{0,4},{4,0},{8,12},{12,8},{16,20},{20,16},{24,28},{28,24},{1,5},{5... | collective-permute-start | bytes 811016 | tf_op jit(solution)/shard_map/ppermute | solution.py:79
  72.6 12.8 %collective-permute-start.13 = (bf16[8,128,256]{2,1,0:T(8,128)(2,1)S(1)}, bf16[8,128,256]{2,1,0:T(8,128)(2,1)S(1)}, u32[]{:S(2)}, u32[]{:S(2)}) collective-permute-start(bf16[8,128,256]{2,1,0:T(8,128)(2,1)S(1)} %slice_dynamic-update-slice_fusion.refs_0_), channel_id=1, source_target_pairs={{0,2},{1,3},{2,0},{3,1},{4,6},{5,7},{6,4},{7,5},{8,10},{9,11},{10,... | collective-permute-start | bytes 1572872 | tf_op jit(solution)/shard_map/ppermute | solution.py:79
  99.1 14.7 %collective-permute-start.19 = (bf16[256,1024]{1,0:T(8,128)(2,1)}, bf16[256,1024]{1,0:T(8,128)(2,1)S(1)}, u32[]{:S(2)}, u32[]{:S(2)}) collective-permute-start(bf16[256,1024]{1,0:T(8,128)(2,1)} %get-tuple-element.188.refs_4_), channel_id=1, source_target_pairs={{0,2},{1,3},{2,0},{3,1},{4,6},{5,7},{6,4},{7,5},{8,10},{9,11},{10,... | collective-permute-start | bytes 1572872 | tf_op jit(solution)/shard_map/ppermute | solution.py:79
  134.0 14.0 %collective-permute-start.24 = (bf16[256,1024]{1,0:T(8,128)(2,1)S(1)}, bf16[256,1024]{1,0:T(8,128)(2,1)S(1)}, u32[]{:S(2)}, u32[]{:S(2)}) collective-permute-start(bf16[256,1024]{1,0:T(8,128)(2,1)S(1)} %add_convert_fusion.4), channel_id=1, source_target_pairs={{0,2},{1,3},{2,0},{3,1},{4,6},{5,7},{6,4},{7,5},{8,10},{9,11},{10,... | collective-permute-start | bytes 1572872 | tf_op jit(solution)/shard_map/ppermute | solution.py:79
  138.1 10.0 %collective-permute-start.23 = (bf16[256,1024]{1,0:T(8,128)(2,1)S(1)}, bf16[256,1024]{1,0:T(8,128)(2,1)S(1)}, u32[]{:S(2)}, u32[]{:S(2)}) collective-permute-start(bf16[256,1024]{1,0:T(8,128)(2,1)S(1)} %convolution_convert_fusion.2), channel_id=1, source_target_pairs={{0,1},{1,0},{2,3},{3,2},{4,5},{5,4},{6,7},{7,6},{8,9},{9,8},{10,11... | collective-permute-start | bytes 1572872 | tf_op jit(solution)/shard_map/ppermute | solution.py:79
  151.5 14.6 %collective-permute-start.27 = (bf16[256,1024]{1,0:T(8,128)(2,1)}, bf16[256,1024]{1,0:T(8,128)(2,1)S(1)}, u32[]{:S(2)}, u32[]{:S(2)}) collective-permute-start(bf16[256,1024]{1,0:T(8,128)(2,1)} %get-tuple-element.197.refs_2_), channel_id=1, source_target_pairs={{0,2},{1,3},{2,0},{3,1},{4,6},{5,7},{6,4},{7,5},{8,10},{9,11},{10,... | collective-permute-start | bytes 1572872 | tf_op jit(solution)/shard_map/ppermute | solution.py:79
  172.3 14.0 %collective-permute-start.30 = (bf16[256,1024]{1,0:T(8,128)(2,1)S(1)}, bf16[256,1024]{1,0:T(8,128)(2,1)S(1)}, u32[]{:S(2)}, u32[]{:S(2)}) collective-permute-start(bf16[256,1024]{1,0:T(8,128)(2,1)S(1)} %add_convert_fusion.3), channel_id=1, source_target_pairs={{0,2},{1,3},{2,0},{3,1},{4,6},{5,7},{6,4},{7,5},{8,10},{9,11},{10,... | collective-permute-start | bytes 1572872 | tf_op jit(solution)/shard_map/ppermute | solution.py:79
  187.1 73.2 %reduce-scatter.6.cloned.1.call-start = ((), (), s32[]{:S(2)}) async-start(), calls=%async_computation.5 | async-start | bytes 1310720 | tf_op jit(solution)/shard_map/reduce_scatter | solution.py:892
  194.5 9.1 %collective-permute-start.31 = (bf16[8,2,32,1024]{3,2,1,0:T(8,128)(2,1)}, bf16[8,2,32,1024]{3,2,1,0:T(8,128)(2,1)S(1)}, u32[]{:S(2)}, u32[]{:S(2)}) collective-permute-start(bf16[8,2,32,1024]{3,2,1,0:T(8,128)(2,1)} %get-tuple-element.214), channel_id=1, source_target_pairs={{0,1},{1,0},{2,3},{3,2},{4,5},{5,4},{6,7},{7,6},{8,9},{9,8},{10,11... | collective-permute-start | bytes 3145736 | tf_op jit(solution)/shard_map/ppermute | solution.py:79
  194.6 9.0 %collective-permute-start.32 = (bf16[256,256]{1,0:T(8,128)(2,1)}, bf16[256,256]{1,0:T(8,128)(2,1)S(1)}, u32[]{:S(2)}, u32[]{:S(2)}) collective-permute-start(bf16[256,256]{1,0:T(8,128)(2,1)} %get-tuple-element.216), channel_id=1, source_target_pairs={{0,1},{1,0},{2,3},{3,2},{4,5},{5,4},{6,7},{7,6},{8,9},{9,8},{10,11... | collective-permute-start | bytes 393224 | tf_op jit(solution)/shard_map/ppermute | solution.py:79
  204.3 25.9 %collective-permute-start.37 = (bf16[4,128,1024]{2,1,0:T(8,128)(2,1)}, bf16[4,128,1024]{2,1,0:T(8,128)(2,1)}, u32[]{:S(2)}, u32[]{:S(2)}) collective-permute-start(bf16[4,128,1024]{2,1,0:T(8,128)(2,1)} %get-tuple-element.243), channel_id=1, source_target_pairs={{0,4},{4,0},{8,12},{12,8},{16,20},{20,16},{24,28},{28,24},{1,5},{5... | collective-permute-start | bytes 3145736 | tf_op jit(solution)/shard_map/ppermute | solution.py:79
  205.4 16.6 %collective-permute-start.35 = (bf16[8,1,32,1024]{3,2,1,0:T(8,128)(2,1)S(1)}, bf16[8,1,32,1024]{3,2,1,0:T(8,128)(2,1)S(1)}, u32[]{:S(2)}, u32[]{:S(2)}) collective-permute-start(bf16[8,1,32,1024]{3,2,1,0:T(8,128)(2,1)S(1)} %dynamic-slice_convert_fusion), channel_id=1, source_target_pairs={{0,2},{1,3},{2,0},{3,1},{4,6},{5,7},{6,4},{7,5},{8,10},{9,11},{10,... | collective-permute-start | bytes 1572872 | tf_op jit(solution)/shard_map/ppermute | solution.py:79
  233.4 53.4 %reduce-scatter.8.cloned.1.call-start = ((), (), s32[]{:S(2)}) async-start(), calls=%async_computation.6 | async-start | bytes 983040 | tf_op jit(solution)/shard_map/reduce_scatter | solution.py:892
  233.7 23.4 %collective-permute-start.36 = (bf16[4,128,768]{2,1,0:T(8,128)(2,1)}, bf16[4,128,768]{2,1,0:T(8,128)(2,1)}, u32[]{:S(2)}, u32[]{:S(2)}) collective-permute-start(bf16[4,128,768]{2,1,0:T(8,128)(2,1)} %get-tuple-element.235), channel_id=1, source_target_pairs={{0,4},{4,0},{8,12},{12,8},{16,20},{20,16},{24,28},{28,24},{1,5},{5... | collective-permute-start | bytes 2359304 | tf_op jit(solution)/shard_map/ppermute | solution.py:79
  263.9 9.3 %collective-permute-start.41 = (bf16[4,32,1024]{2,1,0:T(8,128)(2,1)S(1)}, bf16[4,32,1024]{2,1,0:T(8,128)(2,1)S(1)}, u32[]{:S(2)}, u32[]{:S(2)}) collective-permute-start(bf16[4,32,1024]{2,1,0:T(8,128)(2,1)S(1)} %fusion.18), channel_id=1, source_target_pairs={{0,4},{4,0},{8,12},{12,8},{16,20},{20,16},{24,28},{28,24},{1,5},{5... | collective-permute-start | bytes 786440 | tf_op jit(solution)/shard_map/ppermute | solution.py:79
  265.6 14.7 %collective-permute-start.40 = (bf16[2,128,1024]{2,1,0:T(8,128)(2,1)S(1)}, bf16[2,128,1024]{2,1,0:T(8,128)(2,1)S(1)}, u32[]{:S(2)}, u32[]{:S(2)}) collective-permute-start(bf16[2,128,1024]{2,1,0:T(8,128)(2,1)S(1)} %add_convert_fusion.2), channel_id=1, source_target_pairs={{0,2},{1,3},{2,0},{3,1},{4,6},{5,7},{6,4},{7,5},{8,10},{9,11},{10,... | collective-permute-start | bytes 1572872 | tf_op jit(solution)/shard_map/ppermute | solution.py:79
  267.1 10.3 %collective-permute-start.50 = (bf16[128,1024]{1,0:T(8,128)(2,1)S(1)}, bf16[128,1024]{1,0:T(8,128)(2,1)S(1)}, u32[]{:S(2)}, u32[]{:S(2)}) collective-permute-start(bf16[128,1024]{1,0:T(8,128)(2,1)S(1)} %dynamic-slice_bitcast_fusion), channel_id=1, source_target_pairs={{0,4},{4,0},{8,12},{12,8},{16,20},{20,16},{24,28},{28,24},{1,5},{5... | collective-permute-start | bytes 786440 | tf_op jit(solution)/shard_map/ppermute | solution.py:79
  267.8 12.5 %collective-permute-start.43 = (bf16[32,1024]{1,0:T(8,128)(2,1)S(1)}, bf16[32,1024]{1,0:T(8,128)(2,1)S(1)}, u32[]{:S(2)}, u32[]{:S(2)}) collective-permute-start(bf16[32,1024]{1,0:T(8,128)(2,1)S(1)} %get-tuple-element.306), channel_id=1, source_target_pairs={{0,1},{1,0},{2,3},{3,2},{4,5},{5,4},{6,7},{7,6},{8,9},{9,8},{10,11... | collective-permute-start | bytes 196616 | tf_op jit(solution)/shard_map/ppermute | solution.py:79
  267.9 13.1 %collective-permute-start.44 = (bf16[32,1024]{1,0:T(8,128)(2,1)S(1)}, bf16[32,1024]{1,0:T(8,128)(2,1)S(1)}, u32[]{:S(2)}, u32[]{:S(2)}) collective-permute-start(bf16[32,1024]{1,0:T(8,128)(2,1)S(1)} %get-tuple-element.305), channel_id=1, source_target_pairs={{0,2},{1,3},{2,0},{3,1},{4,6},{5,7},{6,4},{7,5},{8,10},{9,11},{10,... | collective-permute-start | bytes 196616 | tf_op jit(solution)/shard_map/ppermute | solution.py:79
  280.3 12.0 %collective-permute-start.38 = (bf16[2,128,1024]{2,1,0:T(8,128)(2,1)}, bf16[2,128,1024]{2,1,0:T(8,128)(2,1)}, u32[]{:S(2)}, u32[]{:S(2)}) collective-permute-start(bf16[2,128,1024]{2,1,0:T(8,128)(2,1)} %get-tuple-element.261), channel_id=1, source_target_pairs={{0,1},{1,0},{2,3},{3,2},{4,5},{5,4},{6,7},{7,6},{8,9},{9,8},{10,11... | collective-permute-start | bytes 1572872 | tf_op jit(solution)/shard_map/ppermute | solution.py:79
  288.5 9.3 %collective-permute-start.49 = (bf16[1,32,1024]{2,1,0:T(8,128)(2,1)S(1)}, bf16[1,32,1024]{2,1,0:T(8,128)(2,1)S(1)}, u32[]{:S(2)}, u32[]{:S(2)}) collective-permute-start(bf16[1,32,1024]{2,1,0:T(8,128)(2,1)S(1)} %dynamic-slice_convert_fusion.2), channel_id=1, source_target_pairs={{0,16},{4,20},{8,24},{12,28},{16,0},{20,4},{24,8},{28,12},{1,17},{... | collective-permute-start | bytes 196616 | tf_op jit(solution)/shard_map/ppermute | solution.py:79
  (73 other events, 625.9 us)
Sparse Core Ops, SparseCore 0:
  44.4 81.4 all-gather.2
  187.2 42.1 reduce-scatter.3
  233.5 26.7 reduce-scatter.5
  262.5 24.3 reduce-scatter.7

commit v5 on v4

--- a/solution.py
+++ b/solution.py
@@ -722,45 +722,66 @@
     )(spot, *outside(lefts), *outside(rights), *(outside([base]) if base is not None else []))
 
 
-def weight_grad_pair(first, base, second):
-    count = len(first)
+def weight_grad_pair(spot, first, base, second, pages):
+    one, two = len(first), len(second)
     tokens, height = first[0][0].shape
     width = first[0][1].shape[1]
+    rows = height // pages
     tile = 256 if height % 256 == 0 else height
-
-    def body(*refs):
-        base_ref, out, wide, l_one, r_one, l_two, r_two, base_here, sems = refs[4 * count :]
-        pairs = []
-        for k in range(count):
-            at = pl.ds(k * tokens, tokens)
-            pairs += [(refs[2 * k], l_one.at[at, :]), (refs[2 * k + 1], r_one.at[at, :])]
-        for k in range(count):
-            at = pl.ds(k * tokens, tokens)
-            pairs += [(refs[2 * count + 2 * k], l_two.at[at, :]), (refs[2 * count + 2 * k + 1], r_two.at[at, :])]
-        pairs.insert(2 * count, (base_ref, base_here))
+    cut = rows * 3 // 8
+    cuts = [(0, rows)] if cut % 16 else [(0, cut), (cut, rows)]
+    n_sent = len(cuts)
+
+    def body(spot_ref, *refs):
+        blocks = refs[: 2 * (one + two)]
+        base_ref, out, keep = refs[2 * (one + two) : 2 * (one + two) + 3]
+        sends = refs[2 * (one + two) + 3 : 2 * (one + two) + 3 + n_sent]
+        l_one, r_one, l_two, r_two, full, sems = refs[2 * (one + two) + 3 + n_sent :]
+        pairs = [(base_ref, full)]
+        for count, offset, left, right in ((one, 0, l_one, r_one), (two, 2 * one, l_two, r_two)):
+            for k in range(count):
+                at = pl.ds(k * tokens, tokens)
+                pairs += [(blocks[offset + 2 * k], left.at[at, :]), (blocks[offset + 2 * k + 1], right.at[at, :])]
         copies = bring(pairs, sems)
-        for copy in copies[: 2 * count + 1]:
+        for copy in copies[: 2 * one + 1]:
             copy.wait()
         for at in range(0, height, tile):
-            value = mul(l_one[:, at : at + tile], r_one[...], TN) + base_here[at : at + tile, :]
+            value = mul(l_one[:, at : at + tile], r_one[...], TN) + full[at : at + tile, :]
             out[at : at + tile, :] = value.astype(LOW)
-        for copy in copies[2 * count + 1 :]:
+        for copy in copies[2 * one + 1 :]:
             copy.wait()
         for at in range(0, height, tile):
-            wide[at : at + tile, :] = mul(l_two[:, at : at + tile], r_two[...], TN)
+            full[at : at + tile, :] = mul(l_two[:, at : at + tile], r_two[...], TN)
+        low = spot_ref[0] % 2
+        for k in range(pages // 2):
+            keep[k] = full[pl.ds(pl.multiple_of((2 * k + low) * rows, rows), rows), :]
+            start = pl.multiple_of((2 * k + 1 - low) * rows, rows)
+            value = full[pl.ds(start, rows), :].astype(LOW)
+            for ref, (begin, end) in zip(sends, cuts):
+                ref[k] = value[begin:end]
 
     flat = [array for pair in first + second for array in pair]
     return pl.pallas_call(
         body,
-        out_shape=[shaped((height, width), LOW), shaped((height, width), WIDE)],
-        in_specs=[remote()] * (4 * count + 1),
-        out_specs=[near()] * 2,
-        scratch_shapes=[pltpu.VMEM((count * tokens, height), LOW), pltpu.VMEM((count * tokens, width), LOW)] * 2
-        + [pltpu.VMEM((height, width), WIDE), pltpu.SemaphoreType.DMA((4 * count + 1,))],
-        compiler_params=params(20),
-        cost_estimate=cost(4 * count * tokens * height * width, 12 << 20),
+        out_shape=[
+            shaped((height, width), LOW),
+            shaped((pages // 2, rows, width), WIDE),
+        ]
+        + [shaped((pages // 2, end - begin, width), LOW) for begin, end in cuts],
+        in_specs=[scalars()] + [remote()] * (2 * (one + two) + 1),
+        out_specs=[near()] * (2 + n_sent),
+        scratch_shapes=[
+            pltpu.VMEM((one * tokens, height), LOW),
+            pltpu.VMEM((one * tokens, width), LOW),
+            pltpu.VMEM((two * tokens, height), LOW),
+            pltpu.VMEM((two * tokens, width), LOW),
+            pltpu.VMEM((height, width), WIDE),
+            pltpu.SemaphoreType.DMA((2 * (one + two) + 1,)),
+        ],
+        compiler_params=params(26),
+        cost_estimate=cost(2 * (one + two) * tokens * height * width, 16 << 20),
         name="weight_grad_pair",
-    )(*outside(flat), *outside([base]))
+    )(spot, *outside(flat), *outside([base]))
 
 
 def pack_small(spot, sums_proj, cells_grad, sums_one, sums_two, hidden_sum, pages, seqs):
@@ -1087,19 +1108,19 @@
     half = seqs // 2
     if ff_here == width:
         first = list(zip(after(active[half:], ready, close), second_all[half:]))
-        down_part, up_base = weight_grad_pair(first, bases[0], list(zip(normed_all[:half], expanded[:half])))
+        down_part, up_keep, *up_sends = weight_grad_pair(
+            spot, first, bases[0], list(zip(normed_all, expanded)), pages
+        )
     else:
         down_part = weight_grad(spot, active[half:], second_all[half:], pages, False, bases[0])[0]
-        up_base = weight_grad(spot, normed_all[:half], expanded[:half], pages, False)[0]
-    far, down_part, up_base = fence(far, down_part, up_base)
+        up_keep, *up_sends = weight_grad(spot, normed_all, expanded, pages, True)
+    far, down_part, up_keep, *up_sends = fence(far, down_part, up_keep, *up_sends)
     down_sum = scatter_same(down_part)
+    up_early = scatter_first(up_sends[0], pages)
     grad_first, first_low, sums_one, *mix_grads = first_norm_back(
         spot, grad_second, keep, close, far, hat, rstd, vectors, w_mix, contexts, pages
     )
     grad_contexts, mix_grads = mix_grads[:seqs], mix_grads[seqs:]
-    up_keep, up_send = weight_grad(
-        spot, after(normed_all[half:], first_low), expanded[half:], pages, True, up_base
-    )
     grad_contexts = exchange(grad_contexts)
     if mix_grads:
         mix_keep, mix_send = mix_grads
@@ -1108,9 +1129,8 @@
         context = jnp.concatenate(reorder(contexts, seq_index), axis=1)
         grad_mix = jnp.einsum("tc,td->cd", context, first_low, preferred_element_type=WIDE)
         mix_keep, mix_parts = scatter_start(grad_mix.reshape(pages, seqs, rows, width), "seq", seqs, 1, 1)
-    mix_keep, mix_parts, *others = fence(mix_keep, mix_parts, *grad_contexts, up_send)
-    grad_contexts, up_send = others[:seqs], others[seqs]
-    up_got = scatter_first(up_send, pages)
+    mix_keep, mix_parts, up_early, *grad_contexts = fence(mix_keep, mix_parts, up_early, *grad_contexts)
+    up_late = [scatter_first(send, pages) for send in up_sends[1:]]
     mix_total = (mix_keep + mix_parts.astype(WIDE)).reshape(pages, seqs // 2, rows, width)
     mix_keep, mix_parts = scatter_start(mix_total, "seq", seqs, 1, low_seq[1])
     grad_contexts = [grad.reshape(page_count, row_count, span) for grad in grad_contexts]
@@ -1121,7 +1141,10 @@
         grad_proj, sums_proj, cells_grad, proj_keep, proj_send, up_keep, mix_keep, mix_parts
     )
     proj_got = scatter_first(proj_send, pages)
-    up_half = halved(up_keep, after(up_got, down_sum))
+    cut = up_early.shape[1]
+    sums = [up_keep[:, :cut] + after(up_early, down_sum).astype(WIDE)]
+    sums += [up_keep[:, cut:] + part.astype(WIDE) for part in up_late]
+    up_half = jnp.concatenate([part.astype(LOW) for part in sums], axis=1).reshape(-1, ff_here)
     up_sum = scatter_same(up_half)
     parts = input_grad(after(grad_proj, up_half), w_proj, seqs)
     packed = lanes % 32 == 0 and span % 128 == 0 and ff_rows % 128 == 0 and width % (seqs * ff_rows) == 0

time: 309 us -> 309 us (level)
  Pallas kernels: 70.2 us -> 64.6 us
    pallas_call x2 -> x1, Pallas kernels: 12.4 us -> 5.4 us  [weight_grad(): pl.pallas_call(body, out_shape=outs, in_specs=[scalars()] + [remote()] *...]
    reduce_scatter x3, waiting for transfers between devices: 2.69 us -> 7.07 us  [scatter_same(): lax.psum_scatter(values, 'page', scatter_dimension=0, tiled=True, axis_in...]
    convert_element_type x2 -> x1, other arithmetic: 5.35 us -> 2.17 us  [halved(): return (keep + got.astype(WIDE)).astype(LOW).reshape(-1, keep.shape[-1])]
    ppermute x51 -> x52, waiting for transfers between devices: 105 us -> 102 us  [swap(): return lax.ppermute(values, axis, [(i, i ^ mask) for i in range(count)])]
    ppermute x51 -> x52, starting transfers between devices: 38.6 us -> 40.4 us  [swap(): return lax.ppermute(values, axis, [(i, i ^ mask) for i in range(count)])]
    unnamed x121 -> x123, local copies, waits for them, and re-layouts: 7.17 us -> 6.51 us
  transfers between devices with their start and end apart: 55 -> 56, of which waited for: 28 -> 32; matrix products, arithmetic and copies ran while one was open for 11% -> 11% of each run, Pallas kernels for 22% -> 20%
where the time goes in v5:
time: 309 us; the launch traced here: 304 us
  waiting for transfers between devices  120 us (39%)
  Pallas kernels  64.6 us (21%)
  starting transfers between devices  41 us (13%)
  other arithmetic  19 us (6%)
  local copies, waits for them, and re-layouts  17.2 us (6%)
  matrix products  15.9 us (5%)
  between operations  15.5 us (5%)
  blocking collectives  11.3 us (4%)
    ppermute x52, waiting for transfers between devices, swap(): return lax.ppermute(values, axis, [(i, i ^ mask) for i in range(count)])  102 us
    ppermute x52, starting transfers between devices, swap(): return lax.ppermute(values, axis, [(i, i ^ mask) for i in range(count)])  40.4 us
    pallas_call x1, Pallas kernels, attend_back(): pl.pallas_call(body, grid=(page_count,), out_shape=[shaped((page_count, s...  15 us
    all_to_all x1, blocking collectives, to_all(): return lax.all_to_all(values, ('page', 'seq'), 0, 0)  11.3 us
    all_gather x1, waiting for transfers between devices, local(): lax.all_gather(jnp.concatenate([part_up, w_down_low], axis=0), 'page', ax...  10.7 us
    pallas_call x1, Pallas kernels, attend(): pl.pallas_call(body, grid=(page_count,), out_shape=[shaped((page_count, s...  10.5 us
    pallas_call x1, Pallas kernels, weight_grad_pair(): pl.pallas_call(body, out_shape=[shaped((height, width), LOW), shaped((pag...  9.48 us
    reduce_scatter x3, waiting for transfers between devices, scatter_same(): lax.psum_scatter(values, 'page', scatter_dimension=0, tiled=True, axis_in...  7.07 us
  transfers between devices with their start and end apart: 56, of which 32 were waited for; matrix products, arithmetic and copies ran while one was open for 11% of the time, Pallas kernels for 20%

profile of v5, /device:TPU:0, one launch (start us, length us, event | category | flops | bytes accessed | tf_op | source)
XLA Modules:
  0.0 304.4 jit_solution(1971270577946772693)
XLA Ops:
  11.1 2.5 collective-permute-start
  17.3 3.4 %collective-permute-done.1 = bf16[240,256]{1,0:T(8,128)(2,1)S(1)} collective-permute-done((bf16[240,256]{1,0:T(8,128)(2,1)S(1)}, bf16[240,256]{1,0:T(8,128)(2,1)S(1)}, u32[]{:S(2)}, u32[]{:S(2)}) %collective-permute-start.1) | collective-permute-done | bytes 122912 | tf_op jit(solution)/shard_map/ppermute | solution.py:79
  21.1 2.9 collective-permute-start.3
  27.6 10.2 %collective-permute-done.3.refs_1_ = bf16[1,528,256]{2,1,0:T(8,128)(2,1)S(1)} collective-permute-done((bf16[1,528,256]{2,1,0:T(8,128)(2,1)S(1)}, bf16[1,528,256]{2,1,0:T(8,128)(2,1)S(1)}, u32[]{:S(2)}, u32[]{:S(2)}) %collective-permute-start.3) | collective-permute-done | bytes 270368 | tf_op jit(solution)/shard_map/ppermute | solution.py:79
  37.9 5.6 %collective-permute-done.5.refs_3_ = bf16[1,528,256]{2,1,0:T(8,128)(2,1)S(1)} collective-permute-done((bf16[1,528,256]{2,1,0:T(8,128)(2,1)S(1)}, bf16[1,528,256]{2,1,0:T(8,128)(2,1)S(1)}, u32[]{:S(2)}, u32[]{:S(2)}) %collective-permute-start.5) | collective-permute-done | bytes 270368 | tf_op jit(solution)/shard_map/ppermute | solution.py:79
  49.0 5.4 %collective-permute-done.10.refs_7_ = bf16[1,528,256]{2,1,0:T(8,128)(2,1)S(1)} collective-permute-done((bf16[1,528,256]{2,1,0:T(8,128)(2,1)S(1)}, bf16[1,528,256]{2,1,0:T(8,128)(2,1)S(1)}, u32[]{:S(2)}, u32[]{:S(2)}) %collective-permute-start.10) | collective-permute-done | bytes 270368 | tf_op jit(solution)/shard_map/ppermute | solution.py:79
  54.5 5.9 %collective-permute-done.8.refs_5_ = bf16[1,528,256]{2,1,0:T(8,128)(2,1)S(1)} collective-permute-done((bf16[1,528,256]{2,1,0:T(8,128)(2,1)S(1)}, bf16[1,528,256]{2,1,0:T(8,128)(2,1)S(1)}, u32[]{:S(2)}, u32[]{:S(2)}) %collective-permute-start.8) | collective-permute-done | bytes 270368 | tf_op jit(solution)/shard_map/ppermute | solution.py:79
  60.4 10.4 %collective-permute-done.9.refs_6_ = bf16[1,528,256]{2,1,0:T(8,128)(2,1)S(1)} collective-permute-done((bf16[1,528,256]{2,1,0:T(8,128)(2,1)S(1)}, bf16[1,528,256]{2,1,0:T(8,128)(2,1)S(1)}, u32[]{:S(2)}, u32[]{:S(2)}) %collective-permute-start.9) | collective-permute-done | bytes 270368 | tf_op jit(solution)/shard_map/ppermute | solution.py:79
  74.4 10.5 %attend.1 = (bf16[2,512,768]{2,1,0:T(8,128)(2,1)}, f32[2,512,128]{2,1,0:T(8,128)}, bf16[1024,768]{1,0:T(8,128)(2,1)}, bf16[2,128,256]{2,1,0:T(8,128)(2,1)}, bf16...) custom-call(s32[2]{0:T(128)S(1)} %pad_add_fusion.1.spot_ref, ...), custom_call_target="tpu_custom_call" | custom-call | flops 2684354560 | bytes 10485760 | tf_op jit(solution)/shard_map/attend/pallas_call | solution.py:315
  88.6 3.5 %collective-permute-done.15.refs_2_ = bf16[256,256]{1,0:T(8,128)(2,1)S(1)} collective-permute-done((bf16[256,256]{1,0:T(8,128)(2,1)}, bf16[256,256]{1,0:T(8,128)(2,1)S(1)}, u32[]{:S(2)}, u32[]{:S(2)}) %collective-permute-start.15) | collective-permute-done | bytes 131104 | tf_op jit(solution)/shard_map/ppermute | solution.py:79
  94.0 3.9 %mix.1 = (f32[256,1024]{1,0:T(8,128)S(1)}, bf16[256,1024]{1,0:T(8,128)(2,1)}, f32[256,1024]{1,0:T(8,128)}, f32[256,128]{1,0:T(8,128)}) custom-call(s32[2]{0:T(128)S(1)} %pad_add_fusion.1.spot_ref, bf16[256,256]{1,0:T(8,128)(2,1)} %bitcast.261, bf16[256,256]{1,0:T(8,128)(2,1)S(1)} %collective-permute-done.14.refs_1_, ...), custom_call_target="tpu_custom_call" | custom-call | flops 536870912 | bytes 8388608 | tf_op jit(solution)/shard_map/mix/pallas_call | solution.py:524
  99.6 13.7 %collective-permute-done.19.refs_8_ = bf16[256,1024]{1,0:T(8,128)(2,1)S(1)} collective-permute-done((bf16[256,1024]{1,0:T(8,128)(2,1)}, bf16[256,1024]{1,0:T(8,128)(2,1)S(1)}, u32[]{:S(2)}, u32[]{:S(2)}) %collective-permute-start.19) | collective-permute-done | bytes 524320 | tf_op jit(solution)/shard_map/ppermute | solution.py:79
  115.3 10.7 %all-gather.3.cloned.1.call-done = bf16[2048,1024]{1,0:T(8,128)(2,1)} async-done(((bf16[256,1024]{1,0:T(8,128)(2,1)}), bf16[2048,1024]{1,0:T(8,128)(2,1)}) %all-gather.3.cloned.1.call-update) | async-done | bytes 4194320 | tf_op jit(solution)/shard_map/all_gather | solution.py:1015
  126.0 2.7 fusion.59
  140.8 7.3 %collective-permute-done.24.f_ref = bf16[256,1024]{1,0:T(8,128)(2,1)S(1)} collective-permute-done((bf16[256,1024]{1,0:T(8,128)(2,1)S(1)}, bf16[256,1024]{1,0:T(8,128)(2,1)S(1)}, u32[]{:S(2)}, u32[]{:S(2)}) %collective-permute-start.24) | collective-permute-done | bytes 524320 | tf_op jit(solution)/shard_map/ppermute | solution.py:79
  148.1 3.3 %second_norm.1 = (bf16[256,1024]{1,0:T(8,128)(2,1)}, f32[256,1024]{1,0:T(8,128)}, bf16[256,1024]{1,0:T(8,128)(2,1)}, f32[8,1024]{1,0:T(8,128)}) custom-call(f32[256,1024]{1,0:T(8,128)S(1)} %get-tuple-element.184.h_ref, f32[256,1024]{1,0:T(8,128)S(1)} %fusion.64.k_ref, bf16[256,1024]{1,0:T(8,128)(2,1)S(1)} %collective-permute-done.23.n_ref, ...), custom_call_target="tpu_custom_call" | custom-call | flops 7864320 | bytes 7340032 | tf_op jit(solution)/shard_map/second_norm/pallas_call | solution.py:568
  156.5 5.4 %weight_grad.1.refs_12_ = f32[1024,1024]{1,0:T(8,128)} custom-call(s32[2]{0:T(128)S(1)} %pad_add_fusion.1.spot_ref, bf16[256,1024]{1,0:T(8,128)(2,1)} %copy-done.11, bf16[256,1024]{1,0:T(8,128)(2,1)} %copy-done.20, bf16[256,1024]{1,0:T(8,128)(2,1)} %get-tuple-element.197.refs_2_, bf16[256,1024]{1,0:T(8,128)(2,1)} %copy-done.12), custom_call_target="tpu_custom_call" | custom-call | flops 1073741824 | bytes 8388608 | tf_op jit(solution)/shard_map/weight_grad/pallas_call | solution.py:707
  174.0 9.5 %weight_grad_pair.1 = (bf16[1024,1024]{1,0:T(8,128)(2,1)}, f32[4,128,1024]{2,1,0:T(8,128)}, bf16[4,48,1024]{2,1,0:T(8,128)(2,1)}, bf16[4,80,1024]{2,1,0:T(8,128)(2,1)}) custom-call(s32[2]{0:T(128)S(1)} %pad_add_fusion.1.spot_ref, bf16[256,1024]{1,0:T(8,128)(2,1)} %copy-done.50, bf16[256,1024]{1,0:T(8,128)(2,1)} %copy-done.18, bf16[256,1024]{1,0:T(8,128)(2,1)} %copy-done.49, ...), custom_call_target="tpu_custom_call" | custom-call | flops 3221225472 | bytes 16777216 | tf_op jit(solution)/shard_map/weight_grad_pair/pallas_call | solution.py:764
  183.5 3.0 collective-permute-done.30.f_ref
  187.7 7.0 %first_norm_back.1 = (f32[256,1024]{1,0:T(8,128)}, bf16[256,1024]{1,0:T(8,128)(2,1)}, f32[8,1024]{1,0:T(8,128)}, bf16[256,256]{1,0:T(8,128)(2,1)}, bf16[256,256]...) custom-call(s32[2]{0:T(128)S(1)} %pad_add_fusion.1.spot_ref, ...), custom_call_target="tpu_custom_call" | custom-call | flops 536870912 | bytes 8388608 | tf_op jit(solution)/shard_map/first_norm_back/pallas_call | solution.py:633
  198.8 3.4 %collective-permute-done.34 = bf16[256,256]{1,0:T(8,128)(2,1)S(1)} collective-permute-done((bf16[256,256]{1,0:T(8,128)(2,1)}, bf16[256,256]{1,0:T(8,128)(2,1)S(1)}, u32[]{:S(2)}, u32[]{:S(2)}) %collective-permute-start.34) | collective-permute-done | bytes 131104 | tf_op jit(solution)/shard_map/ppermute | solution.py:79
  203.8 3.2 %collective-permute-done.32 = bf16[4,48,1024]{2,1,0:T(8,128)(2,1)S(1)} collective-permute-done((bf16[4,48,1024]{2,1,0:T(8,128)(2,1)}, bf16[4,48,1024]{2,1,0:T(8,128)(2,1)S(1)}, u32[]{:S(2)}, u32[]{:S(2)}) %collective-permute-start.32) | collective-permute-done | bytes 393248 | tf_op jit(solution)/shard_map/ppermute | solution.py:79
  210.7 15.0 %attend_back.1 = (bf16[2,512,768]{2,1,0:T(8,128)(2,1)}, f32[2,8,512]{2,1,0:T(8,128)}, f32[2,8,128]{2,1,0:T(8,128)}, f32[4,128,768]{2,1,0:T(8,128)}, bf16[4,128,768]{2,1,0:T(8,128)(2,1)}) custom-call(s32[2]{0:T(128)S(1)} %pad_add_fusion.1.spot_ref, f32[4]{0:T(128)S(1)} %dynamic_slice.77.bias_ref, bf16[2,512,768]{2,1,0:T(8,128)(2,1)} %get-tuple-element.213.qkv_ref, ...), custom_call_target="tpu_custom_call" | custom-call | flops 4294967296 | bytes 10485760 | tf_op jit(solution)/shard_map/attend_back/pallas_call | solution.py:428
  225.9 3.6 %reduce-scatter.4.cloned.1.call-done = bf16[256,1024]{1,0:T(8,128)(2,1)} async-done(((bf16[1024,1024]{1,0:T(8,128)(2,1)}), bf16[256,1024]{1,0:T(8,128)(2,1)}) %reduce-scatter.4.cloned.1.call-update) | async-done | bytes 524304 | tf_op jit(solution)/shard_map/reduce_scatter | solution.py:913
  233.5 6.8 %input_grad.1 = (f32[2,128,1024]{2,1,0:T(8,128)}, bf16[2,128,1024]{2,1,0:T(8,128)(2,1)}, f32[2,128,1024]{2,1,0:T(8,128)}, bf16[2,128,1024]{2,1,0:T(8,128)(2,1)}) custom-call(bf16[2,512,768]{2,1,0:T(8,128)(2,1)} %get-tuple-element.246.d_ref, bf16[1024,768]{1,0:T(8,128)(2,1)} %get-tuple-element.247.w_ref), custom_call_target="tpu_custom_call" | custom-call | flops 1610612736 | bytes 8388608 | tf_op jit(solution)/shard_map/input_grad/pallas_call | solution.py:851
  242.8 11.3 %all_to_all.5 = f32[32,1,512]{2,1,0:T(1,128)S(1)} all-to-all(f32[32,1,512]{2,1,0:T(1,128)S(1)} %reshape.519), channel_id=1, replica_groups=mesh['page'=8,'seq'=4] {'page','seq'}, dimensions={0} | all-to-all | bytes 131072 | tf_op jit(solution)/shard_map/all_to_all | solution.py:234
  255.6 2.2 add_convert_fusion
  267.7 4.7 %collective-permute-done.42 = bf16[4,32,1024]{2,1,0:T(8,128)(2,1)S(1)} collective-permute-done((bf16[4,32,1024]{2,1,0:T(8,128)(2,1)S(1)}, bf16[4,32,1024]{2,1,0:T(8,128)(2,1)S(1)}, u32[]{:S(2)}, u32[]{:S(2)}) %collective-permute-start.42) | collective-permute-done | bytes 262176 | tf_op jit(solution)/shard_map/ppermute | solution.py:79
  272.5 4.2 %collective-permute-done.51 = bf16[128,1024]{1,0:T(8,128)(2,1)S(1)} collective-permute-done((bf16[128,1024]{1,0:T(8,128)(2,1)S(1)}, bf16[128,1024]{1,0:T(8,128)(2,1)S(1)}, u32[]{:S(2)}, u32[]{:S(2)}) %collective-permute-start.51) | collective-permute-done | bytes 262176 | tf_op jit(solution)/shard_map/ppermute | solution.py:79
  280.2 3.7 %collective-permute-done.43 = bf16[2,32,1024]{2,1,0:T(8,128)(2,1)S(1)} collective-permute-done((bf16[2,32,1024]{2,1,0:T(8,128)(2,1)S(1)}, bf16[2,32,1024]{2,1,0:T(8,128)(2,1)S(1)}, u32[]{:S(2)}, u32[]{:S(2)}) %collective-permute-start.43) | collective-permute-done | bytes 131104 | tf_op jit(solution)/shard_map/ppermute | solution.py:79
  283.9 2.2 reduce-scatter.8.cloned.1.call-done
  291.6 2.3 add_add_fusion
  (328 shorter events, 99.6 us)
Async XLA Ops:
  7.2 118.8 %all-gather.3.cloned.1.call-start = ((), (), s32[]{:S(2)}) async-start(), calls=%async_computation.7 | async-start | bytes 4718592 | tf_op jit(solution)/shard_map/all_gather | solution.py:1015
  14.3 29.1 %collective-permute-start.7 = (bf16[2,128,1024]{2,1,0:T(8,128)(2,1)S(1)}, bf16[2,128,1024]{2,1,0:T(8,128)(2,1)}, u32[]{:S(2)}, u32[]{:S(2)}) collective-permute-start(bf16[2,128,1024]{2,1,0:T(8,128)(2,1)S(1)} %copy-done.26), channel_id=1, source_target_pairs={{0,2},{1,3},{2,0},{3,1},{4,6},{5,7},{6,4},{7,5},{8,10},{9,11},{10,... | collective-permute-start | bytes 1572872 | tf_op jit(solution)/shard_map/ppermute | solution.py:79
  21.1 16.8 %collective-permute-start.3 = (bf16[1,528,256]{2,1,0:T(8,128)(2,1)S(1)}, bf16[1,528,256]{2,1,0:T(8,128)(2,1)S(1)}, u32[]{:S(2)}, u32[]{:S(2)}) collective-permute-start(bf16[1,528,256]{2,1,0:T(8,128)(2,1)S(1)} %fusion.58.refs_0_), channel_id=1, source_target_pairs={{0,16},{4,20},{8,24},{12,28},{16,0},{20,4},{24,8},{28,12},{1,17},{... | collective-permute-start | bytes 811016 | tf_op jit(solution)/shard_map/ppermute | solution.py:79
  24.0 13.9 %collective-permute-start.4 = (bf16[1,528,256]{2,1,0:T(8,128)(2,1)S(1)}, bf16[1,528,256]{2,1,0:T(8,128)(2,1)S(1)}, u32[]{:S(2)}, u32[]{:S(2)}) collective-permute-start(bf16[1,528,256]{2,1,0:T(8,128)(2,1)S(1)} %fusion.58.refs_0_), channel_id=1, source_target_pairs={{0,8},{4,12},{8,0},{12,4},{16,24},{20,28},{24,16},{28,20},{1,9},{5... | collective-permute-start | bytes 811016 | tf_op jit(solution)/shard_map/ppermute | solution.py:79
  25.6 17.8 %collective-permute-start.5 = (bf16[1,528,256]{2,1,0:T(8,128)(2,1)S(1)}, bf16[1,528,256]{2,1,0:T(8,128)(2,1)S(1)}, u32[]{:S(2)}, u32[]{:S(2)}) collective-permute-start(bf16[1,528,256]{2,1,0:T(8,128)(2,1)S(1)} %fusion.58.refs_0_), channel_id=1, source_target_pairs={{0,24},{4,28},{8,16},{12,20},{16,8},{20,12},{24,0},{28,4},{1,25},{... | collective-permute-start | bytes 811016 | tf_op jit(solution)/shard_map/ppermute | solution.py:79
  25.6 17.8 %collective-permute-start.6 = (bf16[1,528,256]{2,1,0:T(8,128)(2,1)S(1)}, bf16[1,528,256]{2,1,0:T(8,128)(2,1)}, u32[]{:S(2)}, u32[]{:S(2)}) collective-permute-start(bf16[1,528,256]{2,1,0:T(8,128)(2,1)S(1)} %fusion.58.refs_0_), channel_id=1, source_target_pairs={{0,4},{4,0},{8,12},{12,8},{16,20},{20,16},{24,28},{28,24},{1,5},{5... | collective-permute-start | bytes 811016 | tf_op jit(solution)/shard_map/ppermute | solution.py:79
  44.3 185.2 %reduce-scatter.4.cloned.1.call-start = ((), (), s32[]{:S(2)}) async-start(), calls=%async_computation.4 | async-start | bytes 2621440 | tf_op jit(solution)/shard_map/reduce_scatter | solution.py:913
  44.6 26.3 %collective-permute-start.11 = (bf16[2,128,1024]{2,1,0:T(8,128)(2,1)S(1)}, bf16[2,128,1024]{2,1,0:T(8,128)(2,1)}, u32[]{:S(2)}, u32[]{:S(2)}) collective-permute-start(bf16[2,128,1024]{2,1,0:T(8,128)(2,1)S(1)} %copy-done.26), channel_id=1, source_target_pairs={{0,1},{1,0},{2,3},{3,2},{4,5},{5,4},{6,7},{7,6},{8,9},{9,8},{10,11... | collective-permute-start | bytes 1572872 | tf_op jit(solution)/shard_map/ppermute | solution.py:79
  44.6 26.2 %collective-permute-start.12 = (bf16[2,128,1024]{2,1,0:T(8,128)(2,1)}, bf16[2,128,1024]{2,1,0:T(8,128)(2,1)}, u32[]{:S(2)}, u32[]{:S(2)}) collective-permute-start(bf16[2,128,1024]{2,1,0:T(8,128)(2,1)} %collective-permute-done.7.refs_10_.refs_6_), channel_id=1, source_target_pairs={{0,1},{1,0},{2,3},{3,2},{4,5},{5,4},{6,7},{7,6},{8,9},{9,8},{10,11... | collective-permute-start | bytes 1572872 | tf_op jit(solution)/shard_map/ppermute | solution.py:79
  45.1 9.3 %collective-permute-start.10 = (bf16[1,528,256]{2,1,0:T(8,128)(2,1)S(1)}, bf16[1,528,256]{2,1,0:T(8,128)(2,1)S(1)}, u32[]{:S(2)}, u32[]{:S(2)}) collective-permute-start(bf16[1,528,256]{2,1,0:T(8,128)(2,1)S(1)} %collective-permute-done.5.refs_3_), channel_id=1, source_target_pairs={{0,4},{4,0},{8,12},{12,8},{16,20},{20,16},{24,28},{28,24},{1,5},{5... | collective-permute-start | bytes 811016 | tf_op jit(solution)/shard_map/ppermute | solution.py:79
  46.6 13.8 %collective-permute-start.8 = (bf16[1,528,256]{2,1,0:T(8,128)(2,1)S(1)}, bf16[1,528,256]{2,1,0:T(8,128)(2,1)S(1)}, u32[]{:S(2)}, u32[]{:S(2)}) collective-permute-start(bf16[1,528,256]{2,1,0:T(8,128)(2,1)S(1)} %collective-permute-done.3.refs_1_), channel_id=1, source_target_pairs={{0,4},{4,0},{8,12},{12,8},{16,20},{20,16},{24,28},{28,24},{1,5},{5... | collective-permute-start | bytes 811016 | tf_op jit(solution)/shard_map/ppermute | solution.py:79
  47.2 23.6 %collective-permute-start.9 = (bf16[1,528,256]{2,1,0:T(8,128)(2,1)S(1)}, bf16[1,528,256]{2,1,0:T(8,128)(2,1)S(1)}, u32[]{:S(2)}, u32[]{:S(2)}) collective-permute-start(bf16[1,528,256]{2,1,0:T(8,128)(2,1)S(1)} %collective-permute-done.4.refs_2_), channel_id=1, source_target_pairs={{0,4},{4,0},{8,12},{12,8},{16,20},{20,16},{24,28},{28,24},{1,5},{5... | collective-permute-start | bytes 811016 | tf_op jit(solution)/shard_map/ppermute | solution.py:79
  72.6 12.3 %collective-permute-start.13 = (bf16[8,128,256]{2,1,0:T(8,128)(2,1)S(1)}, bf16[8,128,256]{2,1,0:T(8,128)(2,1)S(1)}, u32[]{:S(2)}, u32[]{:S(2)}) collective-permute-start(bf16[8,128,256]{2,1,0:T(8,128)(2,1)S(1)} %slice_dynamic-update-slice_fusion.refs_0_), channel_id=1, source_target_pairs={{0,2},{1,3},{2,0},{3,1},{4,6},{5,7},{6,4},{7,5},{8,10},{9,11},{10,... | collective-permute-start | bytes 1572872 | tf_op jit(solution)/shard_map/ppermute | solution.py:79
  98.6 14.7 %collective-permute-start.19 = (bf16[256,1024]{1,0:T(8,128)(2,1)}, bf16[256,1024]{1,0:T(8,128)(2,1)S(1)}, u32[]{:S(2)}, u32[]{:S(2)}) collective-permute-start(bf16[256,1024]{1,0:T(8,128)(2,1)} %get-tuple-element.188.refs_4_), channel_id=1, source_target_pairs={{0,2},{1,3},{2,0},{3,1},{4,6},{5,7},{6,4},{7,5},{8,10},{9,11},{10,... | collective-permute-start | bytes 1572872 | tf_op jit(solution)/shard_map/ppermute | solution.py:79
  134.1 14.0 %collective-permute-start.24 = (bf16[256,1024]{1,0:T(8,128)(2,1)S(1)}, bf16[256,1024]{1,0:T(8,128)(2,1)S(1)}, u32[]{:S(2)}, u32[]{:S(2)}) collective-permute-start(bf16[256,1024]{1,0:T(8,128)(2,1)S(1)} %add_convert_fusion.4), channel_id=1, source_target_pairs={{0,2},{1,3},{2,0},{3,1},{4,6},{5,7},{6,4},{7,5},{8,10},{9,11},{10,... | collective-permute-start | bytes 1572872 | tf_op jit(solution)/shard_map/ppermute | solution.py:79
  138.1 10.0 %collective-permute-start.23 = (bf16[256,1024]{1,0:T(8,128)(2,1)S(1)}, bf16[256,1024]{1,0:T(8,128)(2,1)S(1)}, u32[]{:S(2)}, u32[]{:S(2)}) collective-permute-start(bf16[256,1024]{1,0:T(8,128)(2,1)S(1)} %convolution_convert_fusion.2), channel_id=1, source_target_pairs={{0,1},{1,0},{2,3},{3,2},{4,5},{5,4},{6,7},{7,6},{8,9},{9,8},{10,11... | collective-permute-start | bytes 1572872 | tf_op jit(solution)/shard_map/ppermute | solution.py:79
  151.5 14.6 %collective-permute-start.27 = (bf16[256,1024]{1,0:T(8,128)(2,1)}, bf16[256,1024]{1,0:T(8,128)(2,1)S(1)}, u32[]{:S(2)}, u32[]{:S(2)}) collective-permute-start(bf16[256,1024]{1,0:T(8,128)(2,1)} %get-tuple-element.197.refs_2_), channel_id=1, source_target_pairs={{0,2},{1,3},{2,0},{3,1},{4,6},{5,7},{6,4},{7,5},{8,10},{9,11},{10,... | collective-permute-start | bytes 1572872 | tf_op jit(solution)/shard_map/ppermute | solution.py:79
  172.4 14.0 %collective-permute-start.30 = (bf16[256,1024]{1,0:T(8,128)(2,1)S(1)}, bf16[256,1024]{1,0:T(8,128)(2,1)S(1)}, u32[]{:S(2)}, u32[]{:S(2)}) collective-permute-start(bf16[256,1024]{1,0:T(8,128)(2,1)S(1)} %add_convert_fusion.3), channel_id=1, source_target_pairs={{0,2},{1,3},{2,0},{3,1},{4,6},{5,7},{6,4},{7,5},{8,10},{9,11},{10,... | collective-permute-start | bytes 1572872 | tf_op jit(solution)/shard_map/ppermute | solution.py:79
  187.2 72.3 %reduce-scatter.6.cloned.1.call-start = ((), (), s32[]{:S(2)}) async-start(), calls=%async_computation.5 | async-start | bytes 1310720 | tf_op jit(solution)/shard_map/reduce_scatter | solution.py:913
  194.7 12.3 %collective-permute-start.31 = (bf16[8,2,32,1024]{3,2,1,0:T(8,128)(2,1)}, bf16[8,2,32,1024]{3,2,1,0:T(8,128)(2,1)S(1)}, u32[]{:S(2)}, u32[]{:S(2)}) collective-permute-start(bf16[8,2,32,1024]{3,2,1,0:T(8,128)(2,1)} %get-tuple-element.216), channel_id=1, source_target_pairs={{0,1},{1,0},{2,3},{3,2},{4,5},{5,4},{6,7},{7,6},{8,9},{9,8},{10,11... | collective-permute-start | bytes 3145736 | tf_op jit(solution)/shard_map/ppermute | solution.py:79
  194.8 12.2 %collective-permute-start.32 = (bf16[4,48,1024]{2,1,0:T(8,128)(2,1)}, bf16[4,48,1024]{2,1,0:T(8,128)(2,1)S(1)}, u32[]{:S(2)}, u32[]{:S(2)}) collective-permute-start(bf16[4,48,1024]{2,1,0:T(8,128)(2,1)} %get-tuple-element.217), channel_id=1, source_target_pairs={{0,4},{4,0},{8,12},{12,8},{16,20},{20,16},{24,28},{28,24},{1,5},{5... | collective-permute-start | bytes 1179656 | tf_op jit(solution)/shard_map/ppermute | solution.py:79
  197.9 27.8 %collective-permute-start.38 = (bf16[4,80,1024]{2,1,0:T(8,128)(2,1)}, bf16[4,80,1024]{2,1,0:T(8,128)(2,1)S(1)}, u32[]{:S(2)}, u32[]{:S(2)}) collective-permute-start(bf16[4,80,1024]{2,1,0:T(8,128)(2,1)} %get-tuple-element.245), channel_id=1, source_target_pairs={{0,4},{4,0},{8,12},{12,8},{16,20},{20,16},{24,28},{28,24},{1,5},{5... | collective-permute-start | bytes 1966088 | tf_op jit(solution)/shard_map/ppermute | solution.py:79
  209.0 16.7 %collective-permute-start.36 = (bf16[8,1,32,1024]{3,2,1,0:T(8,128)(2,1)S(1)}, bf16[8,1,32,1024]{3,2,1,0:T(8,128)(2,1)S(1)}, u32[]{:S(2)}, u32[]{:S(2)}) collective-permute-start(bf16[8,1,32,1024]{3,2,1,0:T(8,128)(2,1)S(1)} %dynamic-slice_convert_fusion), channel_id=1, source_target_pairs={{0,2},{1,3},{2,0},{3,1},{4,6},{5,7},{6,4},{7,5},{8,10},{9,11},{10,... | collective-permute-start | bytes 1572872 | tf_op jit(solution)/shard_map/ppermute | solution.py:79
  231.8 54.3 %reduce-scatter.8.cloned.1.call-start = ((), (), s32[]{:S(2)}) async-start(), calls=%async_computation.6 | async-start | bytes 983040 | tf_op jit(solution)/shard_map/reduce_scatter | solution.py:913
  231.9 23.7 %collective-permute-start.37 = (bf16[4,128,768]{2,1,0:T(8,128)(2,1)}, bf16[4,128,768]{2,1,0:T(8,128)(2,1)}, u32[]{:S(2)}, u32[]{:S(2)}) collective-permute-start(bf16[4,128,768]{2,1,0:T(8,128)(2,1)} %get-tuple-element.234), channel_id=1, source_target_pairs={{0,4},{4,0},{8,12},{12,8},{16,20},{20,16},{24,28},{28,24},{1,5},{5... | collective-permute-start | bytes 2359304 | tf_op jit(solution)/shard_map/ppermute | solution.py:79
  263.1 9.3 %collective-permute-start.42 = (bf16[4,32,1024]{2,1,0:T(8,128)(2,1)S(1)}, bf16[4,32,1024]{2,1,0:T(8,128)(2,1)S(1)}, u32[]{:S(2)}, u32[]{:S(2)}) collective-permute-start(bf16[4,32,1024]{2,1,0:T(8,128)(2,1)S(1)} %fusion.18), channel_id=1, source_target_pairs={{0,4},{4,0},{8,12},{12,8},{16,20},{20,16},{24,28},{28,24},{1,5},{5... | collective-permute-start | bytes 786440 | tf_op jit(solution)/shard_map/ppermute | solution.py:79
  264.8 14.7 %collective-permute-start.41 = (bf16[2,128,1024]{2,1,0:T(8,128)(2,1)S(1)}, bf16[2,128,1024]{2,1,0:T(8,128)(2,1)S(1)}, u32[]{:S(2)}, u32[]{:S(2)}) collective-permute-start(bf16[2,128,1024]{2,1,0:T(8,128)(2,1)S(1)} %add_convert_fusion.2), channel_id=1, source_target_pairs={{0,2},{1,3},{2,0},{3,1},{4,6},{5,7},{6,4},{7,5},{8,10},{9,11},{10,... | collective-permute-start | bytes 1572872 | tf_op jit(solution)/shard_map/ppermute | solution.py:79
  266.4 10.3 %collective-permute-start.51 = (bf16[128,1024]{1,0:T(8,128)(2,1)S(1)}, bf16[128,1024]{1,0:T(8,128)(2,1)S(1)}, u32[]{:S(2)}, u32[]{:S(2)}) collective-permute-start(bf16[128,1024]{1,0:T(8,128)(2,1)S(1)} %dynamic-slice_bitcast_fusion), channel_id=1, source_target_pairs={{0,4},{4,0},{8,12},{12,8},{16,20},{20,16},{24,28},{28,24},{1,5},{5... | collective-permute-start | bytes 786440 | tf_op jit(solution)/shard_map/ppermute | solution.py:79
  267.1 12.5 %collective-permute-start.44 = (bf16[32,1024]{1,0:T(8,128)(2,1)S(1)}, bf16[32,1024]{1,0:T(8,128)(2,1)S(1)}, u32[]{:S(2)}, u32[]{:S(2)}) collective-permute-start(bf16[32,1024]{1,0:T(8,128)(2,1)S(1)} %get-tuple-element.306), channel_id=1, source_target_pairs={{0,1},{1,0},{2,3},{3,2},{4,5},{5,4},{6,7},{7,6},{8,9},{9,8},{10,11... | collective-permute-start | bytes 196616 | tf_op jit(solution)/shard_map/ppermute | solution.py:79
  267.1 13.1 %collective-permute-start.45 = (bf16[32,1024]{1,0:T(8,128)(2,1)S(1)}, bf16[32,1024]{1,0:T(8,128)(2,1)S(1)}, u32[]{:S(2)}, u32[]{:S(2)}) collective-permute-start(bf16[32,1024]{1,0:T(8,128)(2,1)S(1)} %get-tuple-element.305), channel_id=1, source_target_pairs={{0,2},{1,3},{2,0},{3,1},{4,6},{5,7},{6,4},{7,5},{8,10},{9,11},{10,... | collective-permute-start | bytes 196616 | tf_op jit(solution)/shard_map/ppermute | solution.py:79
  279.5 12.0 %collective-permute-start.39 = (bf16[2,128,1024]{2,1,0:T(8,128)(2,1)}, bf16[2,128,1024]{2,1,0:T(8,128)(2,1)}, u32[]{:S(2)}, u32[]{:S(2)}) collective-permute-start(bf16[2,128,1024]{2,1,0:T(8,128)(2,1)} %get-tuple-element.261), channel_id=1, source_target_pairs={{0,1},{1,0},{2,3},{3,2},{4,5},{5,4},{6,7},{7,6},{8,9},{9,8},{10,11... | collective-permute-start | bytes 1572872 | tf_op jit(solution)/shard_map/ppermute | solution.py:79
  287.7 9.3 %collective-permute-start.50 = (bf16[1,32,1024]{2,1,0:T(8,128)(2,1)S(1)}, bf16[1,32,1024]{2,1,0:T(8,128)(2,1)S(1)}, u32[]{:S(2)}, u32[]{:S(2)}) collective-permute-start(bf16[1,32,1024]{2,1,0:T(8,128)(2,1)S(1)} %dynamic-slice_convert_fusion.2), channel_id=1, source_target_pairs={{0,16},{4,20},{8,24},{12,28},{16,0},{20,4},{24,8},{28,12},{1,17},{... | collective-permute-start | bytes 196616 | tf_op jit(solution)/shard_map/ppermute | solution.py:79
  (75 other events, 655.1 us)
Sparse Core Ops, SparseCore 0:
  44.4 81.5 all-gather.2
  187.4 42.1 reduce-scatter.3
  232.0 27.5 reduce-scatter.5
  261.7 24.3 reduce-scatter.7
